TPU v7x, 32 devices: a whole 2x2x4 slice. The times are simulated.
32 devices in a mesh: row: 8 (over z, x), col: 4 (over y, core).
Axes of the slice: x: 2, y: 2, z: 4, core: 2. Of those that a mesh axis runs over, the one named last changes fastest.
Arguments:
- obj_re: float32 [1024, 512], P('row', 'col'), may hold values from -6 to 6
- obj_im: float32 [1024, 512], P('row', 'col'), may hold values from -6 to 6
- probe_re: float32 [4, 256, 256], replicated, may hold values from -3 to 3
- probe_im: float32 [4, 256, 256], replicated, may hold values from -3 to 3
- amps: float32 [8, 4, 1, 256, 256], P('row', 'col'), may hold values from 0.2 to 4
- positions: int32 [8, 4, 1, 2], P('row', 'col'), may hold values from -128 to 896, as said below
Outputs:
- new_obj_re: float32 [1024, 512], P('row', 'col')
- new_obj_im: float32 [1024, 512], P('row', 'col')
- new_probe_re: float32 [4, 256, 256], replicated
- new_probe_im: float32 [4, 256, 256], replicated
Inputs may be any that keep to these rules, and one draw needn't show every extreme that they name: `positions`: each position's offsets are multiples of 64. A position stored at [i, j, p] has its row r with i * 128 - 256 // 2 <= r <= (i + 1) * 128 - 256 // 2 and its column c with j * 128 - 256 // 2 <= c <= (j + 1) * 128 - 256 // 2.
All inputs are finite; a program needn't handle non-finite values.
Results may differ from a plain program's by a relative error of at most 0.0055.
Values sent between devices are 32-bit elements; how exact they have to be, the bound alone decides.
No kernel may reach another device: no remote copies, remote signals or barrier semaphores. Data moves between devices by JAX's collectives and lax.ppermute only.
A program may use at most 64 MiB of HBM per device.

v0:
```python
import math

import jax
import jax.numpy as jnp
from jax import lax
from jax.sharding import PartitionSpec as P

ITERS = 3


amp_floor = 0.25
light_ratio = 0.1
mass_ratio = 0.1
probe_step = 6.0


def passed_along(array, axis, by):
    devices = lax.axis_size(axis)
    pairs = [(i, i + by) for i in range(devices) if 0 <= i + by < devices]
    return lax.ppermute(array, axis, pairs)


def with_halo(cells, sides, width):
    for axis, dim in sides:
        count = lax.axis_size(axis)
        ends = count - 1
        head = lax.slice_in_dim(cells, 0, width, axis=dim)
        tail = lax.slice_in_dim(cells, cells.shape[dim] - width, cells.shape[dim], axis=dim)
        cells = jnp.concatenate(
            [
                lax.ppermute(tail, axis, [(i, (i + 1) % count) for i in range(ends)]),
                cells,
                lax.ppermute(head, axis, [((i + 1) % count, i) for i in range(ends)]),
            ],
            axis=dim,
        )
    return cells


def make_tables(width, sign):
    index = jnp.arange(width, dtype=jnp.int32)
    turns = index[:, None] * index[None, :] % width
    angle = turns.astype(jnp.float32) * (2.0 * math.pi / width)
    real = (jnp.cos(angle) / math.sqrt(width)).astype(jnp.bfloat16)
    imag = (sign * jnp.sin(angle) / math.sqrt(width)).astype(jnp.bfloat16)
    right_pair = jnp.concatenate(
        [jnp.concatenate([real, imag], 1), jnp.concatenate([-imag, real], 1)], 0
    )
    return (right_pair, real, imag)


def transform(wave, table):
    right_pair, real, imag = table
    width = real.shape[0]
    half = jnp.einsum("mnc,cd->mnd", wave, right_pair, preferred_element_type=jnp.float32).astype(
        jnp.bfloat16
    )
    first = jnp.einsum("kn,mnd->mkd", real, half, preferred_element_type=jnp.float32)
    second = jnp.einsum("kn,mnd->mkd", imag, half, preferred_element_type=jnp.float32)
    return (first[..., :width] - second[..., width:], first[..., width:] + second[..., :width])


def one_view(window, probe_re, probe_im, view, forward, backward):
    win_re = window[0][None]
    win_im = window[1][None]
    psi = jnp.concatenate(
        [probe_re * win_re - probe_im * win_im, probe_re * win_im + probe_im * win_re], axis=2
    ).astype(jnp.bfloat16)
    spec_re, spec_im = transform(psi, forward)
    modulus = jnp.sqrt(jnp.sum(spec_re * spec_re + spec_im * spec_im, axis=0))
    factor = view / jnp.maximum(modulus, amp_floor) - 1.0
    change = jnp.concatenate([spec_re * factor, spec_im * factor], axis=2).astype(jnp.bfloat16)
    return transform(change, backward)


def place(buffer, piece, row_at, col_at):
    start = (jnp.int32(0), row_at, col_at)
    return lax.dynamic_update_slice(buffer, piece, start)


def send_rows(strip, offset):
    return passed_along(strip, "row", offset)


def send_cols(strip, offset):
    return passed_along(strip, "col", offset)


def fold_back(buffer, rows, cols, rim):
    middle = buffer[:, rim : rim + rows]
    from_below = send_rows(buffer[:, :rim], -1)
    from_above = send_rows(buffer[:, rim + rows :], 1)
    middle = middle.at[:, rows - rim :].add(from_below)
    middle = middle.at[:, :rim].add(from_above)
    core = middle[:, :, rim : rim + cols]
    from_right = send_cols(middle[:, :, :rim], -1)
    from_left = send_cols(middle[:, :, rim + cols :], 1)
    core = core.at[:, :, cols - rim :].add(from_right)
    return core.at[:, :, :rim].add(from_left)


def local(obj_re, obj_im, probe_re, probe_im, amps, positions):
    rows, cols = obj_re.shape
    modes, width = (probe_re.shape[0], probe_re.shape[1])
    rim = width // 2
    forward = make_tables(width, -1.0)
    backward = make_tables(width, 1.0)
    spots = positions[0, 0]
    views = amps[0, 0]
    my_row = lax.axis_index("row")
    my_col = lax.axis_index("col")
    row_base = my_row * rows - rim
    col_base = my_col * cols - rim
    local_rows = spots[:, 0] - row_base
    local_cols = spots[:, 1] - col_base
    wide_rows = rows + 2 * rim
    wide_cols = cols + 2 * rim
    power = jnp.sum(probe_re * probe_re + probe_im * probe_im, axis=0)
    light_buf = jnp.zeros((1, wide_rows, wide_cols), jnp.float32)
    slot = 0
    light_buf = place(light_buf, power[None], local_rows[slot], local_cols[slot])
    light = fold_back(light_buf, rows, cols, rim)[0]
    peak = lax.pmax(jnp.max(light), ("row", "col"))
    denom = light + light_ratio * peak
    state = jnp.stack([obj_re, obj_im])
    grad_re = jnp.zeros((modes, width, width), jnp.float32)
    grad_im = jnp.zeros((modes, width, width), jnp.float32)
    mass = jnp.zeros((width, width), jnp.float32)
    for step in range(ITERS):
        extended = with_halo(state, (("row", 1), ("col", 2)), rim)
        buffer = jnp.zeros((2, wide_rows, wide_cols), jnp.float32)
        last_pass = step == ITERS - 1
        slot = 0
        window = lax.dynamic_slice(
            extended, (jnp.int32(0), local_rows[slot], local_cols[slot]), (2, width, width)
        )
        exit_re, exit_im = one_view(window, probe_re, probe_im, views[slot], forward, backward)
        obj_grad = jnp.stack(
            [
                jnp.sum(probe_re * exit_re + probe_im * exit_im, axis=0),
                jnp.sum(probe_re * exit_im - probe_im * exit_re, axis=0),
            ]
        )
        buffer = place(buffer, obj_grad, local_rows[slot], local_cols[slot])
        if last_pass:
            win_re = window[0][None]
            win_im = window[1][None]
            grad_re = win_re * exit_re + win_im * exit_im
            grad_im = win_re * exit_im - win_im * exit_re
            mass = window[0] * window[0] + window[1] * window[1]
        state = state + fold_back(buffer, rows, cols, rim) / denom[None]
    pixels = width * width
    terms = jnp.concatenate(
        [grad_re.reshape(modes, pixels), grad_im.reshape(modes, pixels), mass.reshape(1, pixels)],
        axis=0,
    )
    probe_flat = jnp.concatenate(
        [probe_re.reshape(modes, pixels), probe_im.reshape(modes, pixels)], axis=0
    )
    summed = lax.psum(terms, ("row", "col"))
    scale = probe_step / (summed[2 * modes] + mass_ratio * jnp.mean(summed[2 * modes]))
    updated = probe_flat + summed[: 2 * modes] * scale[None]
    new_re = updated[:modes].reshape(modes, width, width)
    new_im = updated[modes:].reshape(modes, width, width)
    return (state[0], state[1], new_re, new_im)


def solution(mesh):
    placed = (
        P("row", "col"),
        P("row", "col"),
        P(),
        P(),
        P("row", "col", None, None, None),
        P("row", "col", None, None),
    )
    return jax.shard_map(
        local,
        mesh=mesh,
        in_specs=placed,
        out_specs=(P("row", "col"), P("row", "col"), P(), P()),
        check_vma=False,
    )
```

profile of v0, /device:TPU:0, one launch (start us, length us, event | category | flops | bytes accessed | tf_op | source)
XLA Modules:
  0.0 427.8 jit_solution(1866094221004445587)
XLA Ops:
  8.3 4.9 %collective-permute-start = (f32[2,128,128]{2,1,0:T(8,128)S(1)}, f32[2,128,128]{2,1,0:T(8,128)S(1)}, u32[]{:S(2)}, u32[]{:S(2)}) collective-permute-start(f32[2,128,128]{2,1,0:T(8,128)S(1)} %pad_maximum_fusion.11), channel_id=1, source_target_pairs={{0,4},{4,8},{8,12},{12,16},{16,20},{20,24},{24,28},{1,5},{5,9},{9,... | collective-permute-start | bytes 393224 | tf_op jit(solution)/shard_map/ppermute | solution.py:31
  16.1 3.9 collective-permute-done.1
  41.9 2.8 convolution_bitcast_fusion.8
  44.7 2.7 convolution_bitcast_fusion.9
  48.3 3.4 dynamic_update_slice.13
  54.7 5.2 %collective-permute-start.9 = (f32[1,128,384]{2,1,0:T(8,128)}, f32[1,128,384]{2,1,0:T(8,128)}, u32[]{:S(2)}, u32[]{:S(2)}) collective-permute-start(f32[1,128,384]{2,1,0:T(8,128)} %get-tuple-element.356), channel_id=1, source_target_pairs={{0,4},{4,8},{8,12},{12,16},{16,20},{20,24},{24,28},{1,5},{5,9},{9,... | collective-permute-start | bytes 589832 | tf_op jit(solution)/shard_map/ppermute | solution.py:20
  60.0 3.0 add_reduce_fusion.5
  67.0 5.7 %dynamic_update_slice.12 = f32[2,384,384]{2,1,0:T(8,128)} dynamic-update-slice(f32[2,384,384]{2,1,0:T(8,128)} %broadcast.616.clone, f32[2,256,256]{2,1,0:T(8,128)} %copy.48, s32[]{:T(128)} %constant.548.clone.1, s32[]{:T(128)S(6)} %select_n.65, s32[]{:T(128)S(6)} %select_n.66) | dynamic-update-slice | bytes 1048580 | tf_op jit(solution)/shard_map/dynamic_update_slice | solution.py:78
  76.1 5.3 %collective-permute-start.5 = (f32[2,128,384]{2,1,0:T(8,128)}, f32[2,128,384]{2,1,0:T(8,128)}, u32[]{:S(2)}, u32[]{:S(2)}) collective-permute-start(f32[2,128,384]{2,1,0:T(8,128)} %get-tuple-element.354), channel_id=1, source_target_pairs={{0,4},{4,8},{8,12},{12,16},{16,20},{20,24},{24,28},{1,5},{5,9},{9,... | collective-permute-start | bytes 1179656 | tf_op jit(solution)/shard_map/ppermute | solution.py:20
  83.9 5.2 %collective-permute-start.11 = (f32[1,128,128]{2,1,0:T(8,128)S(1)}, f32[1,128,128]{2,1,0:T(8,128)S(1)}, u32[]{:S(2)}, u32[]{:S(2)}) collective-permute-start(f32[1,128,128]{2,1,0:T(8,128)S(1)} %get-tuple-element.371), channel_id=1, source_target_pairs={{0,1},{1,2},{2,3},{4,5},{5,6},{6,7},{8,9},{9,10},{10,11},{12,13},{... | collective-permute-start | bytes 196616 | tf_op jit(solution)/shard_map/ppermute | solution.py:20
  90.5 44.0 %pmax.7 = f32[]{:T(128)} all-reduce(f32[]{:T(128)} %fusion.146), channel_id=1, replica_groups=mesh['row'=8,'col'=4] {'row','col'}, use_global_device_ids=true, to_apply=%region_5.6 | all-reduce | flops 1 | bytes 8 | tf_op jit(solution)/shard_map/pmax | solution.py:123
  137.8 3.0 collective-permute-start.7
  142.8 4.2 collective-permute-start.12
  148.3 2.6 collective-permute-done.12
  150.8 4.1 collective-permute-done.13
  158.1 4.2 collective-permute-done.15
  174.1 6.9 %dynamic_update_slice.14 = f32[2,384,384]{2,1,0:T(8,128)S(1)} dynamic-update-slice(f32[2,384,384]{2,1,0:T(8,128)S(1)} %broadcast.616.clone.1, f32[2,256,256]{2,1,0:T(8,128)} %copy.58, s32[]{:T(128)} %constant.548.clone.1, s32[]{:T(128)S(6)} %select_n.65, s32[]{:T(128)S(6)} %select_n.66) | dynamic-update-slice | bytes 1048580 | tf_op jit(solution)/shard_map/dynamic_update_slice | solution.py:78
  182.4 4.6 %collective-permute-start.17 = (f32[2,128,384]{2,1,0:T(8,128)S(1)}, f32[2,128,384]{2,1,0:T(8,128)S(1)}, u32[]{:S(2)}, u32[]{:S(2)}) collective-permute-start(f32[2,128,384]{2,1,0:T(8,128)S(1)} %get-tuple-element.352), channel_id=1, source_target_pairs={{0,4},{4,8},{8,12},{12,16},{16,20},{20,24},{24,28},{1,5},{5,9},{9,... | collective-permute-start | bytes 1179656 | tf_op jit(solution)/shard_map/ppermute | solution.py:20
  187.0 3.8 collective-permute-done.16
  190.8 9.8 %collective-permute-done.17 = f32[2,128,384]{2,1,0:T(8,128)S(1)} collective-permute-done((f32[2,128,384]{2,1,0:T(8,128)S(1)}, f32[2,128,384]{2,1,0:T(8,128)S(1)}, u32[]{:S(2)}, u32[]{:S(2)}) %collective-permute-start.17) | collective-permute-done | bytes 393248 | tf_op jit(solution)/shard_map/ppermute | solution.py:20
  202.0 5.2 %collective-permute-start.19 = (f32[2,128,128]{2,1,0:T(8,128)S(1)}, f32[2,128,128]{2,1,0:T(8,128)S(1)}, u32[]{:S(2)}, u32[]{:S(2)}) collective-permute-start(f32[2,128,128]{2,1,0:T(8,128)S(1)} %get-tuple-element.367), channel_id=1, source_target_pairs={{0,1},{1,2},{2,3},{4,5},{5,6},{6,7},{8,9},{9,10},{10,11},{12,13},{... | collective-permute-start | bytes 393224 | tf_op jit(solution)/shard_map/ppermute | solution.py:20
  208.2 4.1 collective-permute-start.20
  214.8 4.4 %collective-permute-done.21 = f32[2,128,128]{2,1,0:T(8,128)S(1)} collective-permute-done((f32[2,128,128]{2,1,0:T(8,128)S(1)}, f32[2,128,128]{2,1,0:T(8,128)S(1)}, u32[]{:S(2)}, u32[]{:S(2)}) %collective-permute-start.21) | collective-permute-done | bytes 131104 | tf_op jit(solution)/shard_map/ppermute | solution.py:33
  219.2 3.2 collective-permute-start.22
  224.2 5.7 %collective-permute-done.23 = f32[2,384,128]{2,1,0:T(8,128)S(1)} collective-permute-done((f32[2,384,128]{2,1,0:T(8,128)S(1)}, f32[2,384,128]{2,1,0:T(8,128)S(1)}, u32[]{:S(2)}, u32[]{:S(2)}) %collective-permute-start.23) | collective-permute-done | bytes 393248 | tf_op jit(solution)/shard_map/ppermute | solution.py:33
  245.2 6.9 %dynamic_update_slice.15 = f32[2,384,384]{2,1,0:T(8,128)S(1)} dynamic-update-slice(f32[2,384,384]{2,1,0:T(8,128)S(1)} %broadcast.616, f32[2,256,256]{2,1,0:T(8,128)} %pad_maximum_fusion.7, s32[]{:T(128)} %constant.548.clone.1, s32[]{:T(128)S(6)} %select_n.65, s32[]{:T(128)S(6)} %select_n.66) | dynamic-update-slice | bytes 1048580 | tf_op jit(solution)/shard_map/dynamic_update_slice | solution.py:78
  254.4 5.4 %collective-permute-start.25 = (f32[2,128,384]{2,1,0:T(8,128)}, f32[2,128,384]{2,1,0:T(8,128)}, u32[]{:S(2)}, u32[]{:S(2)}) collective-permute-start(f32[2,128,384]{2,1,0:T(8,128)} %get-tuple-element.350), channel_id=1, source_target_pairs={{0,4},{4,8},{8,12},{12,16},{16,20},{20,24},{24,28},{1,5},{5,9},{9,... | collective-permute-start | bytes 1179656 | tf_op jit(solution)/shard_map/ppermute | solution.py:20
  259.9 3.9 pad_maximum_fusion
  263.9 9.2 %collective-permute-done.25 = f32[2,128,384]{2,1,0:T(8,128)} collective-permute-done((f32[2,128,384]{2,1,0:T(8,128)}, f32[2,128,384]{2,1,0:T(8,128)}, u32[]{:S(2)}, u32[]{:S(2)}) %collective-permute-start.25) | collective-permute-done | bytes 393248 | tf_op jit(solution)/shard_map/ppermute | solution.py:20
  275.6 9.2 %collective-permute-start.27 = (f32[2,128,128]{2,1,0:T(8,128)S(1)}, f32[2,128,128]{2,1,0:T(8,128)S(1)}, u32[]{:S(2)}, u32[]{:S(2)}) collective-permute-start(f32[2,128,128]{2,1,0:T(8,128)S(1)} %get-tuple-element.365), channel_id=1, source_target_pairs={{0,1},{1,2},{2,3},{4,5},{5,6},{6,7},{8,9},{9,10},{10,11},{12,13},{... | collective-permute-start | bytes 393224 | tf_op jit(solution)/shard_map/ppermute | solution.py:20
  287.9 122.5 %all-reduce.2.cloned.1.call-done = f32[9,65536]{1,0:T(8,128)} async-done(((f32[9,65536]{1,0:T(8,128)}), f32[9,65536]{1,0:T(8,128)}) %all-reduce.2.cloned.1.call-update) | async-done | bytes 2359312 | tf_op jit(solution)/shard_map/psum | solution.py:160
  410.4 2.7 slice_reduce_fusion
  (185 shorter events, 98.2 us)
Async XLA Ops:
  7.2 403.2 %all-reduce.2.cloned.1.call-start = ((), (), s32[]{:S(2)}) async-start(), calls=%async_computation | async-start | bytes 8388608 | tf_op jit(solution)/shard_map/psum | solution.py:160
  8.3 7.8 %collective-permute-start = (f32[2,128,128]{2,1,0:T(8,128)S(1)}, f32[2,128,128]{2,1,0:T(8,128)S(1)}, u32[]{:S(2)}, u32[]{:S(2)}) collective-permute-start(f32[2,128,128]{2,1,0:T(8,128)S(1)} %pad_maximum_fusion.11), channel_id=1, source_target_pairs={{0,4},{4,8},{8,12},{12,16},{16,20},{20,24},{24,28},{1,5},{5,9},{9,... | collective-permute-start | bytes 393224 | tf_op jit(solution)/shard_map/ppermute | solution.py:31
  13.1 6.9 %collective-permute-start.1 = (f32[2,128,128]{2,1,0:T(8,128)S(1)}, f32[2,128,128]{2,1,0:T(8,128)S(1)}, u32[]{:S(2)}, u32[]{:S(2)}) collective-permute-start(f32[2,128,128]{2,1,0:T(8,128)S(1)} %pad_maximum_fusion.11), channel_id=1, source_target_pairs={{4,0},{8,4},{12,8},{16,12},{20,16},{24,20},{28,24},{5,1},{9,5},{13... | collective-permute-start | bytes 393224 | tf_op jit(solution)/shard_map/ppermute | solution.py:33
  21.7 12.0 %collective-permute-start.2 = (f32[2,384,128]{2,1,0:T(8,128)}, f32[2,384,128]{2,1,0:T(8,128)}, u32[]{:S(2)}, u32[]{:S(2)}) collective-permute-start(f32[2,384,128]{2,1,0:T(8,128)} %pad_maximum_fusion.8), channel_id=1, source_target_pairs={{0,1},{1,2},{2,3},{4,5},{5,6},{6,7},{8,9},{9,10},{10,11},{12,13},{... | collective-permute-start | bytes 1179656 | tf_op jit(solution)/shard_map/ppermute | solution.py:31
  23.7 10.0 %collective-permute-start.3 = (f32[2,384,128]{2,1,0:T(8,128)}, f32[2,384,128]{2,1,0:T(8,128)}, u32[]{:S(2)}, u32[]{:S(2)}) collective-permute-start(f32[2,384,128]{2,1,0:T(8,128)} %pad_maximum_fusion.8), channel_id=1, source_target_pairs={{1,0},{2,1},{3,2},{5,4},{6,5},{7,6},{9,8},{10,9},{11,10},{13,12},{... | collective-permute-start | bytes 1179656 | tf_op jit(solution)/shard_map/ppermute | solution.py:33
  53.4 28.0 %collective-permute-start.8 = (f32[1,128,384]{2,1,0:T(8,128)}, f32[1,128,384]{2,1,0:T(8,128)}, u32[]{:S(2)}, u32[]{:S(2)}) collective-permute-start(f32[1,128,384]{2,1,0:T(8,128)} %get-tuple-element.355), channel_id=1, source_target_pairs={{4,0},{8,4},{12,8},{16,12},{20,16},{24,20},{28,24},{5,1},{9,5},{13... | collective-permute-start | bytes 589832 | tf_op jit(solution)/shard_map/ppermute | solution.py:20
  54.7 26.7 %collective-permute-start.9 = (f32[1,128,384]{2,1,0:T(8,128)}, f32[1,128,384]{2,1,0:T(8,128)}, u32[]{:S(2)}, u32[]{:S(2)}) collective-permute-start(f32[1,128,384]{2,1,0:T(8,128)} %get-tuple-element.356), channel_id=1, source_target_pairs={{0,4},{4,8},{8,12},{12,16},{16,20},{20,24},{24,28},{1,5},{5,9},{9,... | collective-permute-start | bytes 589832 | tf_op jit(solution)/shard_map/ppermute | solution.py:20
  74.8 60.4 %collective-permute-start.4 = (f32[2,128,384]{2,1,0:T(8,128)}, f32[2,128,384]{2,1,0:T(8,128)}, u32[]{:S(2)}, u32[]{:S(2)}) collective-permute-start(f32[2,128,384]{2,1,0:T(8,128)} %get-tuple-element.353), channel_id=1, source_target_pairs={{4,0},{8,4},{12,8},{16,12},{20,16},{24,20},{28,24},{5,1},{9,5},{13... | collective-permute-start | bytes 1179656 | tf_op jit(solution)/shard_map/ppermute | solution.py:20
  76.1 59.1 %collective-permute-start.5 = (f32[2,128,384]{2,1,0:T(8,128)}, f32[2,128,384]{2,1,0:T(8,128)}, u32[]{:S(2)}, u32[]{:S(2)}) collective-permute-start(f32[2,128,384]{2,1,0:T(8,128)} %get-tuple-element.354), channel_id=1, source_target_pairs={{0,4},{4,8},{8,12},{12,16},{16,20},{20,24},{24,28},{1,5},{5,9},{9,... | collective-permute-start | bytes 1179656 | tf_op jit(solution)/shard_map/ppermute | solution.py:20
  82.6 6.5 %collective-permute-start.10 = (f32[1,128,128]{2,1,0:T(8,128)S(1)}, f32[1,128,128]{2,1,0:T(8,128)S(1)}, u32[]{:S(2)}, u32[]{:S(2)}) collective-permute-start(f32[1,128,128]{2,1,0:T(8,128)S(1)} %get-tuple-element.370), channel_id=1, source_target_pairs={{1,0},{2,1},{3,2},{5,4},{6,5},{7,6},{9,8},{10,9},{11,10},{13,12},{... | collective-permute-start | bytes 196616 | tf_op jit(solution)/shard_map/ppermute | solution.py:20
  83.9 6.0 %collective-permute-start.11 = (f32[1,128,128]{2,1,0:T(8,128)S(1)}, f32[1,128,128]{2,1,0:T(8,128)S(1)}, u32[]{:S(2)}, u32[]{:S(2)}) collective-permute-start(f32[1,128,128]{2,1,0:T(8,128)S(1)} %get-tuple-element.371), channel_id=1, source_target_pairs={{0,1},{1,2},{2,3},{4,5},{5,6},{6,7},{8,9},{9,10},{10,11},{12,13},{... | collective-permute-start | bytes 196616 | tf_op jit(solution)/shard_map/ppermute | solution.py:20
  136.5 5.2 %collective-permute-start.6 = (f32[2,128,128]{2,1,0:T(8,128)S(1)}, f32[2,128,128]{2,1,0:T(8,128)S(1)}, u32[]{:S(2)}, u32[]{:S(2)}) collective-permute-start(f32[2,128,128]{2,1,0:T(8,128)S(1)} %get-tuple-element.368), channel_id=1, source_target_pairs={{1,0},{2,1},{3,2},{5,4},{6,5},{7,6},{9,8},{10,9},{11,10},{13,12},{... | collective-permute-start | bytes 393224 | tf_op jit(solution)/shard_map/ppermute | solution.py:20
  137.8 4.0 collective-permute-start.7
  142.8 8.1 %collective-permute-start.12 = (f32[2,128,128]{2,1,0:T(8,128)S(1)}, f32[2,128,128]{2,1,0:T(8,128)S(1)}, u32[]{:S(2)}, u32[]{:S(2)}) collective-permute-start(f32[2,128,128]{2,1,0:T(8,128)S(1)} %fusion.63), channel_id=1, source_target_pairs={{0,4},{4,8},{8,12},{12,16},{16,20},{20,24},{24,28},{1,5},{5,9},{9,... | collective-permute-start | bytes 393224 | tf_op jit(solution)/shard_map/ppermute | solution.py:31
  147.0 8.0 %collective-permute-start.13 = (f32[2,128,128]{2,1,0:T(8,128)S(1)}, f32[2,128,128]{2,1,0:T(8,128)S(1)}, u32[]{:S(2)}, u32[]{:S(2)}) collective-permute-start(f32[2,128,128]{2,1,0:T(8,128)S(1)} %fusion.63), channel_id=1, source_target_pairs={{4,0},{8,4},{12,8},{16,12},{20,16},{24,20},{28,24},{5,1},{9,5},{13... | collective-permute-start | bytes 393224 | tf_op jit(solution)/shard_map/ppermute | solution.py:33
  155.0 3.1 collective-permute-start.14
  156.8 5.6 %collective-permute-start.15 = (f32[2,384,128]{2,1,0:T(8,128)S(1)}, f32[2,384,128]{2,1,0:T(8,128)S(1)}, u32[]{:S(2)}, u32[]{:S(2)}) collective-permute-start(f32[2,384,128]{2,1,0:T(8,128)S(1)} %pad_maximum_fusion.9), channel_id=1, source_target_pairs={{1,0},{2,1},{3,2},{5,4},{6,5},{7,6},{9,8},{10,9},{11,10},{13,12},{... | collective-permute-start | bytes 1179656 | tf_op jit(solution)/shard_map/ppermute | solution.py:33
  181.0 27.1 %copy-start.7 = (f32[2,128,128]{2,1,0:T(8,128)S(1)}, f32[2,128,128]{2,1,0:T(8,128)}, u32[]{:S(2)}) copy-start(f32[2,128,128]{2,1,0:T(8,128)} %copy-done.6) | copy-start | bytes 393220
  181.1 27.1 %copy-start.12 = (f32[128,128]{1,0:T(8,128)S(1)}, f32[128,128]{1,0:T(8,128)}, u32[]{:S(2)}) copy-start(f32[128,128]{1,0:T(8,128)} %copy-done.11) | copy-start | bytes 196612
  181.1 9.7 %collective-permute-start.16 = (f32[2,128,384]{2,1,0:T(8,128)S(1)}, f32[2,128,384]{2,1,0:T(8,128)S(1)}, u32[]{:S(2)}, u32[]{:S(2)}) collective-permute-start(f32[2,128,384]{2,1,0:T(8,128)S(1)} %get-tuple-element.351), channel_id=1, source_target_pairs={{4,0},{8,4},{12,8},{16,12},{20,16},{24,20},{28,24},{5,1},{9,5},{13... | collective-permute-start | bytes 1179656 | tf_op jit(solution)/shard_map/ppermute | solution.py:20
  182.4 18.2 %collective-permute-start.17 = (f32[2,128,384]{2,1,0:T(8,128)S(1)}, f32[2,128,384]{2,1,0:T(8,128)S(1)}, u32[]{:S(2)}, u32[]{:S(2)}) collective-permute-start(f32[2,128,384]{2,1,0:T(8,128)S(1)} %get-tuple-element.352), channel_id=1, source_target_pairs={{0,4},{4,8},{8,12},{12,16},{16,20},{20,24},{24,28},{1,5},{5,9},{9,... | collective-permute-start | bytes 1179656 | tf_op jit(solution)/shard_map/ppermute | solution.py:20
  200.7 6.5 %collective-permute-start.18 = (f32[2,128,128]{2,1,0:T(8,128)S(1)}, f32[2,128,128]{2,1,0:T(8,128)S(1)}, u32[]{:S(2)}, u32[]{:S(2)}) collective-permute-start(f32[2,128,128]{2,1,0:T(8,128)S(1)} %get-tuple-element.366), channel_id=1, source_target_pairs={{1,0},{2,1},{3,2},{5,4},{6,5},{7,6},{9,8},{10,9},{11,10},{13,12},{... | collective-permute-start | bytes 393224 | tf_op jit(solution)/shard_map/ppermute | solution.py:20
  202.0 6.2 %collective-permute-start.19 = (f32[2,128,128]{2,1,0:T(8,128)S(1)}, f32[2,128,128]{2,1,0:T(8,128)S(1)}, u32[]{:S(2)}, u32[]{:S(2)}) collective-permute-start(f32[2,128,128]{2,1,0:T(8,128)S(1)} %get-tuple-element.367), channel_id=1, source_target_pairs={{0,1},{1,2},{2,3},{4,5},{5,6},{6,7},{8,9},{9,10},{10,11},{12,13},{... | collective-permute-start | bytes 393224 | tf_op jit(solution)/shard_map/ppermute | solution.py:20
  208.2 22.3 %copy-start.4 = (f32[2,128,128]{2,1,0:T(8,128)}, f32[2,128,128]{2,1,0:T(8,128)S(1)}, u32[]{:S(2)}) copy-start(f32[2,128,128]{2,1,0:T(8,128)S(1)} %fusion.60) | copy-start | bytes 393220
  208.2 6.6 %collective-permute-start.20 = (f32[2,128,128]{2,1,0:T(8,128)S(1)}, f32[2,128,128]{2,1,0:T(8,128)S(1)}, u32[]{:S(2)}, u32[]{:S(2)}) collective-permute-start(f32[2,128,128]{2,1,0:T(8,128)S(1)} %fusion.60), channel_id=1, source_target_pairs={{0,4},{4,8},{8,12},{12,16},{16,20},{20,24},{24,28},{1,5},{5,9},{9,... | collective-permute-start | bytes 393224 | tf_op jit(solution)/shard_map/ppermute | solution.py:31
  212.3 6.9 %collective-permute-start.21 = (f32[2,128,128]{2,1,0:T(8,128)S(1)}, f32[2,128,128]{2,1,0:T(8,128)S(1)}, u32[]{:S(2)}, u32[]{:S(2)}) collective-permute-start(f32[2,128,128]{2,1,0:T(8,128)S(1)} %fusion.60), channel_id=1, source_target_pairs={{4,0},{8,4},{12,8},{16,12},{20,16},{24,20},{28,24},{5,1},{9,5},{13... | collective-permute-start | bytes 393224 | tf_op jit(solution)/shard_map/ppermute | solution.py:33
  219.2 4.9 %collective-permute-start.22 = (f32[2,384,128]{2,1,0:T(8,128)S(1)}, f32[2,384,128]{2,1,0:T(8,128)S(1)}, u32[]{:S(2)}, u32[]{:S(2)}) collective-permute-start(f32[2,384,128]{2,1,0:T(8,128)S(1)} %pad_maximum_fusion.10), channel_id=1, source_target_pairs={{0,1},{1,2},{2,3},{4,5},{5,6},{6,7},{8,9},{9,10},{10,11},{12,13},{... | collective-permute-start | bytes 1179656 | tf_op jit(solution)/shard_map/ppermute | solution.py:31
  222.4 7.4 %collective-permute-start.23 = (f32[2,384,128]{2,1,0:T(8,128)S(1)}, f32[2,384,128]{2,1,0:T(8,128)S(1)}, u32[]{:S(2)}, u32[]{:S(2)}) collective-permute-start(f32[2,384,128]{2,1,0:T(8,128)S(1)} %pad_maximum_fusion.10), channel_id=1, source_target_pairs={{1,0},{2,1},{3,2},{5,4},{6,5},{7,6},{9,8},{10,9},{11,10},{13,12},{... | collective-permute-start | bytes 1179656 | tf_op jit(solution)/shard_map/ppermute | solution.py:33
  253.1 10.7 %collective-permute-start.24 = (f32[2,128,384]{2,1,0:T(8,128)}, f32[2,128,384]{2,1,0:T(8,128)}, u32[]{:S(2)}, u32[]{:S(2)}) collective-permute-start(f32[2,128,384]{2,1,0:T(8,128)} %get-tuple-element.349), channel_id=1, source_target_pairs={{4,0},{8,4},{12,8},{16,12},{20,16},{24,20},{28,24},{5,1},{9,5},{13... | collective-permute-start | bytes 1179656 | tf_op jit(solution)/shard_map/ppermute | solution.py:20
  254.4 18.6 %collective-permute-start.25 = (f32[2,128,384]{2,1,0:T(8,128)}, f32[2,128,384]{2,1,0:T(8,128)}, u32[]{:S(2)}, u32[]{:S(2)}) collective-permute-start(f32[2,128,384]{2,1,0:T(8,128)} %get-tuple-element.350), channel_id=1, source_target_pairs={{0,4},{4,8},{8,12},{12,16},{16,20},{20,24},{24,28},{1,5},{5,9},{9,... | collective-permute-start | bytes 1179656 | tf_op jit(solution)/shard_map/ppermute | solution.py:20
  274.3 12.9 %collective-permute-start.26 = (f32[2,128,128]{2,1,0:T(8,128)S(1)}, f32[2,128,128]{2,1,0:T(8,128)S(1)}, u32[]{:S(2)}, u32[]{:S(2)}) collective-permute-start(f32[2,128,128]{2,1,0:T(8,128)S(1)} %get-tuple-element.364), channel_id=1, source_target_pairs={{1,0},{2,1},{3,2},{5,4},{6,5},{7,6},{9,8},{10,9},{11,10},{13,12},{... | collective-permute-start | bytes 393224 | tf_op jit(solution)/shard_map/ppermute | solution.py:20
  275.6 11.6 %collective-permute-start.27 = (f32[2,128,128]{2,1,0:T(8,128)S(1)}, f32[2,128,128]{2,1,0:T(8,128)S(1)}, u32[]{:S(2)}, u32[]{:S(2)}) collective-permute-start(f32[2,128,128]{2,1,0:T(8,128)S(1)} %get-tuple-element.365), channel_id=1, source_target_pairs={{0,1},{1,2},{2,3},{4,5},{5,6},{6,7},{8,9},{9,10},{10,11},{12,13},{... | collective-permute-start | bytes 393224 | tf_op jit(solution)/shard_map/ppermute | solution.py:20
  (28 other events, 149.6 us)
Sparse Core Ops, SparseCore 0:
  264.0 146.3 all-reduce.1
where the time goes:
time: 436 us; the launch traced here: 428 us
  waiting for transfers between devices  173 us (40%)
  starting transfers between devices  81.8 us (19%)
  local copies, waits for them, and re-layouts  48.8 us (11%)
  blocking collectives  44 us (10%)
  other arithmetic  38.4 us (9%)
  matrix products  23.7 us (5%)
  between operations  17.8 us (4%)
    psum x1, waiting for transfers between devices, local(): summed = lax.psum(terms, ('row', 'col'))  122 us
    ppermute x16, starting transfers between devices, passed_along(): return lax.ppermute(array, axis, pairs)  53.4 us
    pmax x1, blocking collectives, local(): peak = lax.pmax(jnp.max(light), ('row', 'col'))  44 us
    ppermute x16, waiting for transfers between devices, passed_along(): return lax.ppermute(array, axis, pairs)  24.7 us
    dynamic_update_slice x4, local copies, waits for them, and re-layouts, place(): return lax.dynamic_update_slice(buffer, piece, start)  22.9 us
    ppermute x6, waiting for transfers between devices, with_halo(): lax.ppermute(head, axis, [((i + 1) % count, i) for i in range(ends)])  22.3 us
    ppermute x6, starting transfers between devices, with_halo(): lax.ppermute(tail, axis, [(i, (i + 1) % count) for i in range(ends)])  20.2 us
    unnamed x72, local copies, waits for them, and re-layouts  13.4 us
  transfers between devices with their start and end apart: 29, of which 14 were waited for; matrix products, arithmetic and copies ran while one was open for 8% of the time, Pallas kernels for 0%

commit v1 on v0

v1 whole, which is shorter than its diff:
```python
import functools
import math

import jax
import jax.numpy as jnp
import numpy as np
from jax import lax
from jax.experimental import pallas as pl
from jax.experimental.pallas import tpu as pltpu
from jax.sharding import PartitionSpec as P

ITERS = 3

amp_floor = 0.25
light_ratio = 0.1
mass_ratio = 0.1
probe_step = 6.0

F32 = jnp.float32
BF16 = jnp.bfloat16
KEEP_ROWS = 16
HEAD = 2


def tables(width):
    index = np.arange(width)
    angle = (index[:, None] * index[None, :] % width) * (2.0 * math.pi / width)
    real = (np.cos(angle) / math.sqrt(width)).astype(np.float32)
    imag = (-np.sin(angle) / math.sqrt(width)).astype(np.float32)
    right = np.block([[real, imag], [-imag, real]]).astype(BF16)
    left = np.block([[real, -imag], [imag, real]]).astype(BF16)
    return right, left


def near_pairs(count):
    return [(i, i ^ 1) for i in range(count)]


def far_pairs(count):
    return [(i, (i + 1 if i % 2 else i - 1) % count) for i in range(count)]


def swap_near(array, axis):
    return lax.ppermute(array, axis, near_pairs(lax.axis_size(axis)))


def swap_far(array, axis):
    return lax.ppermute(array, axis, far_pairs(lax.axis_size(axis)))


def call(body, outs, scratch=(), smem=1, limit=None, cost=None):
    def run(*args):
        specs = [pl.BlockSpec(memory_space=pltpu.SMEM)] * smem
        specs += [pl.BlockSpec(memory_space=pltpu.VMEM)] * (len(args) - smem)
        return pl.pallas_call(
            body,
            out_shape=[jax.ShapeDtypeStruct(s, F32) for s in outs],
            in_specs=specs,
            out_specs=[pl.BlockSpec(memory_space=pltpu.VMEM)] * len(outs),
            scratch_shapes=list(scratch),
            compiler_params=pltpu.CompilerParams(vmem_limit_bytes=limit),
            cost_estimate=cost,
        )(*args)

    return run


class Place:
    def __init__(self, sc, sizes):
        n_row, n_col, rows, cols, rim = sizes
        self.i, self.j = sc[0], sc[1]
        self.even_row = self.i % 2 == 0
        self.even_col = self.j % 2 == 0
        self.up = self.i > 0
        self.down = self.i < n_row - 1
        self.has_left = self.j > 0
        self.has_right = self.j < n_col - 1
        self.far_row = jnp.where(self.even_row, self.i, n_row - 1 - self.i) > 0
        self.far_col = jnp.where(self.even_col, self.j, n_col - 1 - self.j) > 0
        near = jnp.where(self.even_col, self.j + 1, self.j - 1)
        far = jnp.where(self.even_col, self.j - 1, self.j + 1)
        far = jnp.where(self.far_col, far, self.j)

        def row_of(col):
            at = sc[HEAD + 2 * (self.i * n_col + col)]
            return pl.multiple_of(at - (self.i * rows - rim), rim // 2)

        self.row = row_of(self.j)
        self.near_row = row_of(near)
        self.far_row_at = row_of(far)
        self.col = sc[HEAD + 2 * (self.i * n_col + self.j) + 1] - (self.j * cols - rim)


def light_body(sizes, n_dev, sc, pr, pi, out, buf, pw):
    n_row, n_col, rows, cols, rim = sizes
    width = 2 * rim
    half = rim // 2
    power = jnp.sum(pr[...] * pr[...] + pi[...] * pi[...], axis=0)
    lane = lax.broadcasted_iota(jnp.int32, (width, rim), 1)
    a, b = power[:, :rim], power[:, rim:]
    ra, rb = pltpu.roll(a, half, 1), pltpu.roll(b, half, 1)
    zero = jnp.zeros((width, rim), F32)
    pw[0] = jnp.concatenate([a, b, zero], axis=1)
    pw[1] = jnp.concatenate(
        [jnp.where(lane < half, 0.0, ra), jnp.where(lane < half, ra, rb), jnp.where(lane < half, rb, 0.0)],
        axis=1,
    )
    buf[...] = jnp.zeros_like(buf)

    def add(p, carry):
        row = pl.multiple_of(sc[HEAD + 2 * p] + rim, half)
        col = sc[HEAD + 2 * p + 1] + rim
        odd = (col // half) % 2
        at = (pl.ds(row, width), pl.ds(pl.multiple_of(col - odd * half, rim), width + rim))
        buf[at] += pw[odd]
        return carry

    lax.fori_loop(0, n_dev, add, 0)

    def peak_of(k, best):
        at = pl.multiple_of(k * rows + rim, rim)
        return jnp.maximum(best, jnp.max(buf[pl.ds(at, rows), rim : rim + n_col * cols]))

    peak = lax.fori_loop(0, n_row, peak_of, jnp.float32(0.0))
    mine = buf[
        pl.ds(pl.multiple_of(sc[0] * rows + rim, rim), rows),
        pl.ds(pl.multiple_of(sc[1] * cols + rim, rim), cols),
    ]
    out[...] = mine + light_ratio * peak


def halo_body(sizes, sc, s, near, far, mid, to_near, to_far, ext):
    n_row, n_col, rows, cols, rim = sizes
    at = Place(sc, sizes)
    width = 2 * rim
    above = jnp.where(at.even_row, far[...], near[...])
    below = jnp.where(at.even_row, near[...], far[...])
    ext[:, :rim] = jnp.where(at.up, above, 0.0)
    ext[:, rim : rim + rows] = s[...]
    ext[:, rim + rows :] = jnp.where(at.down, below, 0.0)
    mid[...] = ext[:, pl.ds(at.row, width)]
    to_near[...] = ext[:, pl.ds(at.near_row, width)]
    to_far[...] = ext[:, pl.ds(at.far_row_at, width)]


def view_body(sizes, last, sc, mid, near, far, pr, pi, view, right_t, left_t, *refs):
    if last:
        gm, to_near, to_far, keep, send, spec_scr, win_scr, term_scr = refs
    else:
        gm, to_near, to_far, spec_scr, win_scr = refs
    n_row, n_col, rows, cols, rim = sizes
    at = Place(sc, sizes)
    modes, width = pr.shape[0], pr.shape[1]
    half = rim // 2
    lane = lax.broadcasted_iota(jnp.int32, (width, rim), 1)
    first = at.col == 0
    middle = at.col == half
    for part in range(2):
        a, b = near[part], far[part]
        lft = jnp.where(at.has_left, jnp.where(at.even_col, b, a), 0.0)
        rgt = jnp.where(at.has_right, jnp.where(at.even_col, a, b), 0.0)
        own = mid[part]
        rl, ro, rr = (pltpu.roll(t, half, 1) for t in (lft, own, rgt))
        win_scr[part, :, :rim] = jnp.where(
            first, lft, jnp.where(middle, jnp.where(lane < half, rl, ro), own)
        )
        win_scr[part, :, rim:] = jnp.where(
            first, own, jnp.where(middle, jnp.where(lane < half, ro, rr), rgt)
        )
    total = jnp.zeros((width, width), F32)
    for m in range(modes):
        wr, wi = win_scr[0], win_scr[1]
        psi = jnp.concatenate(
            [pr[m] * wr - pi[m] * wi, pr[m] * wi + pi[m] * wr], axis=1
        ).astype(BF16)
        mixed = jnp.dot(psi, right_t[...], preferred_element_type=F32).astype(BF16)
        tall = jnp.concatenate([mixed[:, :width], mixed[:, width:]], axis=0)
        spec = jnp.dot(left_t[...], tall, preferred_element_type=F32)
        spec_scr[m] = spec
        total = total + (spec[:width] * spec[:width] + spec[width:] * spec[width:])
    factor = view[...] / jnp.maximum(jnp.sqrt(total), amp_floor) - 1.0
    grad = [jnp.zeros((width, width), F32), jnp.zeros((width, width), F32)]
    for m in range(modes):
        change = jnp.concatenate(
            [spec_scr[m, :width] * factor, spec_scr[m, width:] * factor], axis=1
        ).astype(BF16)
        mixed = jnp.dot(change, left_t[...], preferred_element_type=F32).astype(BF16)
        tall = jnp.concatenate([mixed[:, :width], mixed[:, width:]], axis=0)
        back = jnp.dot(right_t[...], tall, preferred_element_type=F32)
        er, ei = back[:width], back[width:]
        grad[0] = grad[0] + (pr[m] * er + pi[m] * ei)
        grad[1] = grad[1] + (pr[m] * ei - pi[m] * er)
        if last:
            wr, wi = win_scr[0], win_scr[1]
            term_scr[m] = wr * er + wi * ei
            term_scr[modes + m] = wr * ei - wi * er
    for part in range(2):
        a, b = grad[part][:, :rim], grad[part][:, rim:]
        ra, rb = pltpu.roll(a, half, 1), pltpu.roll(b, half, 1)
        low = lane < half
        lft = jnp.where(first, a, jnp.where(middle, jnp.where(low, 0.0, ra), 0.0))
        own = jnp.where(first, b, jnp.where(middle, jnp.where(low, ra, rb), a))
        rgt = jnp.where(first, 0.0, jnp.where(middle, jnp.where(low, rb, 0.0), b))
        gm[part] = own
        to_near[part] = jnp.where(at.even_col, rgt, lft)
        to_far[part] = jnp.where(at.even_col, lft, rgt)
    if last:
        wr, wi = win_scr[0], win_scr[1]
        term_scr[2 * modes] = wr * wr + wi * wi
        bit = at.j % 2
        keep[...] = term_scr[:, pl.ds(pl.multiple_of(bit * rim, rim), rim)]
        send[...] = term_scr[:, pl.ds(pl.multiple_of((1 - bit) * rim, rim), rim)]


def fold_body(sizes, sc, gm, near, far, own, to_near, to_far, buf):
    n_row, n_col, rows, cols, rim = sizes
    at = Place(sc, sizes)
    width = 2 * rim
    buf[...] = jnp.zeros_like(buf)
    buf[:, pl.ds(at.row, width)] = gm[...]
    buf[:, pl.ds(at.near_row, width)] += near[...]
    buf[:, pl.ds(at.far_row_at, width)] += jnp.where(at.far_col, far[...], 0.0)
    top, bottom = buf[:, :rim], buf[:, rim + rows :]
    own[...] = buf[:, rim : rim + rows]
    to_near[...] = jnp.where(at.even_row, bottom, top)
    to_far[...] = jnp.where(at.even_row, top, bottom)


def step_body(sizes, sc, s, own, near, far, denom, out):
    at = Place(sc, sizes)
    grad = own[...] + near[...] + jnp.where(at.far_row, far[...], 0.0)
    out[...] = s[...] + grad / denom[...][None]


def bit_of(sc, axis, level):
    return lax.shift_right_logical(sc[axis], level) % 2


def halve_body(levels, height, shared, sc, *refs):
    count = len(levels)
    ins = 1 if shared else count
    cur, got, out = refs[:ins], refs[ins : 2 * ins], refs[2 * ins :]
    for c, (axis, level) in enumerate(levels):
        bit = bit_of(sc, axis, level)
        each = out[2 * c].shape[0]
        for which, offset in ((0, bit * height), (1, (1 - bit) * height)):
            rows = pl.ds(pl.multiple_of(offset, 8), height)
            if shared:
                at = (slice(c * each, (c + 1) * each), rows)
                out[2 * c + which][...] = cur[0][at] + got[0][at]
            else:
                out[2 * c + which][...] = cur[c][:, rows] + got[c][:, rows]


def gather_sum_body(count, sc, *refs):
    cur, got, out = refs[:count], refs[count : 2 * count], refs[2 * count]
    each = cur[0].shape[0]
    for c in range(count):
        out[c * each : (c + 1) * each] = cur[c][...] + got[c][...]


def spread_sum_body(count, sc, cur, got, *out):
    each = out[0].shape[0]
    for c in range(count):
        at = slice(c * each, (c + 1) * each)
        out[c][...] = cur[at] + got[at]


def sum_body(sc, cur, got, out):
    out[...] = cur[...] + got[...]


def join_body(levels, height, shared, sc, *refs):
    count = len(levels)
    cur, got, out = refs[:count], refs[count : 2 * count], refs[2 * count :]
    for c, (axis, level) in enumerate(levels):
        bit = bit_of(sc, axis, level)
        each = cur[c].shape[0]
        for src, offset in ((cur[c], bit * height), (got[c], (1 - bit) * height)):
            rows = pl.ds(pl.multiple_of(offset, 8), height)
            if shared:
                out[0][c * each : (c + 1) * each, rows] = src[...]
            else:
                out[c][:, rows] = src[...]


def probe_body(rim, sc, mine, got, pr, pi, new_re, new_im):
    modes = pr.shape[0]
    pixels = 4 * rim * rim
    bit = sc[1] % 2
    mean = (jnp.sum(mine[2 * modes]) + jnp.sum(got[2 * modes])) / pixels
    for src, offset in ((mine, bit * rim), (got, (1 - bit) * rim)):
        rows = pl.ds(pl.multiple_of(offset, rim), rim)
        scale = probe_step / (src[2 * modes] + mass_ratio * mean)
        for m in range(modes):
            new_re[m, rows] = pr[m, rows] + src[m] * scale
            new_im[m, rows] = pi[m, rows] + src[modes + m] * scale


def swap_bit(array, where):
    axis, level = where
    name = ("row", "col")[axis]
    count = lax.axis_size(name)
    return lax.ppermute(array, name, [(i, i ^ (1 << level)) for i in range(count)])


def sum_terms(sc, keep, send, n_row, n_col):
    parts, height, width = keep.shape
    colors = 3
    each = parts // colors
    row_bits = [(0, k) for k in range(n_row.bit_length() - 1)]
    col_bits = [(1, k) for k in range(1, n_col.bit_length() - 1)]
    rest = []
    while row_bits or col_bits:
        if row_bits:
            rest.append(row_bits.pop(0))
        if col_bits:
            rest.append(col_bits.pop(0))
    turn = rest[:colors]
    orders = [turn[c:] + turn[:c] for c in range(colors)]
    tail = rest[colors:]
    got = swap_bit(send, (1, 0))
    curs, gots, shared = [keep], [got], True
    steps = []
    for r in range(len(turn)):
        levels = [orders[c][r] for c in range(colors)]
        height //= 2
        outs = [(each, height, width)] * (2 * colors)
        res = call(functools.partial(halve_body, levels, height, shared), outs)(sc, *curs, *gots)
        curs, sends = res[0::2], res[1::2]
        gots = [swap_bit(a, w) for a, w in zip(sends, levels)]
        shared = False
        steps.append(levels)
    (cur,) = call(functools.partial(gather_sum_body, colors), [(parts, height, width)])(
        sc, *curs, *gots
    )
    for where in tail[:-1]:
        got = swap_bit(cur, where)
        (cur,) = call(sum_body, [cur.shape])(sc, cur, got)
    got = swap_bit(cur, tail[-1])
    curs = call(functools.partial(spread_sum_body, colors), [(each, height, width)] * colors)(
        sc, cur, got
    )
    for levels in reversed(steps):
        gots = [swap_bit(a, w) for a, w in zip(curs, levels)]
        final = levels is steps[0]
        shape = (each, 2 * height, width)
        outs = [(parts, 2 * height, width)] if final else [shape] * colors
        curs = call(functools.partial(join_body, levels, height, final), outs)(sc, *curs, *gots)
        height *= 2
    mine = curs[0]
    return mine, swap_bit(mine, (1, 0))


def local(obj_re, obj_im, probe_re, probe_im, amps, positions):
    rows, cols = obj_re.shape
    modes, width = probe_re.shape[0], probe_re.shape[1]
    rim = width // 2
    n_row, n_col = lax.axis_size("row"), lax.axis_size("col")
    n_dev = n_row * n_col
    sizes = (n_row, n_col, rows, cols, rim)
    right_np, left_np = tables(width)
    right_t, left_t = jnp.asarray(right_np), jnp.asarray(left_np)
    mine = jnp.broadcast_to(jnp.pad(positions.reshape(1, 2), ((0, 0), (0, 126))), (n_dev, 128))
    spots = lax.all_to_all(mine, ("row", "col"), 0, 0, tiled=True)[:, :2].reshape(-1)
    here = jnp.stack([lax.axis_index("row"), lax.axis_index("col")]).astype(jnp.int32)
    sc = jnp.concatenate([here, spots])
    view = amps.reshape(width, width)

    grid = (n_row * rows + 2 * rim, n_col * cols + 3 * rim)
    (denom,) = call(
        functools.partial(light_body, sizes, n_dev),
        [(rows, cols)],
        [pltpu.VMEM(grid, F32), pltpu.VMEM((2, width, width + rim), F32)],
    )(sc, probe_re, probe_im)

    strip = (2, width, cols)
    tile = (2, rows, cols)
    tall = pltpu.VMEM((2, rows + 2 * rim, cols), F32)
    halo = call(functools.partial(halo_body, sizes), [strip] * 3, [tall])
    fold = call(functools.partial(fold_body, sizes), [tile] * 3, [tall])
    step = call(functools.partial(step_body, sizes), [tile])
    scratch = [pltpu.VMEM((modes, 2 * width, width), F32), pltpu.VMEM((2, width, width), F32)]
    terms = (2 * modes + 1, rim, width)

    state = jnp.stack([obj_re, obj_im])
    for turn in range(ITERS):
        last = turn == ITERS - 1
        far, near = swap_far(state, "row"), swap_near(state, "row")
        mid, to_near, to_far = halo(sc, state, near, far)
        far, near = swap_far(to_far, "col"), swap_near(to_near, "col")
        outs = [strip] * 3 + ([terms] * 2 if last else [])
        scr = scratch + ([pltpu.VMEM((2 * modes + 1, width, width), F32)] if last else [])
        res = call(functools.partial(view_body, sizes, last), outs, scr)(
            sc, mid, near, far, probe_re, probe_im, view, right_t, left_t
        )
        gm, to_near, to_far = res[:3]
        far, near = swap_far(to_far, "col"), swap_near(to_near, "col")
        own, to_near, to_far = fold(sc, gm, near, far)
        far, near = swap_far(to_far, "row"), swap_near(to_near, "row")
        (state,) = step(sc, state, own, near, far, denom)
    mine, other = sum_terms(sc, res[3], res[4], n_row, n_col)
    shape = (modes, width, width)
    new_re, new_im = call(functools.partial(probe_body, rim), [shape] * 2)(
        sc, mine, other, probe_re, probe_im
    )
    return (state[0], state[1], new_re, new_im)


def solution(mesh):
    placed = (
        P("row", "col"),
        P("row", "col"),
        P(),
        P(),
        P("row", "col", None, None, None),
        P("row", "col", None, None),
    )
    return jax.shard_map(
        local,
        mesh=mesh,
        in_specs=placed,
        out_specs=(P("row", "col"), P("row", "col"), P(), P()),
        check_vma=False,
    )
```

time: 436 us -> 249 us (0.57); the launches traced: 428 us -> 248 us
  Pallas kernels: 0 us -> 64.4 us
  waiting for transfers between devices: 173 us -> 109 us
  blocking collectives: 44 us -> 0 us
  other arithmetic: 38.4 us -> 1.56 us
  local copies, waits for them, and re-layouts: 48.8 us -> 18.1 us
  starting transfers between devices: 81.8 us -> 54.7 us
  matrix products: 23.7 us -> 0 us
  between operations: 17.8 us -> 0.78 us
    psum x1 -> x0, waiting for transfers between devices: 122 us -> none  [local(): summed = lax.psum(terms, ('row', 'col'))]
    pallas_call x0 -> x22, Pallas kernels: none -> 64.4 us  [run(): pl.pallas_call(body, out_shape=[jax.ShapeDtypeStruct(s, F32) for s in out...]
    ppermute x28 -> x45, waiting for transfers between devices: 50.8 us -> 107 us  [the longest x12 53.4 us: swap_far(): return lax.ppermute(array, axis, far_pairs(lax.axis_size(axis)))]
    pmax x1 -> x0, blocking collectives: 44 us -> none  [local(): peak = lax.pmax(jnp.max(light), ('row', 'col'))]
    ppermute x28 -> x45, starting transfers between devices: 81.7 us -> 47.4 us  [the longest x12 26.2 us: swap_far(): return lax.ppermute(array, axis, far_pairs(lax.axis_size(axis)))]
    dot_general x18 -> x0, matrix products: 23.7 us -> none  [the longest x6 9.73 us: transform(): jnp.einsum('kn,mnd->mkd', imag, half, preferred_element_type=jnp.float32)]
    dynamic_update_slice x4 -> x0, local copies, waits for them, and re-layouts: 22.9 us -> none  [place(): return lax.dynamic_update_slice(buffer, piece, start)]
    concatenate x7 -> x1, other arithmetic: 8.75 us -> 0.67 us  [local(): sc = jnp.concatenate([here, spots])]
  transfers between devices with their start and end apart: 29 -> 46, of which waited for: 14 -> 37; matrix products, arithmetic and copies ran while one was open for 8% -> 1% of each run, Pallas kernels for 0% -> 4%
where the time goes in v1:
time: 249 us; the launch traced here: 248 us
  waiting for transfers between devices  109 us (44%)
  Pallas kernels  64.4 us (26%)
  starting transfers between devices  54.7 us (22%)
  local copies, waits for them, and re-layouts  18.1 us (7%)
    pallas_call x22, Pallas kernels, run(): pl.pallas_call(body, out_shape=[jax.ShapeDtypeStruct(s, F32) for s in out...  64.4 us
    ppermute x12, waiting for transfers between devices, swap_far(): return lax.ppermute(array, axis, far_pairs(lax.axis_size(axis)))  53.4 us
    ppermute x21, waiting for transfers between devices, swap_bit(): lax.ppermute(array, name, [(i, i ^ 1 << level) for i in range(count)])  35.2 us
    ppermute x12, starting transfers between devices, swap_far(): return lax.ppermute(array, axis, far_pairs(lax.axis_size(axis)))  26.2 us
    ppermute x12, waiting for transfers between devices, swap_near(): return lax.ppermute(array, axis, near_pairs(lax.axis_size(axis)))  18.7 us
    ppermute x21, starting transfers between devices, swap_bit(): lax.ppermute(array, name, [(i, i ^ 1 << level) for i in range(count)])  18.7 us
    unnamed x96, local copies, waits for them, and re-layouts  15.2 us
    all_to_all x1, starting transfers between devices, local(): lax.all_to_all(mine, ('row', 'col'), 0, 0, tiled=True)[:, :2].reshape(-1)  7.33 us
  transfers between devices with their start and end apart: 46, of which 37 were waited for; matrix products, arithmetic and copies ran while one was open for 1% of the time, Pallas kernels for 4%

profile of v1, /device:TPU:0, one launch (start us, length us, event | category | flops | bytes accessed | tf_op | source)
XLA Modules:
  0.0 248.5 jit_solution(9648612197827554718)
XLA Ops:
  1.9 7.3 %all-to-all-start = ((s32[32,1,128]{2,1,0:T(1,128)}), s32[32,1,128]{2,1,0:T(1,128)S(1)}, u32[]{:S(2)}, u32[]{:S(2)}) async-start(s32[32,1,128]{2,1,0:T(1,128)} %broadcast_in_dim.2), calls=%async_computation | async-start | bytes 32768 | tf_op jit(solution)/shard_map/all_to_all | solution.py:365
  10.1 4.6 %collective-permute-start.1 = (f32[2,128,128]{2,1,0:T(8,128)S(1)}, f32[2,128,128]{2,1,0:T(8,128)S(1)}, u32[]{:S(2)}, u32[]{:S(2)}) collective-permute-start(f32[2,128,128]{2,1,0:T(8,128)S(1)} %pad_maximum_fusion.s), channel_id=1, source_target_pairs={{0,28},{4,8},{8,4},{12,16},{16,12},{20,24},{24,20},{28,0},{1,29},{... | collective-permute-start | bytes 393224 | tf_op jit(solution)/shard_map/ppermute | solution.py:48
  18.7 2.7 %collective-permute-done.near = f32[2,128,128]{2,1,0:T(8,128)S(1)} collective-permute-done((f32[2,128,128]{2,1,0:T(8,128)S(1)}, f32[2,128,128]{2,1,0:T(8,128)S(1)}, u32[]{:S(2)}, u32[]{:S(2)}) %collective-permute-start) | collective-permute-done | bytes 131104 | tf_op jit(solution)/shard_map/ppermute | solution.py:44
  25.8 6.4 %collective-permute-done.3.far = f32[2,256,128]{2,1,0:T(8,128)S(1)} collective-permute-done((f32[2,256,128]{2,1,0:T(8,128)}, f32[2,256,128]{2,1,0:T(8,128)S(1)}, u32[]{:S(2)}, u32[]{:S(2)}) %collective-permute-start.3) | collective-permute-done | bytes 262176 | tf_op jit(solution)/shard_map/ppermute | solution.py:48
  32.9 6.6 %shard_map.112 = (f32[2,256,128]{2,1,0:T(8,128)}, f32[2,256,128]{2,1,0:T(8,128)}, f32[2,256,128]{2,1,0:T(8,128)}) custom-call(s32[66]{0:T(128)} %pad_add_fusion.sc, f32[2,256,128]{2,1,0:T(8,128)} %get-tuple-element.62.mid, f32[2,256,128]{2,1,0:T(8,128)} %copy-done.5, f32[2,256,128]{2,1,0:T(8,128)} %copy-done.7, f32[4,256,256]{2,1,0:T(8,128)} %pr.9, ...), custom_call_target="tpu_custom_call" | custom-call | tf_op jit(solution)/shard_map/pallas_call | solution.py:55
  41.4 7.3 %collective-permute-done.5.far = f32[2,256,128]{2,1,0:T(8,128)S(1)} collective-permute-done((f32[2,256,128]{2,1,0:T(8,128)}, f32[2,256,128]{2,1,0:T(8,128)S(1)}, u32[]{:S(2)}, u32[]{:S(2)}) %collective-permute-start.5) | collective-permute-done | bytes 262176 | tf_op jit(solution)/shard_map/ppermute | solution.py:48
  51.3 3.1 %collective-permute-start.7 = (f32[2,128,128]{2,1,0:T(8,128)}, f32[2,128,128]{2,1,0:T(8,128)S(1)}, u32[]{:S(2)}, u32[]{:S(2)}) collective-permute-start(f32[2,128,128]{2,1,0:T(8,128)} %get-tuple-element.70), channel_id=1, source_target_pairs={{0,28},{4,8},{8,4},{12,16},{16,12},{20,24},{24,20},{28,0},{1,29},{... | collective-permute-start | bytes 393224 | tf_op jit(solution)/shard_map/ppermute | solution.py:48
  54.5 5.9 %shard_map.114.denom = f32[128,128]{1,0:T(8,128)} custom-call(s32[66]{0:T(128)} %pad_add_fusion.sc, f32[4,256,256]{2,1,0:T(8,128)} %pr.9, f32[4,256,256]{2,1,0:T(8,128)} %pi.9), custom_call_target="tpu_custom_call" | custom-call | tf_op jit(solution)/shard_map/pallas_call | solution.py:55
  65.0 5.7 %collective-permute-done.9.far = f32[2,128,128]{2,1,0:T(8,128)S(1)} collective-permute-done((f32[2,128,128]{2,1,0:T(8,128)}, f32[2,128,128]{2,1,0:T(8,128)S(1)}, u32[]{:S(2)}, u32[]{:S(2)}) %collective-permute-start.9) | collective-permute-done | bytes 131104 | tf_op jit(solution)/shard_map/ppermute | solution.py:48
  76.8 6.4 %collective-permute-done.11.far = f32[2,256,128]{2,1,0:T(8,128)S(1)} collective-permute-done((f32[2,256,128]{2,1,0:T(8,128)}, f32[2,256,128]{2,1,0:T(8,128)S(1)}, u32[]{:S(2)}, u32[]{:S(2)}) %collective-permute-start.11) | collective-permute-done | bytes 262176 | tf_op jit(solution)/shard_map/ppermute | solution.py:48
  83.9 6.6 %shard_map.117 = (f32[2,256,128]{2,1,0:T(8,128)}, f32[2,256,128]{2,1,0:T(8,128)}, f32[2,256,128]{2,1,0:T(8,128)}) custom-call(s32[66]{0:T(128)} %pad_add_fusion.sc, f32[2,256,128]{2,1,0:T(8,128)} %get-tuple-element.71.mid, f32[2,256,128]{2,1,0:T(8,128)} %copy-done.6, f32[2,256,128]{2,1,0:T(8,128)} %copy-done.8, f32[4,256,256]{2,1,0:T(8,128)} %pr.9, ...), custom_call_target="tpu_custom_call" | custom-call | tf_op jit(solution)/shard_map/pallas_call | solution.py:55
  92.4 7.3 %collective-permute-done.13.far = f32[2,256,128]{2,1,0:T(8,128)S(1)} collective-permute-done((f32[2,256,128]{2,1,0:T(8,128)}, f32[2,256,128]{2,1,0:T(8,128)S(1)}, u32[]{:S(2)}, u32[]{:S(2)}) %collective-permute-start.13) | collective-permute-done | bytes 262176 | tf_op jit(solution)/shard_map/ppermute | solution.py:48
  102.3 2.9 %collective-permute-start.15 = (f32[2,128,128]{2,1,0:T(8,128)}, f32[2,128,128]{2,1,0:T(8,128)S(1)}, u32[]{:S(2)}, u32[]{:S(2)}) collective-permute-start(f32[2,128,128]{2,1,0:T(8,128)} %get-tuple-element.79), channel_id=1, source_target_pairs={{0,28},{4,8},{8,4},{12,16},{16,12},{20,24},{24,20},{28,0},{1,29},{... | collective-permute-start | bytes 393224 | tf_op jit(solution)/shard_map/ppermute | solution.py:48
  105.2 5.7 %collective-permute-done.14.near = f32[2,128,128]{2,1,0:T(8,128)S(1)} collective-permute-done((f32[2,128,128]{2,1,0:T(8,128)}, f32[2,128,128]{2,1,0:T(8,128)S(1)}, u32[]{:S(2)}, u32[]{:S(2)}) %collective-permute-start.14) | collective-permute-done | bytes 131104 | tf_op jit(solution)/shard_map/ppermute | solution.py:44
  113.3 2.9 %collective-permute-start.17 = (f32[2,128,128]{2,1,0:T(8,128)}, f32[2,128,128]{2,1,0:T(8,128)S(1)}, u32[]{:S(2)}, u32[]{:S(2)}) collective-permute-start(f32[2,128,128]{2,1,0:T(8,128)} %shard_map.119.s), channel_id=1, source_target_pairs={{0,28},{4,8},{8,4},{12,16},{16,12},{20,24},{24,20},{28,0},{1,29},{... | collective-permute-start | bytes 393224 | tf_op jit(solution)/shard_map/ppermute | solution.py:48
  116.2 5.0 %collective-permute-done.17.far = f32[2,128,128]{2,1,0:T(8,128)S(1)} collective-permute-done((f32[2,128,128]{2,1,0:T(8,128)}, f32[2,128,128]{2,1,0:T(8,128)S(1)}, u32[]{:S(2)}, u32[]{:S(2)}) %collective-permute-start.17) | collective-permute-done | bytes 131104 | tf_op jit(solution)/shard_map/ppermute | solution.py:48
  127.8 6.4 %collective-permute-done.19.far = f32[2,256,128]{2,1,0:T(8,128)S(1)} collective-permute-done((f32[2,256,128]{2,1,0:T(8,128)}, f32[2,256,128]{2,1,0:T(8,128)S(1)}, u32[]{:S(2)}, u32[]{:S(2)}) %collective-permute-start.19) | collective-permute-done | bytes 262176 | tf_op jit(solution)/shard_map/ppermute | solution.py:48
  134.9 7.8 %shard_map.121 = (f32[2,256,128]{2,1,0:T(8,128)}, f32[2,256,128]{2,1,0:T(8,128)}, f32[2,256,128]{2,1,0:T(8,128)}, f32[9,128,256]{2,1,0:T(8,128)}, f32[9,128,256]{2,1,0:T(8,128)}) custom-call(s32[66]{0:T(128)} %pad_add_fusion.sc, f32[2,256,128]{2,1,0:T(8,128)} %get-tuple-element.80.mid, f32[2,256,128]{2,1,0:T(8,128)} %copy-done.3, f32[2,256,128]{2,1,0:T(8,128)} %copy-done.4, ...), custom_call_target="tpu_custom_call" | custom-call | tf_op jit(solution)/shard_map/pallas_call | solution.py:55
  143.3 2.7 %collective-permute-done.24.refs_1_ = f32[9,128,256]{2,1,0:T(8,128)S(1)} collective-permute-done((f32[9,128,256]{2,1,0:T(8,128)}, f32[9,128,256]{2,1,0:T(8,128)S(1)}, u32[]{:S(2)}, u32[]{:S(2)}) %collective-permute-start.24) | collective-permute-done | bytes 1179680 | tf_op jit(solution)/shard_map/ppermute | solution.py:304
  147.0 2.8 %shard_map.124 = (f32[3,64,256]{2,1,0:T(8,128)}, f32[3,64,256]{2,1,0:T(8,128)}, f32[3,64,256]{2,1,0:T(8,128)}, f32[3,64,256]{2,1,0:T(8,128)}, f32[3,64,256]{2,1,0:T(8,128)}, /*index=5*/f32[3,64,256]{2,1,0:T(8,128)}) custom-call(s32[66]{0:T(128)} %pad_add_fusion.sc, f32[9,128,256]{2,1,0:T(8,128)} %get-tuple-element.89.refs_0_, f32[9,128,256]{2,1,0:T(8,128)} %copy-done.1), custom_call_target="tpu_custom_call" | custom-call | tf_op jit(solution)/shard_map/pallas_call | solution.py:55
  151.3 5.9 %collective-permute-done.25.refs_3_ = f32[3,64,256]{2,1,0:T(8,128)S(1)} collective-permute-done((f32[3,64,256]{2,1,0:T(8,128)}, f32[3,64,256]{2,1,0:T(8,128)S(1)}, u32[]{:S(2)}, u32[]{:S(2)}) %collective-permute-start.25) | collective-permute-done | bytes 196640 | tf_op jit(solution)/shard_map/ppermute | solution.py:304
  159.1 2.2 shard_map.125
  163.9 2.3 collective-permute-done.28.refs_3_
  179.5 7.5 %collective-permute-done.34.got = f32[9,16,256]{2,1,0:T(8,128)S(1)} collective-permute-done((f32[9,16,256]{2,1,0:T(8,128)}, f32[9,16,256]{2,1,0:T(8,128)S(1)}, u32[]{:S(2)}, u32[]{:S(2)}) %collective-permute-start.34) | collective-permute-done | bytes 147488 | tf_op jit(solution)/shard_map/ppermute | solution.py:304
  191.1 2.5 %collective-permute-done.35.refs_3_ = f32[3,16,256]{2,1,0:T(8,128)S(1)} collective-permute-done((f32[3,16,256]{2,1,0:T(8,128)}, f32[3,16,256]{2,1,0:T(8,128)S(1)}, u32[]{:S(2)}, u32[]{:S(2)}) %collective-permute-start.35) | collective-permute-done | bytes 49184 | tf_op jit(solution)/shard_map/ppermute | solution.py:304
  198.3 2.2 collective-permute-start.39
  201.6 2.5 %collective-permute-done.39.refs_4_ = f32[3,32,256]{2,1,0:T(8,128)S(1)} collective-permute-done((f32[3,32,256]{2,1,0:T(8,128)}, f32[3,32,256]{2,1,0:T(8,128)S(1)}, u32[]{:S(2)}, u32[]{:S(2)}) %collective-permute-start.39) | collective-permute-done | bytes 98336 | tf_op jit(solution)/shard_map/ppermute | solution.py:304
  210.6 3.3 %collective-permute-done.41.refs_3_ = f32[3,64,256]{2,1,0:T(8,128)S(1)} collective-permute-done((f32[3,64,256]{2,1,0:T(8,128)}, f32[3,64,256]{2,1,0:T(8,128)S(1)}, u32[]{:S(2)}, u32[]{:S(2)}) %collective-permute-start.41) | collective-permute-done | bytes 196640 | tf_op jit(solution)/shard_map/ppermute | solution.py:304
  216.3 2.4 shard_map.131.mine
  222.2 5.4 %collective-permute-done.21.far = f32[2,256,128]{2,1,0:T(8,128)S(1)} collective-permute-done((f32[2,256,128]{2,1,0:T(8,128)S(1)}, f32[2,256,128]{2,1,0:T(8,128)S(1)}, u32[]{:S(2)}, u32[]{:S(2)}) %collective-permute-start.21) | collective-permute-done | bytes 262176 | tf_op jit(solution)/shard_map/ppermute | solution.py:48
  233.3 4.2 %collective-permute-done.22.near = f32[2,128,128]{2,1,0:T(8,128)S(1)} collective-permute-done((f32[2,128,128]{2,1,0:T(8,128)}, f32[2,128,128]{2,1,0:T(8,128)S(1)}, u32[]{:S(2)}, u32[]{:S(2)}) %collective-permute-start.22) | collective-permute-done | bytes 131104 | tf_op jit(solution)/shard_map/ppermute | solution.py:44
  244.5 4.0 %shard_map.132 = (f32[4,256,256]{2,1,0:T(8,128)}, f32[4,256,256]{2,1,0:T(8,128)}) custom-call(s32[66]{0:T(128)} %pad_add_fusion.sc, f32[9,128,256]{2,1,0:T(8,128)} %shard_map.131.mine, f32[9,128,256]{2,1,0:T(8,128)} %copy-done, f32[4,256,256]{2,1,0:T(8,128)} %pr.9, f32[4,256,256]{2,1,0:T(8,128)} %pi.9), custom_call_target="tpu_custom_call" | custom-call | tf_op jit(solution)/shard_map/pallas_call | solution.py:55
  (184 shorter events, 97.1 us)
Async XLA Ops:
  1.9 14.4 %all-to-all-start = ((s32[32,1,128]{2,1,0:T(1,128)}), s32[32,1,128]{2,1,0:T(1,128)S(1)}, u32[]{:S(2)}, u32[]{:S(2)}) async-start(s32[32,1,128]{2,1,0:T(1,128)} %broadcast_in_dim.2), calls=%async_computation | async-start | bytes 32768 | tf_op jit(solution)/shard_map/all_to_all | solution.py:365
  10.1 8.5 %collective-permute-start.1 = (f32[2,128,128]{2,1,0:T(8,128)S(1)}, f32[2,128,128]{2,1,0:T(8,128)S(1)}, u32[]{:S(2)}, u32[]{:S(2)}) collective-permute-start(f32[2,128,128]{2,1,0:T(8,128)S(1)} %pad_maximum_fusion.s), channel_id=1, source_target_pairs={{0,28},{4,8},{8,4},{12,16},{16,12},{20,24},{24,20},{28,0},{1,29},{... | collective-permute-start | bytes 393224 | tf_op jit(solution)/shard_map/ppermute | solution.py:48
  14.7 6.6 %collective-permute-start = (f32[2,128,128]{2,1,0:T(8,128)S(1)}, f32[2,128,128]{2,1,0:T(8,128)S(1)}, u32[]{:S(2)}, u32[]{:S(2)}) collective-permute-start(f32[2,128,128]{2,1,0:T(8,128)S(1)} %pad_maximum_fusion.s), channel_id=1, source_target_pairs={{0,4},{4,0},{8,12},{12,8},{16,20},{20,16},{24,28},{28,24},{1,5},{5... | collective-permute-start | bytes 393224 | tf_op jit(solution)/shard_map/ppermute | solution.py:44
  24.0 8.1 %collective-permute-start.3 = (f32[2,256,128]{2,1,0:T(8,128)}, f32[2,256,128]{2,1,0:T(8,128)S(1)}, u32[]{:S(2)}, u32[]{:S(2)}) collective-permute-start(f32[2,256,128]{2,1,0:T(8,128)} %get-tuple-element.64), channel_id=1, source_target_pairs={{0,3},{1,2},{2,1},{3,0},{4,7},{5,6},{6,5},{7,4},{8,11},{9,10},{10,... | collective-permute-start | bytes 786440 | tf_op jit(solution)/shard_map/ppermute | solution.py:48
  40.0 8.6 %collective-permute-start.5 = (f32[2,256,128]{2,1,0:T(8,128)}, f32[2,256,128]{2,1,0:T(8,128)S(1)}, u32[]{:S(2)}, u32[]{:S(2)}) collective-permute-start(f32[2,256,128]{2,1,0:T(8,128)} %get-tuple-element.67), channel_id=1, source_target_pairs={{0,3},{1,2},{2,1},{3,0},{4,7},{5,6},{6,5},{7,4},{8,11},{9,10},{10,... | collective-permute-start | bytes 786440 | tf_op jit(solution)/shard_map/ppermute | solution.py:48
  51.3 9.0 %collective-permute-start.6 = (f32[2,128,128]{2,1,0:T(8,128)}, f32[2,128,128]{2,1,0:T(8,128)S(1)}, u32[]{:S(2)}, u32[]{:S(2)}) collective-permute-start(f32[2,128,128]{2,1,0:T(8,128)} %get-tuple-element.69), channel_id=1, source_target_pairs={{0,4},{4,0},{8,12},{12,8},{16,20},{20,16},{24,28},{28,24},{1,5},{5... | collective-permute-start | bytes 393224 | tf_op jit(solution)/shard_map/ppermute | solution.py:44
  51.3 9.0 %collective-permute-start.7 = (f32[2,128,128]{2,1,0:T(8,128)}, f32[2,128,128]{2,1,0:T(8,128)S(1)}, u32[]{:S(2)}, u32[]{:S(2)}) collective-permute-start(f32[2,128,128]{2,1,0:T(8,128)} %get-tuple-element.70), channel_id=1, source_target_pairs={{0,28},{4,8},{8,4},{12,16},{16,12},{20,24},{24,20},{28,0},{1,29},{... | collective-permute-start | bytes 393224 | tf_op jit(solution)/shard_map/ppermute | solution.py:48
  62.8 8.0 %collective-permute-start.9 = (f32[2,128,128]{2,1,0:T(8,128)}, f32[2,128,128]{2,1,0:T(8,128)S(1)}, u32[]{:S(2)}, u32[]{:S(2)}) collective-permute-start(f32[2,128,128]{2,1,0:T(8,128)} %shard_map.115.s), channel_id=1, source_target_pairs={{0,28},{4,8},{8,4},{12,16},{16,12},{20,24},{24,20},{28,0},{1,29},{... | collective-permute-start | bytes 393224 | tf_op jit(solution)/shard_map/ppermute | solution.py:48
  65.0 7.3 %collective-permute-start.8 = (f32[2,128,128]{2,1,0:T(8,128)}, f32[2,128,128]{2,1,0:T(8,128)S(1)}, u32[]{:S(2)}, u32[]{:S(2)}) collective-permute-start(f32[2,128,128]{2,1,0:T(8,128)} %shard_map.115.s), channel_id=1, source_target_pairs={{0,4},{4,0},{8,12},{12,8},{16,20},{20,16},{24,28},{28,24},{1,5},{5... | collective-permute-start | bytes 393224 | tf_op jit(solution)/shard_map/ppermute | solution.py:44
  75.0 8.1 %collective-permute-start.11 = (f32[2,256,128]{2,1,0:T(8,128)}, f32[2,256,128]{2,1,0:T(8,128)S(1)}, u32[]{:S(2)}, u32[]{:S(2)}) collective-permute-start(f32[2,256,128]{2,1,0:T(8,128)} %get-tuple-element.73), channel_id=1, source_target_pairs={{0,3},{1,2},{2,1},{3,0},{4,7},{5,6},{6,5},{7,4},{8,11},{9,10},{10,... | collective-permute-start | bytes 786440 | tf_op jit(solution)/shard_map/ppermute | solution.py:48
  91.0 8.6 %collective-permute-start.13 = (f32[2,256,128]{2,1,0:T(8,128)}, f32[2,256,128]{2,1,0:T(8,128)S(1)}, u32[]{:S(2)}, u32[]{:S(2)}) collective-permute-start(f32[2,256,128]{2,1,0:T(8,128)} %get-tuple-element.76), channel_id=1, source_target_pairs={{0,3},{1,2},{2,1},{3,0},{4,7},{5,6},{6,5},{7,4},{8,11},{9,10},{10,... | collective-permute-start | bytes 786440 | tf_op jit(solution)/shard_map/ppermute | solution.py:48
  102.3 8.5 %collective-permute-start.14 = (f32[2,128,128]{2,1,0:T(8,128)}, f32[2,128,128]{2,1,0:T(8,128)S(1)}, u32[]{:S(2)}, u32[]{:S(2)}) collective-permute-start(f32[2,128,128]{2,1,0:T(8,128)} %get-tuple-element.78), channel_id=1, source_target_pairs={{0,4},{4,0},{8,12},{12,8},{16,20},{20,16},{24,28},{28,24},{1,5},{5... | collective-permute-start | bytes 393224 | tf_op jit(solution)/shard_map/ppermute | solution.py:44
  102.3 8.5 %collective-permute-start.15 = (f32[2,128,128]{2,1,0:T(8,128)}, f32[2,128,128]{2,1,0:T(8,128)S(1)}, u32[]{:S(2)}, u32[]{:S(2)}) collective-permute-start(f32[2,128,128]{2,1,0:T(8,128)} %get-tuple-element.79), channel_id=1, source_target_pairs={{0,28},{4,8},{8,4},{12,16},{16,12},{20,24},{24,20},{28,0},{1,29},{... | collective-permute-start | bytes 393224 | tf_op jit(solution)/shard_map/ppermute | solution.py:48
  113.3 7.9 %collective-permute-start.17 = (f32[2,128,128]{2,1,0:T(8,128)}, f32[2,128,128]{2,1,0:T(8,128)S(1)}, u32[]{:S(2)}, u32[]{:S(2)}) collective-permute-start(f32[2,128,128]{2,1,0:T(8,128)} %shard_map.119.s), channel_id=1, source_target_pairs={{0,28},{4,8},{8,4},{12,16},{16,12},{20,24},{24,20},{28,0},{1,29},{... | collective-permute-start | bytes 393224 | tf_op jit(solution)/shard_map/ppermute | solution.py:48
  116.2 7.2 %collective-permute-start.16 = (f32[2,128,128]{2,1,0:T(8,128)}, f32[2,128,128]{2,1,0:T(8,128)S(1)}, u32[]{:S(2)}, u32[]{:S(2)}) collective-permute-start(f32[2,128,128]{2,1,0:T(8,128)} %shard_map.119.s), channel_id=1, source_target_pairs={{0,4},{4,0},{8,12},{12,8},{16,20},{20,16},{24,28},{28,24},{1,5},{5... | collective-permute-start | bytes 393224 | tf_op jit(solution)/shard_map/ppermute | solution.py:44
  126.1 8.1 %collective-permute-start.19 = (f32[2,256,128]{2,1,0:T(8,128)}, f32[2,256,128]{2,1,0:T(8,128)S(1)}, u32[]{:S(2)}, u32[]{:S(2)}) collective-permute-start(f32[2,256,128]{2,1,0:T(8,128)} %get-tuple-element.82), channel_id=1, source_target_pairs={{0,3},{1,2},{2,1},{3,0},{4,7},{5,6},{6,5},{7,4},{8,11},{9,10},{10,... | collective-permute-start | bytes 786440 | tf_op jit(solution)/shard_map/ppermute | solution.py:48
  149.8 7.4 %collective-permute-start.25 = (f32[3,64,256]{2,1,0:T(8,128)}, f32[3,64,256]{2,1,0:T(8,128)S(1)}, u32[]{:S(2)}, u32[]{:S(2)}) collective-permute-start(f32[3,64,256]{2,1,0:T(8,128)} %get-tuple-element.94), channel_id=1, source_target_pairs={{0,4},{4,0},{8,12},{12,8},{16,20},{20,16},{24,28},{28,24},{1,5},{5... | collective-permute-start | bytes 589832 | tf_op jit(solution)/shard_map/ppermute | solution.py:304
  149.8 7.4 %collective-permute-start.26 = (f32[3,64,256]{2,1,0:T(8,128)}, f32[3,64,256]{2,1,0:T(8,128)S(1)}, u32[]{:S(2)}, u32[]{:S(2)}) collective-permute-start(f32[3,64,256]{2,1,0:T(8,128)} %get-tuple-element.95), channel_id=1, source_target_pairs={{0,2},{1,3},{2,0},{3,1},{4,6},{5,7},{6,4},{7,5},{8,10},{9,11},{10,... | collective-permute-start | bytes 589832 | tf_op jit(solution)/shard_map/ppermute | solution.py:304
  151.3 7.1 %collective-permute-start.27 = (f32[3,64,256]{2,1,0:T(8,128)}, f32[3,64,256]{2,1,0:T(8,128)S(1)}, u32[]{:S(2)}, u32[]{:S(2)}) collective-permute-start(f32[3,64,256]{2,1,0:T(8,128)} %get-tuple-element.96), channel_id=1, source_target_pairs={{0,8},{4,12},{8,0},{12,4},{16,24},{20,28},{24,16},{28,20},{1,9},{5... | collective-permute-start | bytes 589832 | tf_op jit(solution)/shard_map/ppermute | solution.py:304
  161.3 4.8 %collective-permute-start.28 = (f32[3,32,256]{2,1,0:T(8,128)}, f32[3,32,256]{2,1,0:T(8,128)S(1)}, u32[]{:S(2)}, u32[]{:S(2)}) collective-permute-start(f32[3,32,256]{2,1,0:T(8,128)} %get-tuple-element.100), channel_id=1, source_target_pairs={{0,2},{1,3},{2,0},{3,1},{4,6},{5,7},{6,4},{7,5},{8,10},{9,11},{10,... | collective-permute-start | bytes 294920 | tf_op jit(solution)/shard_map/ppermute | solution.py:304
  161.8 4.8 %collective-permute-start.29 = (f32[3,32,256]{2,1,0:T(8,128)}, f32[3,32,256]{2,1,0:T(8,128)S(1)}, u32[]{:S(2)}, u32[]{:S(2)}) collective-permute-start(f32[3,32,256]{2,1,0:T(8,128)} %get-tuple-element.101), channel_id=1, source_target_pairs={{0,8},{4,12},{8,0},{12,4},{16,24},{20,28},{24,16},{28,20},{1,9},{5... | collective-permute-start | bytes 294920 | tf_op jit(solution)/shard_map/ppermute | solution.py:304
  162.1 4.8 %collective-permute-start.30 = (f32[3,32,256]{2,1,0:T(8,128)}, f32[3,32,256]{2,1,0:T(8,128)S(1)}, u32[]{:S(2)}, u32[]{:S(2)}) collective-permute-start(f32[3,32,256]{2,1,0:T(8,128)} %get-tuple-element.102), channel_id=1, source_target_pairs={{0,4},{4,0},{8,12},{12,8},{16,20},{20,16},{24,28},{28,24},{1,5},{5... | collective-permute-start | bytes 294920 | tf_op jit(solution)/shard_map/ppermute | solution.py:304
  169.5 5.0 %collective-permute-start.31 = (f32[3,16,256]{2,1,0:T(8,128)}, f32[3,16,256]{2,1,0:T(8,128)S(1)}, u32[]{:S(2)}, u32[]{:S(2)}) collective-permute-start(f32[3,16,256]{2,1,0:T(8,128)} %get-tuple-element.106), channel_id=1, source_target_pairs={{0,8},{4,12},{8,0},{12,4},{16,24},{20,28},{24,16},{28,20},{1,9},{5... | collective-permute-start | bytes 147464 | tf_op jit(solution)/shard_map/ppermute | solution.py:304
  179.5 7.6 %collective-permute-start.34 = (f32[9,16,256]{2,1,0:T(8,128)}, f32[9,16,256]{2,1,0:T(8,128)S(1)}, u32[]{:S(2)}, u32[]{:S(2)}) collective-permute-start(f32[9,16,256]{2,1,0:T(8,128)} %shard_map.127.cur), channel_id=1, source_target_pairs={{0,16},{4,20},{8,24},{12,28},{16,0},{20,4},{24,8},{28,12},{1,17},{... | collective-permute-start | bytes 442376 | tf_op jit(solution)/shard_map/ppermute | solution.py:304
  198.3 5.8 %collective-permute-start.39 = (f32[3,32,256]{2,1,0:T(8,128)}, f32[3,32,256]{2,1,0:T(8,128)S(1)}, u32[]{:S(2)}, u32[]{:S(2)}) collective-permute-start(f32[3,32,256]{2,1,0:T(8,128)} %get-tuple-element.113.refs_1_), channel_id=1, source_target_pairs={{0,8},{4,12},{8,0},{12,4},{16,24},{20,28},{24,16},{28,20},{1,9},{5... | collective-permute-start | bytes 294920 | tf_op jit(solution)/shard_map/ppermute | solution.py:304
  208.1 5.9 %collective-permute-start.41 = (f32[3,64,256]{2,1,0:T(8,128)}, f32[3,64,256]{2,1,0:T(8,128)S(1)}, u32[]{:S(2)}, u32[]{:S(2)}) collective-permute-start(f32[3,64,256]{2,1,0:T(8,128)} %get-tuple-element.115.refs_0_), channel_id=1, source_target_pairs={{0,4},{4,0},{8,12},{12,8},{16,20},{20,16},{24,28},{28,24},{1,5},{5... | collective-permute-start | bytes 589832 | tf_op jit(solution)/shard_map/ppermute | solution.py:304
  209.1 5.9 %collective-permute-start.42 = (f32[3,64,256]{2,1,0:T(8,128)}, f32[3,64,256]{2,1,0:T(8,128)S(1)}, u32[]{:S(2)}, u32[]{:S(2)}) collective-permute-start(f32[3,64,256]{2,1,0:T(8,128)} %get-tuple-element.116.refs_1_), channel_id=1, source_target_pairs={{0,2},{1,3},{2,0},{3,1},{4,6},{5,7},{6,4},{7,5},{8,10},{9,11},{10,... | collective-permute-start | bytes 589832 | tf_op jit(solution)/shard_map/ppermute | solution.py:304
  209.5 5.9 %collective-permute-start.43 = (f32[3,64,256]{2,1,0:T(8,128)}, f32[3,64,256]{2,1,0:T(8,128)S(1)}, u32[]{:S(2)}, u32[]{:S(2)}) collective-permute-start(f32[3,64,256]{2,1,0:T(8,128)} %get-tuple-element.117.refs_2_), channel_id=1, source_target_pairs={{0,8},{4,12},{8,0},{12,4},{16,24},{20,28},{24,16},{28,20},{1,9},{5... | collective-permute-start | bytes 589832 | tf_op jit(solution)/shard_map/ppermute | solution.py:304
  218.8 24.7 %collective-permute-start.44 = (f32[9,128,256]{2,1,0:T(8,128)}, f32[9,128,256]{2,1,0:T(8,128)S(1)}, u32[]{:S(2)}, u32[]{:S(2)}) collective-permute-start(f32[9,128,256]{2,1,0:T(8,128)} %shard_map.131.mine), channel_id=1, source_target_pairs={{0,1},{1,0},{2,3},{3,2},{4,5},{5,4},{6,7},{7,6},{8,9},{9,8},{10,11... | collective-permute-start | bytes 3538952 | tf_op jit(solution)/shard_map/ppermute | solution.py:304
  219.3 8.4 %collective-permute-start.21 = (f32[2,256,128]{2,1,0:T(8,128)S(1)}, f32[2,256,128]{2,1,0:T(8,128)S(1)}, u32[]{:S(2)}, u32[]{:S(2)}) collective-permute-start(f32[2,256,128]{2,1,0:T(8,128)S(1)} %copy-done.46), channel_id=1, source_target_pairs={{0,3},{1,2},{2,1},{3,0},{4,7},{5,6},{6,5},{7,4},{8,11},{9,10},{10,... | collective-permute-start | bytes 786440 | tf_op jit(solution)/shard_map/ppermute | solution.py:48
  230.3 7.1 %collective-permute-start.22 = (f32[2,128,128]{2,1,0:T(8,128)}, f32[2,128,128]{2,1,0:T(8,128)S(1)}, u32[]{:S(2)}, u32[]{:S(2)}) collective-permute-start(f32[2,128,128]{2,1,0:T(8,128)} %get-tuple-element.87), channel_id=1, source_target_pairs={{0,4},{4,0},{8,12},{12,8},{16,20},{20,16},{24,28},{28,24},{1,5},{5... | collective-permute-start | bytes 393224 | tf_op jit(solution)/shard_map/ppermute | solution.py:44
  231.3 8.1 %collective-permute-start.23 = (f32[2,128,128]{2,1,0:T(8,128)}, f32[2,128,128]{2,1,0:T(8,128)S(1)}, u32[]{:S(2)}, u32[]{:S(2)}) collective-permute-start(f32[2,128,128]{2,1,0:T(8,128)} %get-tuple-element.88), channel_id=1, source_target_pairs={{0,28},{4,8},{8,4},{12,16},{16,12},{20,24},{24,20},{28,0},{1,29},{... | collective-permute-start | bytes 393224 | tf_op jit(solution)/shard_map/ppermute | solution.py:48
  (62 other events, 158.9 us)

commit v2 on v1

--- a/solution.py
+++ b/solution.py
@@ -9,6 +9,7 @@
 from jax.experimental.pallas import tpu as pltpu
 from jax.sharding import PartitionSpec as P
 
+
 ITERS = 3
 
 amp_floor = 0.25
@@ -18,7 +19,6 @@
 
 F32 = jnp.float32
 BF16 = jnp.bfloat16
-KEEP_ROWS = 16
 HEAD = 2
 
 
@@ -40,16 +40,20 @@
     return [(i, (i + 1 if i % 2 else i - 1) % count) for i in range(count)]
 
 
-def swap_near(array, axis):
-    return lax.ppermute(array, axis, near_pairs(lax.axis_size(axis)))
-
-
-def swap_far(array, axis):
-    return lax.ppermute(array, axis, far_pairs(lax.axis_size(axis)))
-
-
-def call(body, outs, scratch=(), smem=1, limit=None, cost=None):
+def swap(array, axis, far):
+    pairs = (far_pairs if far else near_pairs)(lax.axis_size(axis))
+    return lax.ppermute(array, axis, pairs)
+
+
+def swap_both(to_near, to_far, axis):
+    return swap(to_near, axis, False), swap(to_far, axis, True)
+
+
+def call(body, outs, scratch=(), smem=1, extra=1 << 20, cost=None):
     def run(*args):
+        held = sum(4 * math.prod(s) for s in outs) + sum(a.size * a.dtype.itemsize for a in args[smem:])
+        held += sum(math.prod(s.shape) * 4 for s in scratch)
+        grant = held + extra
         specs = [pl.BlockSpec(memory_space=pltpu.SMEM)] * smem
         specs += [pl.BlockSpec(memory_space=pltpu.VMEM)] * (len(args) - smem)
         return pl.pallas_call(
@@ -58,7 +62,7 @@
             in_specs=specs,
             out_specs=[pl.BlockSpec(memory_space=pltpu.VMEM)] * len(outs),
             scratch_shapes=list(scratch),
-            compiler_params=pltpu.CompilerParams(vmem_limit_bytes=limit),
+            compiler_params=pltpu.CompilerParams(vmem_limit_bytes=grant),
             cost_estimate=cost,
         )(*args)
 
@@ -129,8 +133,31 @@
     out[...] = mine + light_ratio * peak
 
 
+def stage_body(*refs):
+    count = len(refs) // 2
+    ins, outs, sem = refs[:count], refs[count : 2 * count], refs[2 * count]
+    copies = [pltpu.make_async_copy(a, b, sem.at[k]) for k, (a, b) in enumerate(zip(ins, outs))]
+    for copy in copies:
+        copy.start()
+    for copy in copies:
+        copy.wait()
+
+
+def stage(*arrays):
+    size = sum(a.size * a.dtype.itemsize for a in arrays)
+    return pl.pallas_call(
+        stage_body,
+        out_shape=[jax.ShapeDtypeStruct(a.shape, a.dtype) for a in arrays],
+        in_specs=[pl.BlockSpec(memory_space=pl.ANY)] * len(arrays),
+        out_specs=[pl.BlockSpec(memory_space=pltpu.VMEM)] * len(arrays),
+        scratch_shapes=[pltpu.SemaphoreType.DMA((len(arrays),))],
+        compiler_params=pltpu.CompilerParams(vmem_limit_bytes=size + (1 << 20)),
+        cost_estimate=pl.CostEstimate(flops=0, bytes_accessed=2 * size, transcendentals=0),
+    )(*arrays)
+
+
 def halo_body(sizes, sc, s, near, far, mid, to_near, to_far, ext):
-    n_row, n_col, rows, cols, rim = sizes
+    _, _, rows, _, rim = sizes
     at = Place(sc, sizes)
     width = 2 * rim
     above = jnp.where(at.even_row, far[...], near[...])
@@ -148,7 +175,7 @@
         gm, to_near, to_far, keep, send, spec_scr, win_scr, term_scr = refs
     else:
         gm, to_near, to_far, spec_scr, win_scr = refs
-    n_row, n_col, rows, cols, rim = sizes
+    _, _, _, _, rim = sizes
     at = Place(sc, sizes)
     modes, width = pr.shape[0], pr.shape[1]
     half = rim // 2
@@ -213,7 +240,7 @@
 
 
 def fold_body(sizes, sc, gm, near, far, own, to_near, to_far, buf):
-    n_row, n_col, rows, cols, rim = sizes
+    _, _, rows, _, rim = sizes
     at = Place(sc, sizes)
     width = 2 * rim
     buf[...] = jnp.zeros_like(buf)
@@ -304,7 +331,7 @@
     return lax.ppermute(array, name, [(i, i ^ (1 << level)) for i in range(count)])
 
 
-def sum_terms(sc, keep, send, n_row, n_col):
+def sum_terms(sc, keep, send, n_row, n_col, beside):
     parts, height, width = keep.shape
     colors = 3
     each = parts // colors
@@ -329,6 +356,7 @@
         res = call(functools.partial(halve_body, levels, height, shared), outs)(sc, *curs, *gots)
         curs, sends = res[0::2], res[1::2]
         gots = [swap_bit(a, w) for a, w in zip(sends, levels)]
+        gots = beside(r, gots)
         shared = False
         steps.append(levels)
     (cur,) = call(functools.partial(gather_sum_body, colors), [(parts, height, width)])(
@@ -362,16 +390,20 @@
     right_np, left_np = tables(width)
     right_t, left_t = jnp.asarray(right_np), jnp.asarray(left_np)
     mine = jnp.broadcast_to(jnp.pad(positions.reshape(1, 2), ((0, 0), (0, 126))), (n_dev, 128))
-    spots = lax.all_to_all(mine, ("row", "col"), 0, 0, tiled=True)[:, :2].reshape(-1)
+    spots = lax.all_to_all(mine, ("row", "col"), 0, 0, tiled=True)
+    spots = spots[:, :2].reshape(-1)
     here = jnp.stack([lax.axis_index("row"), lax.axis_index("col")]).astype(jnp.int32)
     sc = jnp.concatenate([here, spots])
     view = amps.reshape(width, width)
+    probe_re, probe_im, view, right_t, left_t = stage(probe_re, probe_im, view, right_t, left_t)
 
     grid = (n_row * rows + 2 * rim, n_col * cols + 3 * rim)
     (denom,) = call(
         functools.partial(light_body, sizes, n_dev),
         [(rows, cols)],
         [pltpu.VMEM(grid, F32), pltpu.VMEM((2, width, width + rim), F32)],
+        extra=4 << 20,
+        cost=pl.CostEstimate(flops=8 * n_dev * width * width, bytes_accessed=10**7, transcendentals=0),
     )(sc, probe_re, probe_im)
 
     strip = (2, width, cols)
@@ -386,25 +418,40 @@
     state = jnp.stack([obj_re, obj_im])
     for turn in range(ITERS):
         last = turn == ITERS - 1
-        far, near = swap_far(state, "row"), swap_near(state, "row")
+        near, far = swap_both(state, state, "row")
         mid, to_near, to_far = halo(sc, state, near, far)
-        far, near = swap_far(to_far, "col"), swap_near(to_near, "col")
+        near, far = swap_both(to_near, to_far, "col")
         outs = [strip] * 3 + ([terms] * 2 if last else [])
         scr = scratch + ([pltpu.VMEM((2 * modes + 1, width, width), F32)] if last else [])
-        res = call(functools.partial(view_body, sizes, last), outs, scr)(
+        res = call(functools.partial(view_body, sizes, last), outs, scr, extra=8 << 20)(
             sc, mid, near, far, probe_re, probe_im, view, right_t, left_t
         )
         gm, to_near, to_far = res[:3]
-        far, near = swap_far(to_far, "col"), swap_near(to_near, "col")
+        near, far = swap_both(to_near, to_far, "col")
+        if last:
+            break
         own, to_near, to_far = fold(sc, gm, near, far)
-        far, near = swap_far(to_far, "row"), swap_near(to_near, "row")
+        near, far = swap_both(to_near, to_far, "row")
         (state,) = step(sc, state, own, near, far, denom)
-    mine, other = sum_terms(sc, res[3], res[4], n_row, n_col)
+
+    held = {}
+
+    def beside(r, gots):
+        if r == 0:
+            *gots, a, b = lax.optimization_barrier([*gots, near, far])
+            held["own"], to_near, to_far = fold(sc, gm, a, b)
+            held["both"] = swap_both(to_near, to_far, "row")
+        elif r == 1:
+            *gots, a, b = lax.optimization_barrier([*gots, *held["both"]])
+            (held["state"],) = step(sc, state, held["own"], a, b, denom)
+        return gots
+
+    mine, other = sum_terms(sc, res[3], res[4], n_row, n_col, beside)
     shape = (modes, width, width)
     new_re, new_im = call(functools.partial(probe_body, rim), [shape] * 2)(
         sc, mine, other, probe_re, probe_im
     )
-    return (state[0], state[1], new_re, new_im)
+    return (held["state"][0], held["state"][1], new_re, new_im)
 
 
 def solution(mesh):
@@ -416,6 +463,7 @@
         P("row", "col", None, None, None),
         P("row", "col", None, None),
     )
+
     return jax.shard_map(
         local,
         mesh=mesh,

time: 249 us -> 186 us (0.75)
  Pallas kernels: 64.4 us -> 31.1 us
  waiting for transfers between devices: 109 us -> 90.2 us
  local copies, waits for them, and re-layouts: 18.1 us -> 7.52 us
    pallas_call x22, Pallas kernels: 64.4 us -> 30.8 us  [run(): pl.pallas_call(body, out_shape=[jax.ShapeDtypeStruct(s, F32) for s in out...]
    ppermute x24, waiting for transfers between devices: 72.1 us -> 56.9 us  [swap(): return lax.ppermute(array, axis, pairs)]
    unnamed x96 -> x10, local copies, waits for them, and re-layouts: 15.2 us -> 5.48 us
    ppermute x21, waiting for transfers between devices: 35.2 us -> 31.7 us  [swap_bit(): lax.ppermute(array, name, [(i, i ^ 1 << level) for i in range(count)])]
  transfers between devices with their start and end apart: 46 -> 46, of which waited for: 37 -> 35; matrix products, arithmetic and copies ran while one was open for 1% -> 1% of each run, Pallas kernels for 4% -> 3%
where the time goes in v2:
time: 186 us; the launch traced here: 185 us
  waiting for transfers between devices  90.2 us (48%)
  starting transfers between devices  54.5 us (29%)
  Pallas kernels  31.1 us (17%)
  local copies, waits for them, and re-layouts  7.52 us (4%)
    ppermute x24, waiting for transfers between devices, swap(): return lax.ppermute(array, axis, pairs)  56.9 us
    ppermute x21, waiting for transfers between devices, swap_bit(): lax.ppermute(array, name, [(i, i ^ 1 << level) for i in range(count)])  31.7 us
    pallas_call x22, Pallas kernels, run(): pl.pallas_call(body, out_shape=[jax.ShapeDtypeStruct(s, F32) for s in out...  30.8 us
    ppermute x24, starting transfers between devices, swap(): return lax.ppermute(array, axis, pairs)  28.8 us
    ppermute x21, starting transfers between devices, swap_bit(): lax.ppermute(array, name, [(i, i ^ 1 << level) for i in range(count)])  18.3 us
    all_to_all x1, starting transfers between devices, local(): spots = lax.all_to_all(mine, ('row', 'col'), 0, 0, tiled=True)  7.33 us
    unnamed x10, local copies, waits for them, and re-layouts  5.48 us
  transfers between devices with their start and end apart: 46, of which 35 were waited for; matrix products, arithmetic and copies ran while one was open for 1% of the time, Pallas kernels for 3%

profile of v2, /device:TPU:0, one launch (start us, length us, event | category | flops | bytes accessed | tf_op | source)
XLA Modules:
  0.0 185.1 jit_solution(11357666218689299792)
XLA Ops:
  1.9 7.3 %all-to-all-start = ((s32[32,1,128]{2,1,0:T(1,128)}), s32[32,1,128]{2,1,0:T(1,128)S(1)}, u32[]{:S(2)}, u32[]{:S(2)}) async-start(s32[32,1,128]{2,1,0:T(1,128)} %broadcast_in_dim.2), calls=%async_computation | async-start | bytes 32768 | tf_op jit(solution)/shard_map/all_to_all | solution.py:393
  10.1 4.6 %collective-permute-start.1 = (f32[2,128,128]{2,1,0:T(8,128)S(1)}, f32[2,128,128]{2,1,0:T(8,128)S(1)}, u32[]{:S(2)}, u32[]{:S(2)}) collective-permute-start(f32[2,128,128]{2,1,0:T(8,128)S(1)} %pad_maximum_fusion.s), channel_id=1, source_target_pairs={{0,28},{4,8},{8,4},{12,16},{16,12},{20,24},{24,20},{28,0},{1,29},{... | collective-permute-start | bytes 393224 | tf_op jit(solution)/shard_map/ppermute | solution.py:45
  16.5 2.1 %collective-permute-done.1.far = f32[2,128,128]{2,1,0:T(8,128)S(1)} collective-permute-done((f32[2,128,128]{2,1,0:T(8,128)S(1)}, f32[2,128,128]{2,1,0:T(8,128)S(1)}, u32[]{:S(2)}, u32[]{:S(2)}) %collective-permute-start.1) | collective-permute-done | bytes 131104 | tf_op jit(solution)/shard_map/ppermute | solution.py:45
  18.6 2.7 %collective-permute-done.near = f32[2,128,128]{2,1,0:T(8,128)S(1)} collective-permute-done((f32[2,128,128]{2,1,0:T(8,128)S(1)}, f32[2,128,128]{2,1,0:T(8,128)S(1)}, u32[]{:S(2)}, u32[]{:S(2)}) %collective-permute-start) | collective-permute-done | bytes 131104 | tf_op jit(solution)/shard_map/ppermute | solution.py:45
  30.1 4.4 %shard_map.113 = (f32[2,256,128]{2,1,0:T(8,128)S(1)}, f32[2,256,128]{2,1,0:T(8,128)S(1)}, f32[2,256,128]{2,1,0:T(8,128)S(1)}) custom-call(s32[66]{0:T(128)S(1)} %pad_add_fusion.sc, f32[2,256,128]{2,1,0:T(8,128)S(1)} %get-tuple-element.77.mid, f32[2,256,128]{2,1,0:T(8,128)S(1)} %collective-permute-done.2.near, f32[2,256,128]{2,1,0:T(8,128)S(1)} %collective-permute-done.3.far, ...), custom_call_target="tpu_custom_call" | custom-call | tf_op jit(solution)/shard_map/pallas_call | solution.py:59
  36.3 7.0 %collective-permute-done.5.far = f32[2,256,128]{2,1,0:T(8,128)S(1)} collective-permute-done((f32[2,256,128]{2,1,0:T(8,128)S(1)}, f32[2,256,128]{2,1,0:T(8,128)S(1)}, u32[]{:S(2)}, u32[]{:S(2)}) %collective-permute-start.5) | collective-permute-done | bytes 262176 | tf_op jit(solution)/shard_map/ppermute | solution.py:45
  44.1 3.1 %collective-permute-start.7 = (f32[2,128,128]{2,1,0:T(8,128)S(1)}, f32[2,128,128]{2,1,0:T(8,128)S(1)}, u32[]{:S(2)}, u32[]{:S(2)}) collective-permute-start(f32[2,128,128]{2,1,0:T(8,128)S(1)} %get-tuple-element.90), channel_id=1, source_target_pairs={{0,28},{4,8},{8,4},{12,16},{16,12},{20,24},{24,20},{28,0},{1,29},{... | collective-permute-start | bytes 393224 | tf_op jit(solution)/shard_map/ppermute | solution.py:45
  47.2 4.2 %shard_map.115.denom = f32[128,128]{1,0:T(8,128)S(1)} custom-call(s32[66]{0:T(128)S(1)} %pad_add_fusion.sc, f32[4,256,256]{2,1,0:T(8,128)S(1)} %get-tuple-element.80.pr, f32[4,256,256]{2,1,0:T(8,128)S(1)} %get-tuple-element.81.pi), custom_call_target="tpu_custom_call" | custom-call | flops 16777216 | bytes 10000000 | tf_op jit(solution)/shard_map/pallas_call | solution.py:59
  53.0 2.8 %collective-permute-start.9 = (f32[2,128,128]{2,1,0:T(8,128)S(1)}, f32[2,128,128]{2,1,0:T(8,128)S(1)}, u32[]{:S(2)}, u32[]{:S(2)}) collective-permute-start(f32[2,128,128]{2,1,0:T(8,128)S(1)} %shard_map.116.s), channel_id=1, source_target_pairs={{0,28},{4,8},{8,4},{12,16},{16,12},{20,24},{24,20},{28,0},{1,29},{... | collective-permute-start | bytes 393224 | tf_op jit(solution)/shard_map/ppermute | solution.py:45
  55.8 4.9 %collective-permute-done.9.far = f32[2,128,128]{2,1,0:T(8,128)S(1)} collective-permute-done((f32[2,128,128]{2,1,0:T(8,128)S(1)}, f32[2,128,128]{2,1,0:T(8,128)S(1)}, u32[]{:S(2)}, u32[]{:S(2)}) %collective-permute-start.9) | collective-permute-done | bytes 131104 | tf_op jit(solution)/shard_map/ppermute | solution.py:45
  65.1 6.5 %collective-permute-done.11.far = f32[2,256,128]{2,1,0:T(8,128)S(1)} collective-permute-done((f32[2,256,128]{2,1,0:T(8,128)S(1)}, f32[2,256,128]{2,1,0:T(8,128)S(1)}, u32[]{:S(2)}, u32[]{:S(2)}) %collective-permute-start.11) | collective-permute-done | bytes 262176 | tf_op jit(solution)/shard_map/ppermute | solution.py:45
  71.5 4.4 %shard_map.118 = (f32[2,256,128]{2,1,0:T(8,128)S(1)}, f32[2,256,128]{2,1,0:T(8,128)S(1)}, f32[2,256,128]{2,1,0:T(8,128)S(1)}) custom-call(s32[66]{0:T(128)S(1)} %pad_add_fusion.sc, f32[2,256,128]{2,1,0:T(8,128)S(1)} %get-tuple-element.91.mid, f32[2,256,128]{2,1,0:T(8,128)S(1)} %collective-permute-done.10.near, ...), custom_call_target="tpu_custom_call" | custom-call | tf_op jit(solution)/shard_map/pallas_call | solution.py:59
  77.6 7.2 %collective-permute-done.13.far = f32[2,256,128]{2,1,0:T(8,128)S(1)} collective-permute-done((f32[2,256,128]{2,1,0:T(8,128)S(1)}, f32[2,256,128]{2,1,0:T(8,128)S(1)}, u32[]{:S(2)}, u32[]{:S(2)}) %collective-permute-start.13) | collective-permute-done | bytes 262176 | tf_op jit(solution)/shard_map/ppermute | solution.py:45
  85.5 2.3 %collective-permute-start.15 = (f32[2,128,128]{2,1,0:T(8,128)S(1)}, f32[2,128,128]{2,1,0:T(8,128)S(1)}, u32[]{:S(2)}, u32[]{:S(2)}) collective-permute-start(f32[2,128,128]{2,1,0:T(8,128)S(1)} %get-tuple-element.99), channel_id=1, source_target_pairs={{0,28},{4,8},{8,4},{12,16},{16,12},{20,24},{24,20},{28,0},{1,29},{... | collective-permute-start | bytes 393224 | tf_op jit(solution)/shard_map/ppermute | solution.py:45
  87.8 3.9 %collective-permute-done.14.near = f32[2,128,128]{2,1,0:T(8,128)S(1)} collective-permute-done((f32[2,128,128]{2,1,0:T(8,128)S(1)}, f32[2,128,128]{2,1,0:T(8,128)S(1)}, u32[]{:S(2)}, u32[]{:S(2)}) %collective-permute-start.14) | collective-permute-done | bytes 131104 | tf_op jit(solution)/shard_map/ppermute | solution.py:45
  91.6 2.2 %collective-permute-done.15.far = f32[2,128,128]{2,1,0:T(8,128)S(1)} collective-permute-done((f32[2,128,128]{2,1,0:T(8,128)S(1)}, f32[2,128,128]{2,1,0:T(8,128)S(1)}, u32[]{:S(2)}, u32[]{:S(2)}) %collective-permute-start.15) | collective-permute-done | bytes 131104 | tf_op jit(solution)/shard_map/ppermute | solution.py:45
  94.4 2.3 %collective-permute-start.17 = (f32[2,128,128]{2,1,0:T(8,128)S(1)}, f32[2,128,128]{2,1,0:T(8,128)S(1)}, u32[]{:S(2)}, u32[]{:S(2)}) collective-permute-start(f32[2,128,128]{2,1,0:T(8,128)S(1)} %shard_map.120.s), channel_id=1, source_target_pairs={{0,28},{4,8},{8,4},{12,16},{16,12},{20,24},{24,20},{28,0},{1,29},{... | collective-permute-start | bytes 393224 | tf_op jit(solution)/shard_map/ppermute | solution.py:45
  96.7 5.5 %collective-permute-done.17.far = f32[2,128,128]{2,1,0:T(8,128)S(1)} collective-permute-done((f32[2,128,128]{2,1,0:T(8,128)S(1)}, f32[2,128,128]{2,1,0:T(8,128)S(1)}, u32[]{:S(2)}, u32[]{:S(2)}) %collective-permute-start.17) | collective-permute-done | bytes 131104 | tf_op jit(solution)/shard_map/ppermute | solution.py:45
  106.3 6.3 %collective-permute-done.19.far = f32[2,256,128]{2,1,0:T(8,128)S(1)} collective-permute-done((f32[2,256,128]{2,1,0:T(8,128)S(1)}, f32[2,256,128]{2,1,0:T(8,128)S(1)}, u32[]{:S(2)}, u32[]{:S(2)}) %collective-permute-start.19) | collective-permute-done | bytes 262176 | tf_op jit(solution)/shard_map/ppermute | solution.py:45
  112.6 5.0 %shard_map.122 = (f32[2,256,128]{2,1,0:T(8,128)S(1)}, f32[2,256,128]{2,1,0:T(8,128)S(1)}, f32[2,256,128]{2,1,0:T(8,128)S(1)}, f32[9,128,256]{2,1,0:T(8,128)S(1)}, f32[9,128,256]{2,1,0:T(8,128)S(1)}) custom-call(s32[66]{0:T(128)S(1)} %pad_add_fusion.sc, f32[2,256,128]{2,1,0:T(8,128)S(1)} %get-tuple-element.100.mid, ...), custom_call_target="tpu_custom_call" | custom-call | tf_op jit(solution)/shard_map/pallas_call | solution.py:59
  123.0 3.5 %collective-permute-done.25.far = f32[2,256,128]{2,1,0:T(8,128)S(1)} collective-permute-done((f32[2,256,128]{2,1,0:T(8,128)S(1)}, f32[2,256,128]{2,1,0:T(8,128)S(1)}, u32[]{:S(2)}, u32[]{:S(2)}) %collective-permute-start.25) | collective-permute-done | bytes 262176 | tf_op jit(solution)/shard_map/ppermute | solution.py:45
  128.5 2.5 %collective-permute-done.22.refs_4_ = f32[3,64,256]{2,1,0:T(8,128)S(1)} collective-permute-done((f32[3,64,256]{2,1,0:T(8,128)S(1)}, f32[3,64,256]{2,1,0:T(8,128)S(1)}, u32[]{:S(2)}, u32[]{:S(2)}) %collective-permute-start.22) | collective-permute-done | bytes 196640 | tf_op jit(solution)/shard_map/ppermute | solution.py:331
  132.3 2.4 %collective-permute-start.30 = (f32[2,128,128]{2,1,0:T(8,128)S(1)}, f32[2,128,128]{2,1,0:T(8,128)S(1)}, u32[]{:S(2)}, u32[]{:S(2)}) collective-permute-start(f32[2,128,128]{2,1,0:T(8,128)S(1)} %get-tuple-element.124), channel_id=1, source_target_pairs={{0,28},{4,8},{8,4},{12,16},{16,12},{20,24},{24,20},{28,0},{1,29},{... | collective-permute-start | bytes 393224 | tf_op jit(solution)/shard_map/ppermute | solution.py:45
  137.6 2.5 %collective-permute-done.26.refs_3_ = f32[3,32,256]{2,1,0:T(8,128)S(1)} collective-permute-done((f32[3,32,256]{2,1,0:T(8,128)S(1)}, f32[3,32,256]{2,1,0:T(8,128)S(1)}, u32[]{:S(2)}, u32[]{:S(2)}) %collective-permute-start.26) | collective-permute-done | bytes 98336 | tf_op jit(solution)/shard_map/ppermute | solution.py:331
  144.8 2.2 %collective-permute-done.31.refs_3_ = f32[3,16,256]{2,1,0:T(8,128)S(1)} collective-permute-done((f32[3,16,256]{2,1,0:T(8,128)S(1)}, f32[3,16,256]{2,1,0:T(8,128)S(1)}, u32[]{:S(2)}, u32[]{:S(2)}) %collective-permute-start.31) | collective-permute-done | bytes 49184 | tf_op jit(solution)/shard_map/ppermute | solution.py:331
  148.5 2.6 %collective-permute-start.34 = (f32[9,16,256]{2,1,0:T(8,128)S(1)}, f32[9,16,256]{2,1,0:T(8,128)S(1)}, u32[]{:S(2)}, u32[]{:S(2)}) collective-permute-start(f32[9,16,256]{2,1,0:T(8,128)S(1)} %shard_map.128.cur), channel_id=1, source_target_pairs={{0,16},{4,20},{8,24},{12,28},{16,0},{20,4},{24,8},{28,12},{1,17},{... | collective-permute-start | bytes 442376 | tf_op jit(solution)/shard_map/ppermute | solution.py:331
  151.1 5.2 %collective-permute-done.34.got = f32[9,16,256]{2,1,0:T(8,128)S(1)} collective-permute-done((f32[9,16,256]{2,1,0:T(8,128)S(1)}, f32[9,16,256]{2,1,0:T(8,128)S(1)}, u32[]{:S(2)}, u32[]{:S(2)}) %collective-permute-start.34) | collective-permute-done | bytes 147488 | tf_op jit(solution)/shard_map/ppermute | solution.py:331
  156.9 2.1 %collective-permute-start.36 = (f32[3,16,256]{2,1,0:T(8,128)S(1)}, f32[3,16,256]{2,1,0:T(8,128)S(1)}, u32[]{:S(2)}, u32[]{:S(2)}) collective-permute-start(f32[3,16,256]{2,1,0:T(8,128)S(1)} %get-tuple-element.140.refs_1_), channel_id=1, source_target_pairs={{0,4},{4,0},{8,12},{12,8},{16,20},{20,16},{24,28},{28,24},{1,5},{5... | collective-permute-start | bytes 147464 | tf_op jit(solution)/shard_map/ppermute | solution.py:331
  161.1 2.0 %collective-permute-done.37.refs_5_ = f32[3,16,256]{2,1,0:T(8,128)S(1)} collective-permute-done((f32[3,16,256]{2,1,0:T(8,128)S(1)}, f32[3,16,256]{2,1,0:T(8,128)S(1)}, u32[]{:S(2)}, u32[]{:S(2)}) %collective-permute-start.37) | collective-permute-done | bytes 49184 | tf_op jit(solution)/shard_map/ppermute | solution.py:331
  167.1 2.3 %collective-permute-done.38.refs_3_ = f32[3,32,256]{2,1,0:T(8,128)S(1)} collective-permute-done((f32[3,32,256]{2,1,0:T(8,128)S(1)}, f32[3,32,256]{2,1,0:T(8,128)S(1)}, u32[]{:S(2)}, u32[]{:S(2)}) %collective-permute-start.38) | collective-permute-done | bytes 98336 | tf_op jit(solution)/shard_map/ppermute | solution.py:331
  174.6 2.9 %collective-permute-done.41.refs_3_ = f32[3,64,256]{2,1,0:T(8,128)S(1)} collective-permute-done((f32[3,64,256]{2,1,0:T(8,128)S(1)}, f32[3,64,256]{2,1,0:T(8,128)S(1)}, u32[]{:S(2)}, u32[]{:S(2)}) %collective-permute-start.41) | collective-permute-done | bytes 196640 | tf_op jit(solution)/shard_map/ppermute | solution.py:331
  182.7 2.4 %shard_map.133 = (f32[4,256,256]{2,1,0:T(8,128)}, f32[4,256,256]{2,1,0:T(8,128)}) custom-call(s32[66]{0:T(128)S(1)} %pad_add_fusion.sc, f32[9,128,256]{2,1,0:T(8,128)S(1)} %shard_map.132.mine, f32[9,128,256]{2,1,0:T(8,128)S(1)} %collective-permute-done.44.got, f32[4,256,256]{2,1,0:T(8,128)S(1)} %get-tuple-element.80.pr, f32[4,256,256]{2,1,0:T(8,128)S(1)} %get-tuple-element.81.pi), custom_call_target="tpu_custom_call" | custom-call | tf_op jit(solution)/shard_map/pallas_call | solution.py:59
  (99 shorter events, 63.0 us)
Async XLA Ops:
  1.9 14.4 %all-to-all-start = ((s32[32,1,128]{2,1,0:T(1,128)}), s32[32,1,128]{2,1,0:T(1,128)S(1)}, u32[]{:S(2)}, u32[]{:S(2)}) async-start(s32[32,1,128]{2,1,0:T(1,128)} %broadcast_in_dim.2), calls=%async_computation | async-start | bytes 32768 | tf_op jit(solution)/shard_map/all_to_all | solution.py:393
  10.1 8.5 %collective-permute-start.1 = (f32[2,128,128]{2,1,0:T(8,128)S(1)}, f32[2,128,128]{2,1,0:T(8,128)S(1)}, u32[]{:S(2)}, u32[]{:S(2)}) collective-permute-start(f32[2,128,128]{2,1,0:T(8,128)S(1)} %pad_maximum_fusion.s), channel_id=1, source_target_pairs={{0,28},{4,8},{8,4},{12,16},{16,12},{20,24},{24,20},{28,0},{1,29},{... | collective-permute-start | bytes 393224 | tf_op jit(solution)/shard_map/ppermute | solution.py:45
  14.7 6.6 %collective-permute-start = (f32[2,128,128]{2,1,0:T(8,128)S(1)}, f32[2,128,128]{2,1,0:T(8,128)S(1)}, u32[]{:S(2)}, u32[]{:S(2)}) collective-permute-start(f32[2,128,128]{2,1,0:T(8,128)S(1)} %pad_maximum_fusion.s), channel_id=1, source_target_pairs={{0,4},{4,0},{8,12},{12,8},{16,20},{20,16},{24,28},{28,24},{1,5},{5... | collective-permute-start | bytes 393224 | tf_op jit(solution)/shard_map/ppermute | solution.py:45
  22.0 7.6 %collective-permute-start.2 = (f32[2,256,128]{2,1,0:T(8,128)S(1)}, f32[2,256,128]{2,1,0:T(8,128)S(1)}, u32[]{:S(2)}, u32[]{:S(2)}) collective-permute-start(f32[2,256,128]{2,1,0:T(8,128)S(1)} %get-tuple-element.78), channel_id=1, source_target_pairs={{0,1},{1,0},{2,3},{3,2},{4,5},{5,4},{6,7},{7,6},{8,9},{9,8},{10,11... | collective-permute-start | bytes 786440 | tf_op jit(solution)/shard_map/ppermute | solution.py:45
  22.1 8.1 %collective-permute-start.3 = (f32[2,256,128]{2,1,0:T(8,128)S(1)}, f32[2,256,128]{2,1,0:T(8,128)S(1)}, u32[]{:S(2)}, u32[]{:S(2)}) collective-permute-start(f32[2,256,128]{2,1,0:T(8,128)S(1)} %get-tuple-element.79), channel_id=1, source_target_pairs={{0,3},{1,2},{2,1},{3,0},{4,7},{5,6},{6,5},{7,4},{8,11},{9,10},{10,... | collective-permute-start | bytes 786440 | tf_op jit(solution)/shard_map/ppermute | solution.py:45
  35.0 8.3 %collective-permute-start.5 = (f32[2,256,128]{2,1,0:T(8,128)S(1)}, f32[2,256,128]{2,1,0:T(8,128)S(1)}, u32[]{:S(2)}, u32[]{:S(2)}) collective-permute-start(f32[2,256,128]{2,1,0:T(8,128)S(1)} %get-tuple-element.87), channel_id=1, source_target_pairs={{0,3},{1,2},{2,1},{3,0},{4,7},{5,6},{6,5},{7,4},{8,11},{9,10},{10,... | collective-permute-start | bytes 786440 | tf_op jit(solution)/shard_map/ppermute | solution.py:45
  44.0 7.5 %collective-permute-start.6 = (f32[2,128,128]{2,1,0:T(8,128)S(1)}, f32[2,128,128]{2,1,0:T(8,128)S(1)}, u32[]{:S(2)}, u32[]{:S(2)}) collective-permute-start(f32[2,128,128]{2,1,0:T(8,128)S(1)} %get-tuple-element.89), channel_id=1, source_target_pairs={{0,4},{4,0},{8,12},{12,8},{16,20},{20,16},{24,28},{28,24},{1,5},{5... | collective-permute-start | bytes 393224 | tf_op jit(solution)/shard_map/ppermute | solution.py:45
  44.1 8.3 %collective-permute-start.7 = (f32[2,128,128]{2,1,0:T(8,128)S(1)}, f32[2,128,128]{2,1,0:T(8,128)S(1)}, u32[]{:S(2)}, u32[]{:S(2)}) collective-permute-start(f32[2,128,128]{2,1,0:T(8,128)S(1)} %get-tuple-element.90), channel_id=1, source_target_pairs={{0,28},{4,8},{8,4},{12,16},{16,12},{20,24},{24,20},{28,0},{1,29},{... | collective-permute-start | bytes 393224 | tf_op jit(solution)/shard_map/ppermute | solution.py:45
  53.0 7.7 %collective-permute-start.9 = (f32[2,128,128]{2,1,0:T(8,128)S(1)}, f32[2,128,128]{2,1,0:T(8,128)S(1)}, u32[]{:S(2)}, u32[]{:S(2)}) collective-permute-start(f32[2,128,128]{2,1,0:T(8,128)S(1)} %shard_map.116.s), channel_id=1, source_target_pairs={{0,28},{4,8},{8,4},{12,16},{16,12},{20,24},{24,20},{28,0},{1,29},{... | collective-permute-start | bytes 393224 | tf_op jit(solution)/shard_map/ppermute | solution.py:45
  55.8 6.9 %collective-permute-start.8 = (f32[2,128,128]{2,1,0:T(8,128)S(1)}, f32[2,128,128]{2,1,0:T(8,128)S(1)}, u32[]{:S(2)}, u32[]{:S(2)}) collective-permute-start(f32[2,128,128]{2,1,0:T(8,128)S(1)} %shard_map.116.s), channel_id=1, source_target_pairs={{0,4},{4,0},{8,12},{12,8},{16,20},{20,16},{24,28},{28,24},{1,5},{5... | collective-permute-start | bytes 393224 | tf_op jit(solution)/shard_map/ppermute | solution.py:45
  63.5 8.1 %collective-permute-start.11 = (f32[2,256,128]{2,1,0:T(8,128)S(1)}, f32[2,256,128]{2,1,0:T(8,128)S(1)}, u32[]{:S(2)}, u32[]{:S(2)}) collective-permute-start(f32[2,256,128]{2,1,0:T(8,128)S(1)} %get-tuple-element.93), channel_id=1, source_target_pairs={{0,3},{1,2},{2,1},{3,0},{4,7},{5,6},{6,5},{7,4},{8,11},{9,10},{10,... | collective-permute-start | bytes 786440 | tf_op jit(solution)/shard_map/ppermute | solution.py:45
  76.4 8.3 %collective-permute-start.13 = (f32[2,256,128]{2,1,0:T(8,128)S(1)}, f32[2,256,128]{2,1,0:T(8,128)S(1)}, u32[]{:S(2)}, u32[]{:S(2)}) collective-permute-start(f32[2,256,128]{2,1,0:T(8,128)S(1)} %get-tuple-element.96), channel_id=1, source_target_pairs={{0,3},{1,2},{2,1},{3,0},{4,7},{5,6},{6,5},{7,4},{8,11},{9,10},{10,... | collective-permute-start | bytes 786440 | tf_op jit(solution)/shard_map/ppermute | solution.py:45
  85.4 6.2 %collective-permute-start.14 = (f32[2,128,128]{2,1,0:T(8,128)S(1)}, f32[2,128,128]{2,1,0:T(8,128)S(1)}, u32[]{:S(2)}, u32[]{:S(2)}) collective-permute-start(f32[2,128,128]{2,1,0:T(8,128)S(1)} %get-tuple-element.98), channel_id=1, source_target_pairs={{0,4},{4,0},{8,12},{12,8},{16,20},{20,16},{24,28},{28,24},{1,5},{5... | collective-permute-start | bytes 393224 | tf_op jit(solution)/shard_map/ppermute | solution.py:45
  85.5 8.3 %collective-permute-start.15 = (f32[2,128,128]{2,1,0:T(8,128)S(1)}, f32[2,128,128]{2,1,0:T(8,128)S(1)}, u32[]{:S(2)}, u32[]{:S(2)}) collective-permute-start(f32[2,128,128]{2,1,0:T(8,128)S(1)} %get-tuple-element.99), channel_id=1, source_target_pairs={{0,28},{4,8},{8,4},{12,16},{16,12},{20,24},{24,20},{28,0},{1,29},{... | collective-permute-start | bytes 393224 | tf_op jit(solution)/shard_map/ppermute | solution.py:45
  94.4 7.7 %collective-permute-start.17 = (f32[2,128,128]{2,1,0:T(8,128)S(1)}, f32[2,128,128]{2,1,0:T(8,128)S(1)}, u32[]{:S(2)}, u32[]{:S(2)}) collective-permute-start(f32[2,128,128]{2,1,0:T(8,128)S(1)} %shard_map.120.s), channel_id=1, source_target_pairs={{0,28},{4,8},{8,4},{12,16},{16,12},{20,24},{24,20},{28,0},{1,29},{... | collective-permute-start | bytes 393224 | tf_op jit(solution)/shard_map/ppermute | solution.py:45
  96.7 7.2 %collective-permute-start.16 = (f32[2,128,128]{2,1,0:T(8,128)S(1)}, f32[2,128,128]{2,1,0:T(8,128)S(1)}, u32[]{:S(2)}, u32[]{:S(2)}) collective-permute-start(f32[2,128,128]{2,1,0:T(8,128)S(1)} %shard_map.120.s), channel_id=1, source_target_pairs={{0,4},{4,0},{8,12},{12,8},{16,20},{20,16},{24,28},{28,24},{1,5},{5... | collective-permute-start | bytes 393224 | tf_op jit(solution)/shard_map/ppermute | solution.py:45
  104.5 8.1 %collective-permute-start.19 = (f32[2,256,128]{2,1,0:T(8,128)S(1)}, f32[2,256,128]{2,1,0:T(8,128)S(1)}, u32[]{:S(2)}, u32[]{:S(2)}) collective-permute-start(f32[2,256,128]{2,1,0:T(8,128)S(1)} %get-tuple-element.102), channel_id=1, source_target_pairs={{0,3},{1,2},{2,1},{3,0},{4,7},{5,6},{6,5},{7,4},{8,11},{9,10},{10,... | collective-permute-start | bytes 786440 | tf_op jit(solution)/shard_map/ppermute | solution.py:45
  118.1 4.9 %collective-permute-start.24 = (f32[2,256,128]{2,1,0:T(8,128)S(1)}, f32[2,256,128]{2,1,0:T(8,128)S(1)}, u32[]{:S(2)}, u32[]{:S(2)}) collective-permute-start(f32[2,256,128]{2,1,0:T(8,128)S(1)} %get-tuple-element.109), channel_id=1, source_target_pairs={{0,1},{1,0},{2,3},{3,2},{4,5},{5,4},{6,7},{7,6},{8,9},{9,8},{10,11... | collective-permute-start | bytes 786440 | tf_op jit(solution)/shard_map/ppermute | solution.py:45
  118.2 8.3 %collective-permute-start.25 = (f32[2,256,128]{2,1,0:T(8,128)S(1)}, f32[2,256,128]{2,1,0:T(8,128)S(1)}, u32[]{:S(2)}, u32[]{:S(2)}) collective-permute-start(f32[2,256,128]{2,1,0:T(8,128)S(1)} %get-tuple-element.110), channel_id=1, source_target_pairs={{0,3},{1,2},{2,1},{3,0},{4,7},{5,6},{6,5},{7,4},{8,11},{9,10},{10,... | collective-permute-start | bytes 786440 | tf_op jit(solution)/shard_map/ppermute | solution.py:45
  121.3 7.2 %collective-permute-start.21 = (f32[3,64,256]{2,1,0:T(8,128)S(1)}, f32[3,64,256]{2,1,0:T(8,128)S(1)}, u32[]{:S(2)}, u32[]{:S(2)}) collective-permute-start(f32[3,64,256]{2,1,0:T(8,128)S(1)} %get-tuple-element.106), channel_id=1, source_target_pairs={{0,4},{4,0},{8,12},{12,8},{16,20},{20,16},{24,28},{28,24},{1,5},{5... | collective-permute-start | bytes 589832 | tf_op jit(solution)/shard_map/ppermute | solution.py:331
  121.4 9.7 %collective-permute-start.22 = (f32[3,64,256]{2,1,0:T(8,128)S(1)}, f32[3,64,256]{2,1,0:T(8,128)S(1)}, u32[]{:S(2)}, u32[]{:S(2)}) collective-permute-start(f32[3,64,256]{2,1,0:T(8,128)S(1)} %get-tuple-element.107), channel_id=1, source_target_pairs={{0,2},{1,3},{2,0},{3,1},{4,6},{5,7},{6,4},{7,5},{8,10},{9,11},{10,... | collective-permute-start | bytes 589832 | tf_op jit(solution)/shard_map/ppermute | solution.py:331
  123.0 8.0 %collective-permute-start.23 = (f32[3,64,256]{2,1,0:T(8,128)S(1)}, f32[3,64,256]{2,1,0:T(8,128)S(1)}, u32[]{:S(2)}, u32[]{:S(2)}) collective-permute-start(f32[3,64,256]{2,1,0:T(8,128)S(1)} %get-tuple-element.108), channel_id=1, source_target_pairs={{0,8},{4,12},{8,0},{12,4},{16,24},{20,28},{24,16},{28,20},{1,9},{5... | collective-permute-start | bytes 589832 | tf_op jit(solution)/shard_map/ppermute | solution.py:331
  131.7 10.5 %collective-permute-start.29 = (f32[2,128,128]{2,1,0:T(8,128)S(1)}, f32[2,128,128]{2,1,0:T(8,128)S(1)}, u32[]{:S(2)}, u32[]{:S(2)}) collective-permute-start(f32[2,128,128]{2,1,0:T(8,128)S(1)} %get-tuple-element.123), channel_id=1, source_target_pairs={{0,4},{4,0},{8,12},{12,8},{16,20},{20,16},{24,28},{28,24},{1,5},{5... | collective-permute-start | bytes 393224 | tf_op jit(solution)/shard_map/ppermute | solution.py:45
  132.3 9.8 %collective-permute-start.30 = (f32[2,128,128]{2,1,0:T(8,128)S(1)}, f32[2,128,128]{2,1,0:T(8,128)S(1)}, u32[]{:S(2)}, u32[]{:S(2)}) collective-permute-start(f32[2,128,128]{2,1,0:T(8,128)S(1)} %get-tuple-element.124), channel_id=1, source_target_pairs={{0,28},{4,8},{8,4},{12,16},{16,12},{20,24},{24,20},{28,0},{1,29},{... | collective-permute-start | bytes 393224 | tf_op jit(solution)/shard_map/ppermute | solution.py:45
  135.3 4.7 %collective-permute-start.26 = (f32[3,32,256]{2,1,0:T(8,128)S(1)}, f32[3,32,256]{2,1,0:T(8,128)S(1)}, u32[]{:S(2)}, u32[]{:S(2)}) collective-permute-start(f32[3,32,256]{2,1,0:T(8,128)S(1)} %get-tuple-element.120), channel_id=1, source_target_pairs={{0,2},{1,3},{2,0},{3,1},{4,6},{5,7},{6,4},{7,5},{8,10},{9,11},{10,... | collective-permute-start | bytes 294920 | tf_op jit(solution)/shard_map/ppermute | solution.py:331
  137.6 4.6 %collective-permute-start.28 = (f32[3,32,256]{2,1,0:T(8,128)S(1)}, f32[3,32,256]{2,1,0:T(8,128)S(1)}, u32[]{:S(2)}, u32[]{:S(2)}) collective-permute-start(f32[3,32,256]{2,1,0:T(8,128)S(1)} %get-tuple-element.122), channel_id=1, source_target_pairs={{0,4},{4,0},{8,12},{12,8},{16,20},{20,16},{24,28},{28,24},{1,5},{5... | collective-permute-start | bytes 294920 | tf_op jit(solution)/shard_map/ppermute | solution.py:331
  148.5 7.8 %collective-permute-start.34 = (f32[9,16,256]{2,1,0:T(8,128)S(1)}, f32[9,16,256]{2,1,0:T(8,128)S(1)}, u32[]{:S(2)}, u32[]{:S(2)}) collective-permute-start(f32[9,16,256]{2,1,0:T(8,128)S(1)} %shard_map.128.cur), channel_id=1, source_target_pairs={{0,16},{4,20},{8,24},{12,28},{16,0},{20,4},{24,8},{28,12},{1,17},{... | collective-permute-start | bytes 442376 | tf_op jit(solution)/shard_map/ppermute | solution.py:331
  163.7 5.7 %collective-permute-start.38 = (f32[3,32,256]{2,1,0:T(8,128)S(1)}, f32[3,32,256]{2,1,0:T(8,128)S(1)}, u32[]{:S(2)}, u32[]{:S(2)}) collective-permute-start(f32[3,32,256]{2,1,0:T(8,128)S(1)} %get-tuple-element.142.refs_0_), channel_id=1, source_target_pairs={{0,2},{1,3},{2,0},{3,1},{4,6},{5,7},{6,4},{7,5},{8,10},{9,11},{10,... | collective-permute-start | bytes 294920 | tf_op jit(solution)/shard_map/ppermute | solution.py:331
  164.6 5.7 %collective-permute-start.39 = (f32[3,32,256]{2,1,0:T(8,128)S(1)}, f32[3,32,256]{2,1,0:T(8,128)S(1)}, u32[]{:S(2)}, u32[]{:S(2)}) collective-permute-start(f32[3,32,256]{2,1,0:T(8,128)S(1)} %get-tuple-element.143.refs_1_), channel_id=1, source_target_pairs={{0,8},{4,12},{8,0},{12,4},{16,24},{20,28},{24,16},{28,20},{1,9},{5... | collective-permute-start | bytes 294920 | tf_op jit(solution)/shard_map/ppermute | solution.py:331
  171.8 5.7 %collective-permute-start.41 = (f32[3,64,256]{2,1,0:T(8,128)S(1)}, f32[3,64,256]{2,1,0:T(8,128)S(1)}, u32[]{:S(2)}, u32[]{:S(2)}) collective-permute-start(f32[3,64,256]{2,1,0:T(8,128)S(1)} %get-tuple-element.145.refs_0_), channel_id=1, source_target_pairs={{0,4},{4,0},{8,12},{12,8},{16,20},{20,16},{24,28},{28,24},{1,5},{5... | collective-permute-start | bytes 589832 | tf_op jit(solution)/shard_map/ppermute | solution.py:331
  172.4 5.7 %collective-permute-start.42 = (f32[3,64,256]{2,1,0:T(8,128)S(1)}, f32[3,64,256]{2,1,0:T(8,128)S(1)}, u32[]{:S(2)}, u32[]{:S(2)}) collective-permute-start(f32[3,64,256]{2,1,0:T(8,128)S(1)} %get-tuple-element.146.refs_1_), channel_id=1, source_target_pairs={{0,2},{1,3},{2,0},{3,1},{4,6},{5,7},{6,4},{7,5},{8,10},{9,11},{10,... | collective-permute-start | bytes 589832 | tf_op jit(solution)/shard_map/ppermute | solution.py:331
  173.5 5.7 %collective-permute-start.43 = (f32[3,64,256]{2,1,0:T(8,128)S(1)}, f32[3,64,256]{2,1,0:T(8,128)S(1)}, u32[]{:S(2)}, u32[]{:S(2)}) collective-permute-start(f32[3,64,256]{2,1,0:T(8,128)S(1)} %get-tuple-element.147.refs_2_), channel_id=1, source_target_pairs={{0,8},{4,12},{8,0},{12,4},{16,24},{20,28},{24,16},{28,20},{1,9},{5... | collective-permute-start | bytes 589832 | tf_op jit(solution)/shard_map/ppermute | solution.py:331
  (19 other events, 52.3 us)

commit v3 on v2

--- a/solution.py
+++ b/solution.py
@@ -19,7 +19,7 @@
 
 F32 = jnp.float32
 BF16 = jnp.bfloat16
-HEAD = 2
+COLORS = 3
 
 
 def tables(width):
@@ -49,7 +49,7 @@
     return swap(to_near, axis, False), swap(to_far, axis, True)
 
 
-def call(body, outs, scratch=(), smem=1, extra=1 << 20, cost=None):
+def call(body, outs, scratch=(), smem=0, extra=1 << 20, cost=None):
     def run(*args):
         held = sum(4 * math.prod(s) for s in outs) + sum(a.size * a.dtype.itemsize for a in args[smem:])
         held += sum(math.prod(s.shape) * 4 for s in scratch)
@@ -72,7 +72,7 @@
 class Place:
     def __init__(self, sc, sizes):
         n_row, n_col, rows, cols, rim = sizes
-        self.i, self.j = sc[0], sc[1]
+        self.i, self.j = lax.axis_index("row"), lax.axis_index("col")
         self.even_row = self.i % 2 == 0
         self.even_col = self.j % 2 == 0
         self.up = self.i > 0
@@ -81,18 +81,27 @@
         self.has_right = self.j < n_col - 1
         self.far_row = jnp.where(self.even_row, self.i, n_row - 1 - self.i) > 0
         self.far_col = jnp.where(self.even_col, self.j, n_col - 1 - self.j) > 0
+        if sc is None:
+            return
         near = jnp.where(self.even_col, self.j + 1, self.j - 1)
         far = jnp.where(self.even_col, self.j - 1, self.j + 1)
         far = jnp.where(self.far_col, far, self.j)
 
+        spots = sc[...]
+        index = lax.broadcasted_iota(jnp.int32, spots.shape, 0) * spots.shape[1]
+        index = index + lax.broadcasted_iota(jnp.int32, spots.shape, 1)
+
+        def known(col, part):
+            wanted = 2 * (self.i * n_col + col) + part
+            return jnp.sum(jnp.where(index == wanted, spots, 0.0)).astype(jnp.int32)
+
         def row_of(col):
-            at = sc[HEAD + 2 * (self.i * n_col + col)]
-            return pl.multiple_of(at - (self.i * rows - rim), rim // 2)
+            return pl.multiple_of(known(col, 0) - (self.i * rows - rim), rim // 2)
 
         self.row = row_of(self.j)
         self.near_row = row_of(near)
         self.far_row_at = row_of(far)
-        self.col = sc[HEAD + 2 * (self.i * n_col + self.j) + 1] - (self.j * cols - rim)
+        self.col = known(self.j, 1) - (self.j * cols - rim)
 
 
 def light_body(sizes, n_dev, sc, pr, pi, out, buf, pw):
@@ -112,8 +121,8 @@
     buf[...] = jnp.zeros_like(buf)
 
     def add(p, carry):
-        row = pl.multiple_of(sc[HEAD + 2 * p] + rim, half)
-        col = sc[HEAD + 2 * p + 1] + rim
+        row = pl.multiple_of(sc[2 * p] + rim, half)
+        col = sc[2 * p + 1] + rim
         odd = (col // half) % 2
         at = (pl.ds(row, width), pl.ds(pl.multiple_of(col - odd * half, rim), width + rim))
         buf[at] += pw[odd]
@@ -127,8 +136,8 @@
 
     peak = lax.fori_loop(0, n_row, peak_of, jnp.float32(0.0))
     mine = buf[
-        pl.ds(pl.multiple_of(sc[0] * rows + rim, rim), rows),
-        pl.ds(pl.multiple_of(sc[1] * cols + rim, rim), cols),
+        pl.ds(pl.multiple_of(lax.axis_index("row") * rows + rim, rim), rows),
+        pl.ds(pl.multiple_of(lax.axis_index("col") * cols + rim, rim), cols),
     ]
     out[...] = mine + light_ratio * peak
 
@@ -148,7 +157,7 @@
     return pl.pallas_call(
         stage_body,
         out_shape=[jax.ShapeDtypeStruct(a.shape, a.dtype) for a in arrays],
-        in_specs=[pl.BlockSpec(memory_space=pl.ANY)] * len(arrays),
+        in_specs=[pl.BlockSpec(memory_space=pltpu.HBM)] * len(arrays),
         out_specs=[pl.BlockSpec(memory_space=pltpu.VMEM)] * len(arrays),
         scratch_shapes=[pltpu.SemaphoreType.DMA((len(arrays),))],
         compiler_params=pltpu.CompilerParams(vmem_limit_bytes=size + (1 << 20)),
@@ -172,7 +181,7 @@
 
 def view_body(sizes, last, sc, mid, near, far, pr, pi, view, right_t, left_t, *refs):
     if last:
-        gm, to_near, to_far, keep, send, spec_scr, win_scr, term_scr = refs
+        gm, to_near, to_far, *parts, spec_scr, win_scr, term_scr = refs
     else:
         gm, to_near, to_far, spec_scr, win_scr = refs
     _, _, _, _, rim = sizes
@@ -235,8 +244,11 @@
         wr, wi = win_scr[0], win_scr[1]
         term_scr[2 * modes] = wr * wr + wi * wi
         bit = at.j % 2
-        keep[...] = term_scr[:, pl.ds(pl.multiple_of(bit * rim, rim), rim)]
-        send[...] = term_scr[:, pl.ds(pl.multiple_of((1 - bit) * rim, rim), rim)]
+        each = parts[0].shape[0]
+        for k, part in enumerate(parts):
+            at = slice((k // 2) * each, (k // 2 + 1) * each)
+            offset = (1 - bit if k % 2 else bit) * rim
+            part[...] = term_scr[at, pl.ds(pl.multiple_of(offset, rim), rim)]
 
 
 def fold_body(sizes, sc, gm, near, far, own, to_near, to_far, buf):
@@ -253,75 +265,54 @@
     to_far[...] = jnp.where(at.even_row, top, bottom)
 
 
-def step_body(sizes, sc, s, own, near, far, denom, out):
-    at = Place(sc, sizes)
+def step_body(sizes, s, own, near, far, denom, out):
+    at = Place(None, sizes)
     grad = own[...] + near[...] + jnp.where(at.far_row, far[...], 0.0)
     out[...] = s[...] + grad / denom[...][None]
 
 
-def bit_of(sc, axis, level):
-    return lax.shift_right_logical(sc[axis], level) % 2
-
-
-def halve_body(levels, height, shared, sc, *refs):
-    count = len(levels)
-    ins = 1 if shared else count
-    cur, got, out = refs[:ins], refs[ins : 2 * ins], refs[2 * ins :]
-    for c, (axis, level) in enumerate(levels):
-        bit = bit_of(sc, axis, level)
-        each = out[2 * c].shape[0]
-        for which, offset in ((0, bit * height), (1, (1 - bit) * height)):
-            rows = pl.ds(pl.multiple_of(offset, 8), height)
-            if shared:
-                at = (slice(c * each, (c + 1) * each), rows)
-                out[2 * c + which][...] = cur[0][at] + got[0][at]
-            else:
-                out[2 * c + which][...] = cur[c][:, rows] + got[c][:, rows]
-
-
-def gather_sum_body(count, sc, *refs):
-    cur, got, out = refs[:count], refs[count : 2 * count], refs[2 * count]
-    each = cur[0].shape[0]
-    for c in range(count):
-        out[c * each : (c + 1) * each] = cur[c][...] + got[c][...]
-
-
-def spread_sum_body(count, sc, cur, got, *out):
-    each = out[0].shape[0]
-    for c in range(count):
-        at = slice(c * each, (c + 1) * each)
-        out[c][...] = cur[at] + got[at]
-
-
-def sum_body(sc, cur, got, out):
+def bit_of(axis, level):
+    return lax.shift_right_logical(lax.axis_index(("row", "col")[axis]), level) % 2
+
+
+def halve_body(where, cur, got, keep, send):
+    bit = bit_of(*where)
+    height = keep.shape[1]
+    for out, offset in ((keep, bit * height), (send, (1 - bit) * height)):
+        rows = pl.ds(pl.multiple_of(offset, 8), height)
+        out[...] = cur[:, rows] + got[:, rows]
+
+
+def sum_body(cur, got, out):
     out[...] = cur[...] + got[...]
 
 
-def join_body(levels, height, shared, sc, *refs):
-    count = len(levels)
-    cur, got, out = refs[:count], refs[count : 2 * count], refs[2 * count :]
-    for c, (axis, level) in enumerate(levels):
-        bit = bit_of(sc, axis, level)
-        each = cur[c].shape[0]
-        for src, offset in ((cur[c], bit * height), (got[c], (1 - bit) * height)):
-            rows = pl.ds(pl.multiple_of(offset, 8), height)
-            if shared:
-                out[0][c * each : (c + 1) * each, rows] = src[...]
-            else:
-                out[c][:, rows] = src[...]
-
-
-def probe_body(rim, sc, mine, got, pr, pi, new_re, new_im):
+def join_body(where, cur, got, out):
+    bit = bit_of(*where)
+    height = cur.shape[1]
+    for src, offset in ((cur, bit * height), (got, (1 - bit) * height)):
+        out[:, pl.ds(pl.multiple_of(offset, 8), height)] = src[...]
+
+
+def probe_body(rim, *refs):
+    colors = (len(refs) - 4) // 2
+    mine, got = refs[:colors], refs[colors : 2 * colors]
+    pr, pi, new_re, new_im = refs[2 * colors :]
     modes = pr.shape[0]
+    each = mine[0].shape[0]
     pixels = 4 * rim * rim
-    bit = sc[1] % 2
-    mean = (jnp.sum(mine[2 * modes]) + jnp.sum(got[2 * modes])) / pixels
+    bit = lax.axis_index("col") % 2
+
+    def term(src, k):
+        return src[k // each][k % each]
+
+    mean = (jnp.sum(term(mine, 2 * modes)) + jnp.sum(term(got, 2 * modes))) / pixels
     for src, offset in ((mine, bit * rim), (got, (1 - bit) * rim)):
         rows = pl.ds(pl.multiple_of(offset, rim), rim)
-        scale = probe_step / (src[2 * modes] + mass_ratio * mean)
+        scale = probe_step / (term(src, 2 * modes) + mass_ratio * mean)
         for m in range(modes):
-            new_re[m, rows] = pr[m, rows] + src[m] * scale
-            new_im[m, rows] = pi[m, rows] + src[modes + m] * scale
+            new_re[m, rows] = pr[m, rows] + term(src, m) * scale
+            new_im[m, rows] = pi[m, rows] + term(src, modes + m) * scale
 
 
 def swap_bit(array, where):
@@ -331,10 +322,9 @@
     return lax.ppermute(array, name, [(i, i ^ (1 << level)) for i in range(count)])
 
 
-def sum_terms(sc, keep, send, n_row, n_col, beside):
-    parts, height, width = keep.shape
-    colors = 3
-    each = parts // colors
+def sum_terms(keeps, sends, n_row, n_col, beside):
+    colors = len(keeps)
+    each, height, width = keeps[0].shape
     row_bits = [(0, k) for k in range(n_row.bit_length() - 1)]
     col_bits = [(1, k) for k in range(1, n_col.bit_length() - 1)]
     rest = []
@@ -346,38 +336,48 @@
     turn = rest[:colors]
     orders = [turn[c:] + turn[:c] for c in range(colors)]
     tail = rest[colors:]
-    got = swap_bit(send, (1, 0))
-    curs, gots, shared = [keep], [got], True
-    steps = []
+    curs = list(keeps)
+    gots = [swap_bit(a, (1, 0)) for a in sends]
     for r in range(len(turn)):
-        levels = [orders[c][r] for c in range(colors)]
         height //= 2
-        outs = [(each, height, width)] * (2 * colors)
-        res = call(functools.partial(halve_body, levels, height, shared), outs)(sc, *curs, *gots)
-        curs, sends = res[0::2], res[1::2]
-        gots = [swap_bit(a, w) for a, w in zip(sends, levels)]
-        gots = beside(r, gots)
-        shared = False
-        steps.append(levels)
-    (cur,) = call(functools.partial(gather_sum_body, colors), [(parts, height, width)])(
-        sc, *curs, *gots
-    )
-    for where in tail[:-1]:
-        got = swap_bit(cur, where)
-        (cur,) = call(sum_body, [cur.shape])(sc, cur, got)
-    got = swap_bit(cur, tail[-1])
-    curs = call(functools.partial(spread_sum_body, colors), [(each, height, width)] * colors)(
-        sc, cur, got
-    )
-    for levels in reversed(steps):
-        gots = [swap_bit(a, w) for a, w in zip(curs, levels)]
-        final = levels is steps[0]
-        shape = (each, 2 * height, width)
-        outs = [(parts, 2 * height, width)] if final else [shape] * colors
-        curs = call(functools.partial(join_body, levels, height, final), outs)(sc, *curs, *gots)
+        for c in range(colors):
+            where = orders[c][r]
+            outs = [(each, height, width)] * 2
+            keep, send = call(functools.partial(halve_body, where), outs)(curs[c], gots[c])
+            curs[c], gots[c] = keep, swap_bit(send, where)
+        gots = list(beside(r, gots))
+    for k, where in enumerate([None] + tail):
+        for c in range(colors):
+            (curs[c],) = call(sum_body, [curs[c].shape])(curs[c], gots[c])
+            if k < len(tail):
+                gots[c] = swap_bit(curs[c], tail[k])
+    for r in reversed(range(len(turn))):
+        for c in range(colors):
+            where = orders[c][r]
+            got = swap_bit(curs[c], where)
+            outs = [(each, 2 * height, width)]
+            (curs[c],) = call(functools.partial(join_body, where), outs)(curs[c], got)
         height *= 2
-    mine = curs[0]
-    return mine, swap_bit(mine, (1, 0))
+    return curs, [swap_bit(a, (1, 0)) for a in curs]
+
+
+def enter_body(n_col, pos, spots):
+    at = lax.broadcasted_iota(jnp.int32, spots.shape, 0) * spots.shape[1]
+    at = at + lax.broadcasted_iota(jnp.int32, spots.shape, 1)
+    me = lax.axis_index("row") * n_col + lax.axis_index("col")
+    mine = jnp.where(at == 2 * me, pos[0], jnp.where(at == 2 * me + 1, pos[1], 0))
+    spots[...] = mine.astype(F32)
+
+
+def all_spots(known, n_row, n_col):
+    bits = [(1, k) for k in range(n_col.bit_length() - 1)]
+    local_bits = len(bits)
+    bits += [(0, k) for k in range(n_row.bit_length() - 1)]
+    stops = []
+    for where in bits:
+        known = known + swap_bit(known, where)
+        stops.append(known)
+    return stops[local_bits - 1], known
 
 
 def local(obj_re, obj_im, probe_re, probe_im, amps, positions):
@@ -389,22 +389,23 @@
     sizes = (n_row, n_col, rows, cols, rim)
     right_np, left_np = tables(width)
     right_t, left_t = jnp.asarray(right_np), jnp.asarray(left_np)
-    mine = jnp.broadcast_to(jnp.pad(positions.reshape(1, 2), ((0, 0), (0, 126))), (n_dev, 128))
-    spots = lax.all_to_all(mine, ("row", "col"), 0, 0, tiled=True)
-    spots = spots[:, :2].reshape(-1)
-    here = jnp.stack([lax.axis_index("row"), lax.axis_index("col")]).astype(jnp.int32)
-    sc = jnp.concatenate([here, spots])
+    state = jnp.stack([obj_re, obj_im])
+    shape = (-(-2 * n_row * n_col // 128), 128)
+    (known,) = call(functools.partial(enter_body, n_col), [shape], smem=1)(positions.reshape(2))
+    sc, every = all_spots(known, n_row, n_col)
     view = amps.reshape(width, width)
-    probe_re, probe_im, view, right_t, left_t = stage(probe_re, probe_im, view, right_t, left_t)
+    staged = stage(probe_re, probe_im, view, right_t, left_t)
+    probe_re, probe_im, view, right_t, left_t = staged
 
     grid = (n_row * rows + 2 * rim, n_col * cols + 3 * rim)
     (denom,) = call(
         functools.partial(light_body, sizes, n_dev),
         [(rows, cols)],
         [pltpu.VMEM(grid, F32), pltpu.VMEM((2, width, width + rim), F32)],
+        1,
         extra=4 << 20,
         cost=pl.CostEstimate(flops=8 * n_dev * width * width, bytes_accessed=10**7, transcendentals=0),
-    )(sc, probe_re, probe_im)
+    )(every.reshape(-1).astype(jnp.int32), probe_re, probe_im)
 
     strip = (2, width, cols)
     tile = (2, rows, cols)
@@ -413,15 +414,14 @@
     fold = call(functools.partial(fold_body, sizes), [tile] * 3, [tall])
     step = call(functools.partial(step_body, sizes), [tile])
     scratch = [pltpu.VMEM((modes, 2 * width, width), F32), pltpu.VMEM((2, width, width), F32)]
-    terms = (2 * modes + 1, rim, width)
-
-    state = jnp.stack([obj_re, obj_im])
+    terms = ((2 * modes + 1) // COLORS, rim, width)
+
     for turn in range(ITERS):
         last = turn == ITERS - 1
         near, far = swap_both(state, state, "row")
         mid, to_near, to_far = halo(sc, state, near, far)
         near, far = swap_both(to_near, to_far, "col")
-        outs = [strip] * 3 + ([terms] * 2 if last else [])
+        outs = [strip] * 3 + ([terms] * 2 * COLORS if last else [])
         scr = scratch + ([pltpu.VMEM((2 * modes + 1, width, width), F32)] if last else [])
         res = call(functools.partial(view_body, sizes, last), outs, scr, extra=8 << 20)(
             sc, mid, near, far, probe_re, probe_im, view, right_t, left_t
@@ -432,24 +432,24 @@
             break
         own, to_near, to_far = fold(sc, gm, near, far)
         near, far = swap_both(to_near, to_far, "row")
-        (state,) = step(sc, state, own, near, far, denom)
+        (state,) = step(state, own, near, far, denom)
 
     held = {}
 
     def beside(r, gots):
         if r == 0:
-            *gots, a, b = lax.optimization_barrier([*gots, near, far])
+            gots[0], a, b = lax.optimization_barrier((gots[0], near, far))
             held["own"], to_near, to_far = fold(sc, gm, a, b)
             held["both"] = swap_both(to_near, to_far, "row")
         elif r == 1:
-            *gots, a, b = lax.optimization_barrier([*gots, *held["both"]])
-            (held["state"],) = step(sc, state, held["own"], a, b, denom)
+            gots[2], a, b = lax.optimization_barrier((gots[2], *held["both"]))
+            (held["state"],) = step(state, held["own"], a, b, denom)
         return gots
 
-    mine, other = sum_terms(sc, res[3], res[4], n_row, n_col, beside)
+    mine, other = sum_terms(res[3::2], res[4::2], n_row, n_col, beside)
     shape = (modes, width, width)
     new_re, new_im = call(functools.partial(probe_body, rim), [shape] * 2)(
-        sc, mine, other, probe_re, probe_im
+        *mine, *other, probe_re, probe_im
     )
     return (held["state"][0], held["state"][1], new_re, new_im)
 

time: 186 us -> 157 us (0.84)
  waiting for transfers between devices: 90.2 us -> 75.1 us
  Pallas kernels: 31.1 us -> 20.9 us
    pallas_call x22 -> x39, Pallas kernels: 30.8 us -> 20.6 us  [run(): pl.pallas_call(body, out_shape=[jax.ShapeDtypeStruct(s, F32) for s in out...]
    ppermute x24, waiting for transfers between devices: 56.9 us -> 48.7 us  [swap(): return lax.ppermute(array, axis, pairs)]
    all_to_all x1 -> x0, starting transfers between devices: 7.33 us -> none  [local(): spots = lax.all_to_all(mine, ('row', 'col'), 0, 0, tiled=True)]
    ppermute x21 -> x32, starting transfers between devices: 18.3 us -> 25 us  [swap_bit(): lax.ppermute(array, name, [(i, i ^ 1 << level) for i in range(count)])]
    ppermute x21 -> x32, waiting for transfers between devices: 31.7 us -> 26.4 us  [swap_bit(): lax.ppermute(array, name, [(i, i ^ 1 << level) for i in range(count)])]
    unnamed x10 -> x12, local copies, waits for them, and re-layouts: 5.48 us -> 5.1 us
  transfers between devices with their start and end apart: 46 -> 56, of which waited for: 35 -> 36; matrix products, arithmetic and copies ran while one was open for 1% -> 0% of each run, Pallas kernels for 3% -> 4%
where the time goes in v3:
time: 157 us
  waiting for transfers between devices  75.1 us (48%)
  starting transfers between devices  53.1 us (34%)
  Pallas kernels  20.9 us (13%)
  local copies, waits for them, and re-layouts  5.76 us (4%)
    ppermute x24, waiting for transfers between devices, swap(): return lax.ppermute(array, axis, pairs)  48.7 us
    ppermute x24, starting transfers between devices, swap(): return lax.ppermute(array, axis, pairs)  28.2 us
    ppermute x32, waiting for transfers between devices, swap_bit(): lax.ppermute(array, name, [(i, i ^ 1 << level) for i in range(count)])  26.4 us
    ppermute x32, starting transfers between devices, swap_bit(): lax.ppermute(array, name, [(i, i ^ 1 << level) for i in range(count)])  25 us
    pallas_call x39, Pallas kernels, run(): pl.pallas_call(body, out_shape=[jax.ShapeDtypeStruct(s, F32) for s in out...  20.6 us
    unnamed x12, local copies, waits for them, and re-layouts  5.1 us
  transfers between devices with their start and end apart: 56, of which 36 were waited for; matrix products, arithmetic and copies ran while one was open for 0% of the time, Pallas kernels for 4%

profile of v3, /device:TPU:0, one launch (start us, length us, event | category | flops | bytes accessed | tf_op | source)
XLA Modules:
  0.0 156.9 jit_solution(10781742271379520161)
XLA Ops:
  1.6 6.1 %collective-permute-start.3 = (f32[2,128,128]{2,1,0:T(8,128)S(1)}, f32[2,128,128]{2,1,0:T(8,128)S(1)}, u32[]{:S(2)}, u32[]{:S(2)}) collective-permute-start(f32[2,128,128]{2,1,0:T(8,128)S(1)} %pad_maximum_fusion.s), channel_id=1, source_target_pairs={{0,28},{4,8},{8,4},{12,16},{16,12},{20,24},{24,20},{28,0},{1,29},{... | collective-permute-start | bytes 393224 | tf_op jit(solution)/shard_map/ppermute | solution.py:45
  11.6 2.0 %collective-permute-done.1 = f32[1,128]{1,0:T(1,128)S(1)} collective-permute-done((f32[1,128]{1,0:T(1,128)S(1)}, f32[1,128]{1,0:T(1,128)S(1)}, u32[]{:S(2)}, u32[]{:S(2)}) %collective-permute-start.1) | collective-permute-done | bytes 544 | tf_op jit(solution)/shard_map/ppermute | solution.py:322
  14.2 1.6 %collective-permute-start.5 = (f32[2,256,128]{2,1,0:T(8,128)S(1)}, f32[2,256,128]{2,1,0:T(8,128)S(1)}, u32[]{:S(2)}, u32[]{:S(2)}) collective-permute-start(f32[2,256,128]{2,1,0:T(8,128)S(1)} %get-tuple-element.70), channel_id=1, source_target_pairs={{0,3},{1,2},{2,1},{3,0},{4,7},{5,6},{6,5},{7,4},{8,11},{9,10},{10,... | collective-permute-start | bytes 786440 | tf_op jit(solution)/shard_map/ppermute | solution.py:45
  20.6 1.7 %collective-permute-done.5.far = f32[2,256,128]{2,1,0:T(8,128)S(1)} collective-permute-done((f32[2,256,128]{2,1,0:T(8,128)S(1)}, f32[2,256,128]{2,1,0:T(8,128)S(1)}, u32[]{:S(2)}, u32[]{:S(2)}) %collective-permute-start.5) | collective-permute-done | bytes 262176 | tf_op jit(solution)/shard_map/ppermute | solution.py:45
  22.3 3.8 %shard_map.114 = (f32[2,256,128]{2,1,0:T(8,128)S(1)}, f32[2,256,128]{2,1,0:T(8,128)S(1)}, f32[2,256,128]{2,1,0:T(8,128)S(1)}) custom-call(f32[1,128]{1,0:T(1,128)S(1)} %add.16.sc, f32[2,256,128]{2,1,0:T(8,128)S(1)} %get-tuple-element.68.mid, f32[2,256,128]{2,1,0:T(8,128)S(1)} %collective-permute-done.4.near, f32[2,256,128]{2,1,0:T(8,128)S(1)} %collective-permute-done.5.far, ...), custom_call_target="tpu_custom_call" | custom-call | tf_op jit(solution)/shard_map/pallas_call | solution.py:59
  27.8 1.8 %collective-permute-start.10 = (f32[1,128]{1,0:T(1,128)S(1)}, f32[1,128]{1,0:T(1,128)S(1)}, u32[]{:S(2)}, u32[]{:S(2)}) collective-permute-start(f32[1,128]{1,0:T(1,128)S(1)} %add.16.sc), channel_id=1, source_target_pairs={{0,4},{4,0},{8,12},{12,8},{16,20},{20,16},{24,28},{28,24},{1,5},{5... | collective-permute-start | bytes 1544 | tf_op jit(solution)/shard_map/ppermute | solution.py:322
  29.6 1.8 %collective-permute-done.10 = f32[1,128]{1,0:T(1,128)S(1)} collective-permute-done((f32[1,128]{1,0:T(1,128)S(1)}, f32[1,128]{1,0:T(1,128)S(1)}, u32[]{:S(2)}, u32[]{:S(2)}) %collective-permute-start.10) | collective-permute-done | bytes 544 | tf_op jit(solution)/shard_map/ppermute | solution.py:322
  31.4 3.6 %collective-permute-done.11 = f32[1,128]{1,0:T(1,128)S(1)} collective-permute-done((f32[1,128]{1,0:T(1,128)S(1)}, f32[1,128]{1,0:T(1,128)S(1)}, u32[]{:S(2)}, u32[]{:S(2)}) %collective-permute-start.11) | collective-permute-done | bytes 544 | tf_op jit(solution)/shard_map/ppermute | solution.py:322
  37.5 1.6 %collective-permute-start.9 = (f32[2,128,128]{2,1,0:T(8,128)S(1)}, f32[2,128,128]{2,1,0:T(8,128)S(1)}, u32[]{:S(2)}, u32[]{:S(2)}) collective-permute-start(f32[2,128,128]{2,1,0:T(8,128)S(1)} %get-tuple-element.81), channel_id=1, source_target_pairs={{0,28},{4,8},{8,4},{12,16},{16,12},{20,24},{24,20},{28,0},{1,29},{... | collective-permute-start | bytes 393224 | tf_op jit(solution)/shard_map/ppermute | solution.py:45
  39.4 4.2 %shard_map.116.denom = f32[128,128]{1,0:T(8,128)S(1)} custom-call(s32[128]{0:T(128)S(1)} %convert_bitcast_fusion.sc, f32[4,256,256]{2,1,0:T(8,128)S(1)} %get-tuple-element.71.pr.refs_6_, f32[4,256,256]{2,1,0:T(8,128)S(1)} %get-tuple-element.72.pi.refs_7_), custom_call_target="tpu_custom_call" | custom-call | flops 16777216 | bytes 10000000 | tf_op jit(solution)/shard_map/pallas_call | solution.py:59
  45.2 1.7 %collective-permute-start.14 = (f32[2,128,128]{2,1,0:T(8,128)S(1)}, f32[2,128,128]{2,1,0:T(8,128)S(1)}, u32[]{:S(2)}, u32[]{:S(2)}) collective-permute-start(f32[2,128,128]{2,1,0:T(8,128)S(1)} %shard_map.117.s), channel_id=1, source_target_pairs={{0,28},{4,8},{8,4},{12,16},{16,12},{20,24},{24,20},{28,0},{1,29},{... | collective-permute-start | bytes 393224 | tf_op jit(solution)/shard_map/ppermute | solution.py:45
  46.9 6.1 %collective-permute-done.14.far = f32[2,128,128]{2,1,0:T(8,128)S(1)} collective-permute-done((f32[2,128,128]{2,1,0:T(8,128)S(1)}, f32[2,128,128]{2,1,0:T(8,128)S(1)}, u32[]{:S(2)}, u32[]{:S(2)}) %collective-permute-start.14) | collective-permute-done | bytes 131104 | tf_op jit(solution)/shard_map/ppermute | solution.py:45
  55.5 6.4 %collective-permute-done.16.far = f32[2,256,128]{2,1,0:T(8,128)S(1)} collective-permute-done((f32[2,256,128]{2,1,0:T(8,128)S(1)}, f32[2,256,128]{2,1,0:T(8,128)S(1)}, u32[]{:S(2)}, u32[]{:S(2)}) %collective-permute-start.16) | collective-permute-done | bytes 262176 | tf_op jit(solution)/shard_map/ppermute | solution.py:45
  62.0 3.8 %shard_map.119 = (f32[2,256,128]{2,1,0:T(8,128)S(1)}, f32[2,256,128]{2,1,0:T(8,128)S(1)}, f32[2,256,128]{2,1,0:T(8,128)S(1)}) custom-call(f32[1,128]{1,0:T(1,128)S(1)} %add.16.sc, f32[2,256,128]{2,1,0:T(8,128)S(1)} %get-tuple-element.82.mid, f32[2,256,128]{2,1,0:T(8,128)S(1)} %collective-permute-done.15.near, ...), custom_call_target="tpu_custom_call" | custom-call | tf_op jit(solution)/shard_map/pallas_call | solution.py:59
  67.5 7.1 %collective-permute-done.18.far = f32[2,256,128]{2,1,0:T(8,128)S(1)} collective-permute-done((f32[2,256,128]{2,1,0:T(8,128)S(1)}, f32[2,256,128]{2,1,0:T(8,128)S(1)}, u32[]{:S(2)}, u32[]{:S(2)}) %collective-permute-start.18) | collective-permute-done | bytes 262176 | tf_op jit(solution)/shard_map/ppermute | solution.py:45
  75.0 2.6 %collective-permute-start.20 = (f32[2,128,128]{2,1,0:T(8,128)S(1)}, f32[2,128,128]{2,1,0:T(8,128)S(1)}, u32[]{:S(2)}, u32[]{:S(2)}) collective-permute-start(f32[2,128,128]{2,1,0:T(8,128)S(1)} %get-tuple-element.90), channel_id=1, source_target_pairs={{0,28},{4,8},{8,4},{12,16},{16,12},{20,24},{24,20},{28,0},{1,29},{... | collective-permute-start | bytes 393224 | tf_op jit(solution)/shard_map/ppermute | solution.py:45
  77.5 3.6 %collective-permute-done.19.near = f32[2,128,128]{2,1,0:T(8,128)S(1)} collective-permute-done((f32[2,128,128]{2,1,0:T(8,128)S(1)}, f32[2,128,128]{2,1,0:T(8,128)S(1)}, u32[]{:S(2)}, u32[]{:S(2)}) %collective-permute-start.19) | collective-permute-done | bytes 131104 | tf_op jit(solution)/shard_map/ppermute | solution.py:45
  81.1 2.2 %collective-permute-done.20.far = f32[2,128,128]{2,1,0:T(8,128)S(1)} collective-permute-done((f32[2,128,128]{2,1,0:T(8,128)S(1)}, f32[2,128,128]{2,1,0:T(8,128)S(1)}, u32[]{:S(2)}, u32[]{:S(2)}) %collective-permute-start.20) | collective-permute-done | bytes 131104 | tf_op jit(solution)/shard_map/ppermute | solution.py:45
  83.3 2.8 %collective-permute-start.22 = (f32[2,128,128]{2,1,0:T(8,128)S(1)}, f32[2,128,128]{2,1,0:T(8,128)S(1)}, u32[]{:S(2)}, u32[]{:S(2)}) collective-permute-start(f32[2,128,128]{2,1,0:T(8,128)S(1)} %shard_map.121.s), channel_id=1, source_target_pairs={{0,28},{4,8},{8,4},{12,16},{16,12},{20,24},{24,20},{28,0},{1,29},{... | collective-permute-start | bytes 393224 | tf_op jit(solution)/shard_map/ppermute | solution.py:45
  86.1 4.9 %collective-permute-done.22.far = f32[2,128,128]{2,1,0:T(8,128)S(1)} collective-permute-done((f32[2,128,128]{2,1,0:T(8,128)S(1)}, f32[2,128,128]{2,1,0:T(8,128)S(1)}, u32[]{:S(2)}, u32[]{:S(2)}) %collective-permute-start.22) | collective-permute-done | bytes 131104 | tf_op jit(solution)/shard_map/ppermute | solution.py:45
  91.1 2.5 %collective-permute-done.21.near = f32[2,128,128]{2,1,0:T(8,128)S(1)} collective-permute-done((f32[2,128,128]{2,1,0:T(8,128)S(1)}, f32[2,128,128]{2,1,0:T(8,128)S(1)}, u32[]{:S(2)}, u32[]{:S(2)}) %collective-permute-start.21) | collective-permute-done | bytes 131104 | tf_op jit(solution)/shard_map/ppermute | solution.py:45
  95.3 6.5 %collective-permute-done.24.far = f32[2,256,128]{2,1,0:T(8,128)S(1)} collective-permute-done((f32[2,256,128]{2,1,0:T(8,128)S(1)}, f32[2,256,128]{2,1,0:T(8,128)S(1)}, u32[]{:S(2)}, u32[]{:S(2)}) %collective-permute-start.24) | collective-permute-done | bytes 262176 | tf_op jit(solution)/shard_map/ppermute | solution.py:45
  101.9 4.4 %shard_map.123 = (f32[2,256,128]{2,1,0:T(8,128)S(1)}, f32[2,256,128]{2,1,0:T(8,128)S(1)}, f32[2,256,128]{2,1,0:T(8,128)S(1)}, f32[3,128,256]{2,1,0:T(8,128)S(1)}...) custom-call(f32[1,128]{1,0:T(1,128)S(1)} %add.16.sc, ...), custom_call_target="tpu_custom_call" | custom-call | tf_op jit(solution)/shard_map/pallas_call | solution.py:59
  110.3 5.2 %collective-permute-done.28.far = f32[2,256,128]{2,1,0:T(8,128)S(1)} collective-permute-done((f32[2,256,128]{2,1,0:T(8,128)S(1)}, f32[2,256,128]{2,1,0:T(8,128)S(1)}, u32[]{:S(2)}, u32[]{:S(2)}) %collective-permute-start.28) | collective-permute-done | bytes 262176 | tf_op jit(solution)/shard_map/ppermute | solution.py:45
  116.3 1.7 %collective-permute-start.33 = (f32[2,128,128]{2,1,0:T(8,128)S(1)}, f32[2,128,128]{2,1,0:T(8,128)S(1)}, u32[]{:S(2)}, u32[]{:S(2)}) collective-permute-start(f32[2,128,128]{2,1,0:T(8,128)S(1)} %get-tuple-element.109), channel_id=1, source_target_pairs={{0,28},{4,8},{8,4},{12,16},{16,12},{20,24},{24,20},{28,0},{1,29},{... | collective-permute-start | bytes 393224 | tf_op jit(solution)/shard_map/ppermute | solution.py:45
  120.9 2.5 %collective-permute-done.34.got = f32[3,32,256]{2,1,0:T(8,128)S(1)} collective-permute-done((f32[3,32,256]{2,1,0:T(8,128)S(1)}, f32[3,32,256]{2,1,0:T(8,128)S(1)}, u32[]{:S(2)}, u32[]{:S(2)}) %collective-permute-start.34) | collective-permute-done | bytes 98336 | tf_op jit(solution)/shard_map/ppermute | solution.py:322
  125.9 2.1 %collective-permute-start.43 = (f32[3,16,256]{2,1,0:T(8,128)S(1)}, f32[3,16,256]{2,1,0:T(8,128)S(1)}, u32[]{:S(2)}, u32[]{:S(2)}) collective-permute-start(f32[3,16,256]{2,1,0:T(8,128)S(1)} %get-tuple-element.125), channel_id=1, source_target_pairs={{0,4},{4,0},{8,12},{12,8},{16,20},{20,16},{24,28},{28,24},{1,5},{5... | collective-permute-start | bytes 147464 | tf_op jit(solution)/shard_map/ppermute | solution.py:322
  130.1 1.9 %collective-permute-start.44 = (f32[3,16,256]{2,1,0:T(8,128)S(1)}, f32[3,16,256]{2,1,0:T(8,128)S(1)}, u32[]{:S(2)}, u32[]{:S(2)}) collective-permute-start(f32[3,16,256]{2,1,0:T(8,128)S(1)} %shard_map.139.cur), channel_id=1, source_target_pairs={{0,16},{4,20},{8,24},{12,28},{16,0},{20,4},{24,8},{28,12},{1,17},{... | collective-permute-start | bytes 147464 | tf_op jit(solution)/shard_map/ppermute | solution.py:322
  133.2 2.4 %collective-permute-done.36.got = f32[3,16,256]{2,1,0:T(8,128)S(1)} collective-permute-done((f32[3,16,256]{2,1,0:T(8,128)S(1)}, f32[3,16,256]{2,1,0:T(8,128)S(1)}, u32[]{:S(2)}, u32[]{:S(2)}) %collective-permute-start.36) | collective-permute-done | bytes 49184 | tf_op jit(solution)/shard_map/ppermute | solution.py:322
  136.6 1.9 %collective-permute-start.45 = (f32[3,16,256]{2,1,0:T(8,128)S(1)}, f32[3,16,256]{2,1,0:T(8,128)S(1)}, u32[]{:S(2)}, u32[]{:S(2)}) collective-permute-start(f32[3,16,256]{2,1,0:T(8,128)S(1)} %shard_map.140.cur), channel_id=1, source_target_pairs={{0,4},{4,0},{8,12},{12,8},{16,20},{20,16},{24,28},{28,24},{1,5},{5... | collective-permute-start | bytes 147464 | tf_op jit(solution)/shard_map/ppermute | solution.py:322
  148.3 1.9 %collective-permute-done.39.got = f32[3,64,256]{2,1,0:T(8,128)S(1)} collective-permute-done((f32[3,64,256]{2,1,0:T(8,128)S(1)}, f32[3,64,256]{2,1,0:T(8,128)S(1)}, u32[]{:S(2)}, u32[]{:S(2)}) %collective-permute-start.39) | collective-permute-done | bytes 196640 | tf_op jit(solution)/shard_map/ppermute | solution.py:322
  155.0 1.9 %shard_map.150 = (f32[4,256,256]{2,1,0:T(8,128)}, f32[4,256,256]{2,1,0:T(8,128)}) custom-call(f32[3,128,256]{2,1,0:T(8,128)S(1)} %shard_map.135.refs_0_, f32[3,128,256]{2,1,0:T(8,128)S(1)} %shard_map.143.refs_1_, f32[3,128,256]{2,1,0:T(8,128)S(1)} %shard_map.149.refs_2_, f32[3,128,256]{2,1,0:T(8,128)S(1)} %collective-permute-done.53.refs_3_, ...), custom_call_target="tpu_custom_call" | custom-call | tf_op jit(solution)/shard_map/pallas_call | solution.py:59
  (139 shorter events, 51.5 us)
Async XLA Ops:
  1.6 12.1 %collective-permute-start.3 = (f32[2,128,128]{2,1,0:T(8,128)S(1)}, f32[2,128,128]{2,1,0:T(8,128)S(1)}, u32[]{:S(2)}, u32[]{:S(2)}) collective-permute-start(f32[2,128,128]{2,1,0:T(8,128)S(1)} %pad_maximum_fusion.s), channel_id=1, source_target_pairs={{0,28},{4,8},{8,4},{12,16},{16,12},{20,24},{24,20},{28,0},{1,29},{... | collective-permute-start | bytes 393224 | tf_op jit(solution)/shard_map/ppermute | solution.py:45
  7.7 6.3 %collective-permute-start.2 = (f32[2,128,128]{2,1,0:T(8,128)S(1)}, f32[2,128,128]{2,1,0:T(8,128)S(1)}, u32[]{:S(2)}, u32[]{:S(2)}) collective-permute-start(f32[2,128,128]{2,1,0:T(8,128)S(1)} %pad_maximum_fusion.s), channel_id=1, source_target_pairs={{0,4},{4,0},{8,12},{12,8},{16,20},{20,16},{24,28},{28,24},{1,5},{5... | collective-permute-start | bytes 393224 | tf_op jit(solution)/shard_map/ppermute | solution.py:45
  14.2 6.4 %collective-permute-start.4 = (f32[2,256,128]{2,1,0:T(8,128)S(1)}, f32[2,256,128]{2,1,0:T(8,128)S(1)}, u32[]{:S(2)}, u32[]{:S(2)}) collective-permute-start(f32[2,256,128]{2,1,0:T(8,128)S(1)} %get-tuple-element.69), channel_id=1, source_target_pairs={{0,1},{1,0},{2,3},{3,2},{4,5},{5,4},{6,7},{7,6},{8,9},{9,8},{10,11... | collective-permute-start | bytes 786440 | tf_op jit(solution)/shard_map/ppermute | solution.py:45
  14.2 8.1 %collective-permute-start.5 = (f32[2,256,128]{2,1,0:T(8,128)S(1)}, f32[2,256,128]{2,1,0:T(8,128)S(1)}, u32[]{:S(2)}, u32[]{:S(2)}) collective-permute-start(f32[2,256,128]{2,1,0:T(8,128)S(1)} %get-tuple-element.70), channel_id=1, source_target_pairs={{0,3},{1,2},{2,1},{3,0},{4,7},{5,6},{6,5},{7,4},{8,11},{9,10},{10,... | collective-permute-start | bytes 786440 | tf_op jit(solution)/shard_map/ppermute | solution.py:45
  26.1 9.7 %collective-permute-start.6 = (f32[2,256,128]{2,1,0:T(8,128)S(1)}, f32[2,256,128]{2,1,0:T(8,128)S(1)}, u32[]{:S(2)}, u32[]{:S(2)}) collective-permute-start(f32[2,256,128]{2,1,0:T(8,128)S(1)} %get-tuple-element.77), channel_id=1, source_target_pairs={{0,1},{1,0},{2,3},{3,2},{4,5},{5,4},{6,7},{7,6},{8,9},{9,8},{10,11... | collective-permute-start | bytes 786440 | tf_op jit(solution)/shard_map/ppermute | solution.py:45
  26.6 9.2 %collective-permute-start.7 = (f32[2,256,128]{2,1,0:T(8,128)S(1)}, f32[2,256,128]{2,1,0:T(8,128)S(1)}, u32[]{:S(2)}, u32[]{:S(2)}) collective-permute-start(f32[2,256,128]{2,1,0:T(8,128)S(1)} %get-tuple-element.78), channel_id=1, source_target_pairs={{0,3},{1,2},{2,1},{3,0},{4,7},{5,6},{6,5},{7,4},{8,11},{9,10},{10,... | collective-permute-start | bytes 786440 | tf_op jit(solution)/shard_map/ppermute | solution.py:45
  36.1 7.6 %collective-permute-start.8 = (f32[2,128,128]{2,1,0:T(8,128)S(1)}, f32[2,128,128]{2,1,0:T(8,128)S(1)}, u32[]{:S(2)}, u32[]{:S(2)}) collective-permute-start(f32[2,128,128]{2,1,0:T(8,128)S(1)} %get-tuple-element.80), channel_id=1, source_target_pairs={{0,4},{4,0},{8,12},{12,8},{16,20},{20,16},{24,28},{28,24},{1,5},{5... | collective-permute-start | bytes 393224 | tf_op jit(solution)/shard_map/ppermute | solution.py:45
  37.5 7.7 %collective-permute-start.9 = (f32[2,128,128]{2,1,0:T(8,128)S(1)}, f32[2,128,128]{2,1,0:T(8,128)S(1)}, u32[]{:S(2)}, u32[]{:S(2)}) collective-permute-start(f32[2,128,128]{2,1,0:T(8,128)S(1)} %get-tuple-element.81), channel_id=1, source_target_pairs={{0,28},{4,8},{8,4},{12,16},{16,12},{20,24},{24,20},{28,0},{1,29},{... | collective-permute-start | bytes 393224 | tf_op jit(solution)/shard_map/ppermute | solution.py:45
  45.2 7.8 %collective-permute-start.14 = (f32[2,128,128]{2,1,0:T(8,128)S(1)}, f32[2,128,128]{2,1,0:T(8,128)S(1)}, u32[]{:S(2)}, u32[]{:S(2)}) collective-permute-start(f32[2,128,128]{2,1,0:T(8,128)S(1)} %shard_map.117.s), channel_id=1, source_target_pairs={{0,28},{4,8},{8,4},{12,16},{16,12},{20,24},{24,20},{28,0},{1,29},{... | collective-permute-start | bytes 393224 | tf_op jit(solution)/shard_map/ppermute | solution.py:45
  46.9 6.8 %collective-permute-start.13 = (f32[2,128,128]{2,1,0:T(8,128)S(1)}, f32[2,128,128]{2,1,0:T(8,128)S(1)}, u32[]{:S(2)}, u32[]{:S(2)}) collective-permute-start(f32[2,128,128]{2,1,0:T(8,128)S(1)} %shard_map.117.s), channel_id=1, source_target_pairs={{0,4},{4,0},{8,12},{12,8},{16,20},{20,16},{24,28},{28,24},{1,5},{5... | collective-permute-start | bytes 393224 | tf_op jit(solution)/shard_map/ppermute | solution.py:45
  53.9 8.1 %collective-permute-start.16 = (f32[2,256,128]{2,1,0:T(8,128)S(1)}, f32[2,256,128]{2,1,0:T(8,128)S(1)}, u32[]{:S(2)}, u32[]{:S(2)}) collective-permute-start(f32[2,256,128]{2,1,0:T(8,128)S(1)} %get-tuple-element.84), channel_id=1, source_target_pairs={{0,3},{1,2},{2,1},{3,0},{4,7},{5,6},{6,5},{7,4},{8,11},{9,10},{10,... | collective-permute-start | bytes 786440 | tf_op jit(solution)/shard_map/ppermute | solution.py:45
  66.3 8.3 %collective-permute-start.18 = (f32[2,256,128]{2,1,0:T(8,128)S(1)}, f32[2,256,128]{2,1,0:T(8,128)S(1)}, u32[]{:S(2)}, u32[]{:S(2)}) collective-permute-start(f32[2,256,128]{2,1,0:T(8,128)S(1)} %get-tuple-element.87), channel_id=1, source_target_pairs={{0,3},{1,2},{2,1},{3,0},{4,7},{5,6},{6,5},{7,4},{8,11},{9,10},{10,... | collective-permute-start | bytes 786440 | tf_op jit(solution)/shard_map/ppermute | solution.py:45
  74.9 6.2 %collective-permute-start.19 = (f32[2,128,128]{2,1,0:T(8,128)S(1)}, f32[2,128,128]{2,1,0:T(8,128)S(1)}, u32[]{:S(2)}, u32[]{:S(2)}) collective-permute-start(f32[2,128,128]{2,1,0:T(8,128)S(1)} %get-tuple-element.89), channel_id=1, source_target_pairs={{0,4},{4,0},{8,12},{12,8},{16,20},{20,16},{24,28},{28,24},{1,5},{5... | collective-permute-start | bytes 393224 | tf_op jit(solution)/shard_map/ppermute | solution.py:45
  75.0 8.3 %collective-permute-start.20 = (f32[2,128,128]{2,1,0:T(8,128)S(1)}, f32[2,128,128]{2,1,0:T(8,128)S(1)}, u32[]{:S(2)}, u32[]{:S(2)}) collective-permute-start(f32[2,128,128]{2,1,0:T(8,128)S(1)} %get-tuple-element.90), channel_id=1, source_target_pairs={{0,28},{4,8},{8,4},{12,16},{16,12},{20,24},{24,20},{28,0},{1,29},{... | collective-permute-start | bytes 393224 | tf_op jit(solution)/shard_map/ppermute | solution.py:45
  83.3 7.7 %collective-permute-start.22 = (f32[2,128,128]{2,1,0:T(8,128)S(1)}, f32[2,128,128]{2,1,0:T(8,128)S(1)}, u32[]{:S(2)}, u32[]{:S(2)}) collective-permute-start(f32[2,128,128]{2,1,0:T(8,128)S(1)} %shard_map.121.s), channel_id=1, source_target_pairs={{0,28},{4,8},{8,4},{12,16},{16,12},{20,24},{24,20},{28,0},{1,29},{... | collective-permute-start | bytes 393224 | tf_op jit(solution)/shard_map/ppermute | solution.py:45
  86.1 7.4 %collective-permute-start.21 = (f32[2,128,128]{2,1,0:T(8,128)S(1)}, f32[2,128,128]{2,1,0:T(8,128)S(1)}, u32[]{:S(2)}, u32[]{:S(2)}) collective-permute-start(f32[2,128,128]{2,1,0:T(8,128)S(1)} %shard_map.121.s), channel_id=1, source_target_pairs={{0,4},{4,0},{8,12},{12,8},{16,20},{20,16},{24,28},{28,24},{1,5},{5... | collective-permute-start | bytes 393224 | tf_op jit(solution)/shard_map/ppermute | solution.py:45
  93.8 8.1 %collective-permute-start.24 = (f32[2,256,128]{2,1,0:T(8,128)S(1)}, f32[2,256,128]{2,1,0:T(8,128)S(1)}, u32[]{:S(2)}, u32[]{:S(2)}) collective-permute-start(f32[2,256,128]{2,1,0:T(8,128)S(1)} %get-tuple-element.93), channel_id=1, source_target_pairs={{0,3},{1,2},{2,1},{3,0},{4,7},{5,6},{6,5},{7,4},{8,11},{9,10},{10,... | collective-permute-start | bytes 786440 | tf_op jit(solution)/shard_map/ppermute | solution.py:45
  107.3 8.1 %collective-permute-start.28 = (f32[2,256,128]{2,1,0:T(8,128)S(1)}, f32[2,256,128]{2,1,0:T(8,128)S(1)}, u32[]{:S(2)}, u32[]{:S(2)}) collective-permute-start(f32[2,256,128]{2,1,0:T(8,128)S(1)} %get-tuple-element.99), channel_id=1, source_target_pairs={{0,3},{1,2},{2,1},{3,0},{4,7},{5,6},{6,5},{7,4},{8,11},{9,10},{10,... | collective-permute-start | bytes 786440 | tf_op jit(solution)/shard_map/ppermute | solution.py:45
  108.8 7.0 %collective-permute-start.26 = (f32[3,64,256]{2,1,0:T(8,128)S(1)}, f32[3,64,256]{2,1,0:T(8,128)S(1)}, u32[]{:S(2)}, u32[]{:S(2)}) collective-permute-start(f32[3,64,256]{2,1,0:T(8,128)S(1)} %get-tuple-element.97), channel_id=1, source_target_pairs={{0,4},{4,0},{8,12},{12,8},{16,20},{20,16},{24,28},{28,24},{1,5},{5... | collective-permute-start | bytes 589832 | tf_op jit(solution)/shard_map/ppermute | solution.py:322
  108.9 11.2 %collective-permute-start.41 = (f32[3,64,256]{2,1,0:T(8,128)S(1)}, f32[3,64,256]{2,1,0:T(8,128)S(1)}, u32[]{:S(2)}, u32[]{:S(2)}) collective-permute-start(f32[3,64,256]{2,1,0:T(8,128)S(1)} %get-tuple-element.121), channel_id=1, source_target_pairs={{0,2},{1,3},{2,0},{3,1},{4,6},{5,7},{6,4},{7,5},{8,10},{9,11},{10,... | collective-permute-start | bytes 589832 | tf_op jit(solution)/shard_map/ppermute | solution.py:322
  110.2 10.6 %collective-permute-start.30 = (f32[3,64,256]{2,1,0:T(8,128)S(1)}, f32[3,64,256]{2,1,0:T(8,128)S(1)}, u32[]{:S(2)}, u32[]{:S(2)}) collective-permute-start(f32[3,64,256]{2,1,0:T(8,128)S(1)} %get-tuple-element.106), channel_id=1, source_target_pairs={{0,8},{4,12},{8,0},{12,4},{16,24},{20,28},{24,16},{28,20},{1,9},{5... | collective-permute-start | bytes 589832 | tf_op jit(solution)/shard_map/ppermute | solution.py:322
  116.0 12.0 %collective-permute-start.32 = (f32[2,128,128]{2,1,0:T(8,128)S(1)}, f32[2,128,128]{2,1,0:T(8,128)S(1)}, u32[]{:S(2)}, u32[]{:S(2)}) collective-permute-start(f32[2,128,128]{2,1,0:T(8,128)S(1)} %get-tuple-element.108), channel_id=1, source_target_pairs={{0,4},{4,0},{8,12},{12,8},{16,20},{20,16},{24,28},{28,24},{1,5},{5... | collective-permute-start | bytes 393224 | tf_op jit(solution)/shard_map/ppermute | solution.py:45
  116.3 11.7 %collective-permute-start.33 = (f32[2,128,128]{2,1,0:T(8,128)S(1)}, f32[2,128,128]{2,1,0:T(8,128)S(1)}, u32[]{:S(2)}, u32[]{:S(2)}) collective-permute-start(f32[2,128,128]{2,1,0:T(8,128)S(1)} %get-tuple-element.109), channel_id=1, source_target_pairs={{0,28},{4,8},{8,4},{12,16},{16,12},{20,24},{24,20},{28,0},{1,29},{... | collective-permute-start | bytes 393224 | tf_op jit(solution)/shard_map/ppermute | solution.py:45
  120.2 5.7 %collective-permute-start.42 = (f32[3,32,256]{2,1,0:T(8,128)S(1)}, f32[3,32,256]{2,1,0:T(8,128)S(1)}, u32[]{:S(2)}, u32[]{:S(2)}) collective-permute-start(f32[3,32,256]{2,1,0:T(8,128)S(1)} %get-tuple-element.123), channel_id=1, source_target_pairs={{0,8},{4,12},{8,0},{12,4},{16,24},{20,28},{24,16},{28,20},{1,9},{5... | collective-permute-start | bytes 294920 | tf_op jit(solution)/shard_map/ppermute | solution.py:322
  120.8 7.2 %collective-permute-start.31 = (f32[3,32,256]{2,1,0:T(8,128)S(1)}, f32[3,32,256]{2,1,0:T(8,128)S(1)}, u32[]{:S(2)}, u32[]{:S(2)}) collective-permute-start(f32[3,32,256]{2,1,0:T(8,128)S(1)} %get-tuple-element.107), channel_id=1, source_target_pairs={{0,4},{4,0},{8,12},{12,8},{16,20},{20,16},{24,28},{28,24},{1,5},{5... | collective-permute-start | bytes 294920 | tf_op jit(solution)/shard_map/ppermute | solution.py:322
  123.3 5.6 %collective-permute-start.35 = (f32[3,16,256]{2,1,0:T(8,128)S(1)}, f32[3,16,256]{2,1,0:T(8,128)S(1)}, u32[]{:S(2)}, u32[]{:S(2)}) collective-permute-start(f32[3,16,256]{2,1,0:T(8,128)S(1)} %get-tuple-element.117), channel_id=1, source_target_pairs={{0,8},{4,12},{8,0},{12,4},{16,24},{20,28},{24,16},{28,20},{1,9},{5... | collective-permute-start | bytes 147464 | tf_op jit(solution)/shard_map/ppermute | solution.py:322
  128.9 6.6 %collective-permute-start.36 = (f32[3,16,256]{2,1,0:T(8,128)S(1)}, f32[3,16,256]{2,1,0:T(8,128)S(1)}, u32[]{:S(2)}, u32[]{:S(2)}) collective-permute-start(f32[3,16,256]{2,1,0:T(8,128)S(1)} %shard_map.131.cur), channel_id=1, source_target_pairs={{0,16},{4,20},{8,24},{12,28},{16,0},{20,4},{24,8},{28,12},{1,17},{... | collective-permute-start | bytes 147464 | tf_op jit(solution)/shard_map/ppermute | solution.py:322
  130.1 6.5 %collective-permute-start.44 = (f32[3,16,256]{2,1,0:T(8,128)S(1)}, f32[3,16,256]{2,1,0:T(8,128)S(1)}, u32[]{:S(2)}, u32[]{:S(2)}) collective-permute-start(f32[3,16,256]{2,1,0:T(8,128)S(1)} %shard_map.139.cur), channel_id=1, source_target_pairs={{0,16},{4,20},{8,24},{12,28},{16,0},{20,4},{24,8},{28,12},{1,17},{... | collective-permute-start | bytes 147464 | tf_op jit(solution)/shard_map/ppermute | solution.py:322
  132.2 6.3 %collective-permute-start.49 = (f32[3,16,256]{2,1,0:T(8,128)S(1)}, f32[3,16,256]{2,1,0:T(8,128)S(1)}, u32[]{:S(2)}, u32[]{:S(2)}) collective-permute-start(f32[3,16,256]{2,1,0:T(8,128)S(1)} %shard_map.145.cur), channel_id=1, source_target_pairs={{0,16},{4,20},{8,24},{12,28},{16,0},{20,4},{24,8},{28,12},{1,17},{... | collective-permute-start | bytes 147464 | tf_op jit(solution)/shard_map/ppermute | solution.py:322
  144.4 5.7 %collective-permute-start.39 = (f32[3,64,256]{2,1,0:T(8,128)S(1)}, f32[3,64,256]{2,1,0:T(8,128)S(1)}, u32[]{:S(2)}, u32[]{:S(2)}) collective-permute-start(f32[3,64,256]{2,1,0:T(8,128)S(1)} %shard_map.134.cur), channel_id=1, source_target_pairs={{0,4},{4,0},{8,12},{12,8},{16,20},{20,16},{24,28},{28,24},{1,5},{5... | collective-permute-start | bytes 589832 | tf_op jit(solution)/shard_map/ppermute | solution.py:322
  146.0 5.7 %collective-permute-start.47 = (f32[3,64,256]{2,1,0:T(8,128)S(1)}, f32[3,64,256]{2,1,0:T(8,128)S(1)}, u32[]{:S(2)}, u32[]{:S(2)}) collective-permute-start(f32[3,64,256]{2,1,0:T(8,128)S(1)} %shard_map.142.cur), channel_id=1, source_target_pairs={{0,2},{1,3},{2,0},{3,1},{4,6},{5,7},{6,4},{7,5},{8,10},{9,11},{10,... | collective-permute-start | bytes 589832 | tf_op jit(solution)/shard_map/ppermute | solution.py:322
  147.4 5.7 %collective-permute-start.52 = (f32[3,64,256]{2,1,0:T(8,128)S(1)}, f32[3,64,256]{2,1,0:T(8,128)S(1)}, u32[]{:S(2)}, u32[]{:S(2)}) collective-permute-start(f32[3,64,256]{2,1,0:T(8,128)S(1)} %shard_map.148.cur), channel_id=1, source_target_pairs={{0,8},{4,12},{8,0},{12,4},{16,24},{20,28},{24,16},{28,20},{1,9},{5... | collective-permute-start | bytes 589832 | tf_op jit(solution)/shard_map/ppermute | solution.py:322
  (30 other events, 101.0 us)

commit v4 on v3

--- a/solution.py
+++ b/solution.py
@@ -32,17 +32,23 @@
     return right, left
 
 
-def near_pairs(count):
-    return [(i, i ^ 1) for i in range(count)]
-
-
-def far_pairs(count):
-    return [(i, (i + 1 if i % 2 else i - 1) % count) for i in range(count)]
+def swap_pairs(n_row, n_col, axis, far):
+    pairs = []
+    for i in range(n_row):
+        for j in range(n_col):
+            k, count = (i, n_row) if axis == "row" else (j, n_col)
+            other = k ^ 1 if not far else (k + 1 if k % 2 else k - 1)
+            if axis == "row":
+                to = (other, j) if 0 <= other < count else (i, j ^ 1)
+            else:
+                to = (i, other) if 0 <= other < count else (i ^ 1, j)
+            pairs.append((i * n_col + j, to[0] * n_col + to[1]))
+    return pairs
 
 
 def swap(array, axis, far):
-    pairs = (far_pairs if far else near_pairs)(lax.axis_size(axis))
-    return lax.ppermute(array, axis, pairs)
+    pairs = swap_pairs(lax.axis_size("row"), lax.axis_size("col"), axis, far)
+    return lax.ppermute(array, ("row", "col"), pairs)
 
 
 def swap_both(to_near, to_far, axis):
@@ -181,9 +187,9 @@
 
 def view_body(sizes, last, sc, mid, near, far, pr, pi, view, right_t, left_t, *refs):
     if last:
-        gm, to_near, to_far, *parts, spec_scr, win_scr, term_scr = refs
+        gm, to_near, to_far, *parts, spec_scr, win_scr, wave_scr, mix_scr, term_scr = refs
     else:
-        gm, to_near, to_far, spec_scr, win_scr = refs
+        gm, to_near, to_far, spec_scr, win_scr, wave_scr, mix_scr = refs
     _, _, _, _, rim = sizes
     at = Place(sc, sizes)
     modes, width = pr.shape[0], pr.shape[1]
@@ -203,24 +209,28 @@
         win_scr[part, :, rim:] = jnp.where(
             first, own, jnp.where(middle, jnp.where(lane < half, ro, rr), rgt)
         )
+    for m in range(modes):
+        wr, wi = win_scr[0], win_scr[1]
+        rows_of = slice(m * width, (m + 1) * width)
+        wave_scr[rows_of, :width] = (pr[m] * wr - pi[m] * wi).astype(BF16)
+        wave_scr[rows_of, width:] = (pr[m] * wi + pi[m] * wr).astype(BF16)
+    mix_scr[...] = jnp.dot(wave_scr[...], right_t[...], preferred_element_type=F32).astype(BF16)
     total = jnp.zeros((width, width), F32)
     for m in range(modes):
-        wr, wi = win_scr[0], win_scr[1]
-        psi = jnp.concatenate(
-            [pr[m] * wr - pi[m] * wi, pr[m] * wi + pi[m] * wr], axis=1
-        ).astype(BF16)
-        mixed = jnp.dot(psi, right_t[...], preferred_element_type=F32).astype(BF16)
+        mixed = mix_scr[m * width : (m + 1) * width]
         tall = jnp.concatenate([mixed[:, :width], mixed[:, width:]], axis=0)
         spec = jnp.dot(left_t[...], tall, preferred_element_type=F32)
         spec_scr[m] = spec
         total = total + (spec[:width] * spec[:width] + spec[width:] * spec[width:])
     factor = view[...] / jnp.maximum(jnp.sqrt(total), amp_floor) - 1.0
+    for m in range(modes):
+        rows_of = slice(m * width, (m + 1) * width)
+        wave_scr[rows_of, :width] = (spec_scr[m, :width] * factor).astype(BF16)
+        wave_scr[rows_of, width:] = (spec_scr[m, width:] * factor).astype(BF16)
+    mix_scr[...] = jnp.dot(wave_scr[...], left_t[...], preferred_element_type=F32).astype(BF16)
     grad = [jnp.zeros((width, width), F32), jnp.zeros((width, width), F32)]
     for m in range(modes):
-        change = jnp.concatenate(
-            [spec_scr[m, :width] * factor, spec_scr[m, width:] * factor], axis=1
-        ).astype(BF16)
-        mixed = jnp.dot(change, left_t[...], preferred_element_type=F32).astype(BF16)
+        mixed = mix_scr[m * width : (m + 1) * width]
         tall = jnp.concatenate([mixed[:, :width], mixed[:, width:]], axis=0)
         back = jnp.dot(right_t[...], tall, preferred_element_type=F32)
         er, ei = back[:width], back[width:]
@@ -414,6 +424,7 @@
     fold = call(functools.partial(fold_body, sizes), [tile] * 3, [tall])
     step = call(functools.partial(step_body, sizes), [tile])
     scratch = [pltpu.VMEM((modes, 2 * width, width), F32), pltpu.VMEM((2, width, width), F32)]
+    scratch += [pltpu.VMEM((modes * width, 2 * width), BF16)] * 2
     terms = ((2 * modes + 1) // COLORS, rim, width)
 
     for turn in range(ITERS):

time: 157 us -> 146 us (0.930)
  waiting for transfers between devices: 75.1 us -> 55.4 us
  starting transfers between devices: 53.1 us -> 62.7 us
    ppermute x24, waiting for transfers between devices: 48.7 us -> 30.1 us  [swap(): return lax.ppermute(array, ('row', 'col'), pairs)]
    ppermute x32, starting transfers between devices: 25 us -> 31.2 us  [swap_bit(): lax.ppermute(array, name, [(i, i ^ 1 << level) for i in range(count)])]
    ppermute x24, starting transfers between devices: 28.2 us -> 31.5 us  [swap(): return lax.ppermute(array, ('row', 'col'), pairs)]
  transfers between devices with their start and end apart: 56 -> 56, of which waited for: 36 -> 26; matrix products, arithmetic and copies ran while one was open for 0% -> 0% of each run, Pallas kernels for 4% -> 4%
where the time goes in v4:
time: 146 us; the launch traced here: 145 us
  starting transfers between devices  62.7 us (43%)
  waiting for transfers between devices  55.4 us (38%)
  Pallas kernels  19.6 us (13%)
  local copies, waits for them, and re-layouts  5.76 us (4%)
    ppermute x24, starting transfers between devices, swap(): return lax.ppermute(array, ('row', 'col'), pairs)  31.5 us
    ppermute x32, starting transfers between devices, swap_bit(): lax.ppermute(array, name, [(i, i ^ 1 << level) for i in range(count)])  31.2 us
    ppermute x24, waiting for transfers between devices, swap(): return lax.ppermute(array, ('row', 'col'), pairs)  30.1 us
    ppermute x32, waiting for transfers between devices, swap_bit(): lax.ppermute(array, name, [(i, i ^ 1 << level) for i in range(count)])  25.4 us
    pallas_call x39, Pallas kernels, run(): pl.pallas_call(body, out_shape=[jax.ShapeDtypeStruct(s, F32) for s in out...  19.4 us
    unnamed x12, local copies, waits for them, and re-layouts  5.1 us
  transfers between devices with their start and end apart: 56, of which 26 were waited for; matrix products, arithmetic and copies ran while one was open for 0% of the time, Pallas kernels for 4%

profile of v4, /device:TPU:0, one launch (start us, length us, event | category | flops | bytes accessed | tf_op | source)
XLA Modules:
  0.0 145.5 jit_solution(13312350586353897921)
XLA Ops:
  2.1 4.0 %collective-permute-start.2 = (f32[2,128,128]{2,1,0:T(8,128)S(1)}, f32[2,128,128]{2,1,0:T(8,128)S(1)}, u32[]{:S(2)}, u32[]{:S(2)}) collective-permute-start(f32[2,128,128]{2,1,0:T(8,128)S(1)} %pad_maximum_fusion.s), channel_id=1, source_target_pairs={{0,4},{1,5},{2,6},{3,7},{4,0},{5,1},{6,2},{7,3},{8,12},{9,13},{10,... | collective-permute-start | bytes 393224 | tf_op jit(solution)/shard_map/ppermute | solution.py:51
  10.1 2.0 %collective-permute-done.1 = f32[1,128]{1,0:T(1,128)S(1)} collective-permute-done((f32[1,128]{1,0:T(1,128)S(1)}, f32[1,128]{1,0:T(1,128)S(1)}, u32[]{:S(2)}, u32[]{:S(2)}) %collective-permute-start.1) | collective-permute-done | bytes 544 | tf_op jit(solution)/shard_map/ppermute | solution.py:332
  18.9 3.4 %shard_map.114 = (f32[2,256,128]{2,1,0:T(8,128)S(1)}, f32[2,256,128]{2,1,0:T(8,128)S(1)}, f32[2,256,128]{2,1,0:T(8,128)S(1)}) custom-call(f32[1,128]{1,0:T(1,128)S(1)} %add.16.sc, f32[2,256,128]{2,1,0:T(8,128)S(1)} %get-tuple-element.68.mid, f32[2,256,128]{2,1,0:T(8,128)S(1)} %collective-permute-done.4.near, f32[2,256,128]{2,1,0:T(8,128)S(1)} %collective-permute-done.5.far, ...), custom_call_target="tpu_custom_call" | custom-call | tf_op jit(solution)/shard_map/pallas_call | solution.py:65
  24.5 4.4 %collective-permute-done.10 = f32[1,128]{1,0:T(1,128)S(1)} collective-permute-done((f32[1,128]{1,0:T(1,128)S(1)}, f32[1,128]{1,0:T(1,128)S(1)}, u32[]{:S(2)}, u32[]{:S(2)}) %collective-permute-start.10) | collective-permute-done | bytes 544 | tf_op jit(solution)/shard_map/ppermute | solution.py:332
  30.5 2.0 %collective-permute-done.11 = f32[1,128]{1,0:T(1,128)S(1)} collective-permute-done((f32[1,128]{1,0:T(1,128)S(1)}, f32[1,128]{1,0:T(1,128)S(1)}, u32[]{:S(2)}, u32[]{:S(2)}) %collective-permute-start.11) | collective-permute-done | bytes 544 | tf_op jit(solution)/shard_map/ppermute | solution.py:332
  32.5 2.6 %collective-permute-start.12 = (f32[1,128]{1,0:T(1,128)S(1)}, f32[1,128]{1,0:T(1,128)S(1)}, u32[]{:S(2)}, u32[]{:S(2)}) collective-permute-start(f32[1,128]{1,0:T(1,128)S(1)} %add.18), channel_id=1, source_target_pairs={{0,16},{4,20},{8,24},{12,28},{16,0},{20,4},{24,8},{28,12},{1,17},{... | collective-permute-start | bytes 1544 | tf_op jit(solution)/shard_map/ppermute | solution.py:332
  37.0 4.2 %shard_map.116.denom = f32[128,128]{1,0:T(8,128)S(1)} custom-call(s32[128]{0:T(128)S(1)} %convert_bitcast_fusion.sc, f32[4,256,256]{2,1,0:T(8,128)S(1)} %get-tuple-element.71.pr.refs_6_, f32[4,256,256]{2,1,0:T(8,128)S(1)} %get-tuple-element.72.pi.refs_7_), custom_call_target="tpu_custom_call" | custom-call | flops 16777216 | bytes 10000000 | tf_op jit(solution)/shard_map/pallas_call | solution.py:65
  41.7 4.0 %collective-permute-start.13 = (f32[2,128,128]{2,1,0:T(8,128)S(1)}, f32[2,128,128]{2,1,0:T(8,128)S(1)}, u32[]{:S(2)}, u32[]{:S(2)}) collective-permute-start(f32[2,128,128]{2,1,0:T(8,128)S(1)} %shard_map.117.s), channel_id=1, source_target_pairs={{0,4},{1,5},{2,6},{3,7},{4,0},{5,1},{6,2},{7,3},{8,12},{9,13},{10,... | collective-permute-start | bytes 393224 | tf_op jit(solution)/shard_map/ppermute | solution.py:51
  45.7 3.3 %collective-permute-done.13.near = f32[2,128,128]{2,1,0:T(8,128)S(1)} collective-permute-done((f32[2,128,128]{2,1,0:T(8,128)S(1)}, f32[2,128,128]{2,1,0:T(8,128)S(1)}, u32[]{:S(2)}, u32[]{:S(2)}) %collective-permute-start.13) | collective-permute-done | bytes 131104 | tf_op jit(solution)/shard_map/ppermute | solution.py:51
  49.2 2.5 %collective-permute-start.16 = (f32[2,256,128]{2,1,0:T(8,128)S(1)}, f32[2,256,128]{2,1,0:T(8,128)S(1)}, u32[]{:S(2)}, u32[]{:S(2)}) collective-permute-start(f32[2,256,128]{2,1,0:T(8,128)S(1)} %get-tuple-element.84), channel_id=1, source_target_pairs={{0,4},{1,2},{2,1},{3,7},{4,0},{5,6},{6,5},{7,3},{8,12},{9,10},{10,... | collective-permute-start | bytes 786440 | tf_op jit(solution)/shard_map/ppermute | solution.py:51
  51.8 4.3 %collective-permute-done.16.far = f32[2,256,128]{2,1,0:T(8,128)S(1)} collective-permute-done((f32[2,256,128]{2,1,0:T(8,128)S(1)}, f32[2,256,128]{2,1,0:T(8,128)S(1)}, u32[]{:S(2)}, u32[]{:S(2)}) %collective-permute-start.16) | collective-permute-done | bytes 262176 | tf_op jit(solution)/shard_map/ppermute | solution.py:51
  56.1 3.4 %shard_map.119 = (f32[2,256,128]{2,1,0:T(8,128)S(1)}, f32[2,256,128]{2,1,0:T(8,128)S(1)}, f32[2,256,128]{2,1,0:T(8,128)S(1)}) custom-call(f32[1,128]{1,0:T(1,128)S(1)} %add.16.sc, f32[2,256,128]{2,1,0:T(8,128)S(1)} %get-tuple-element.82.mid, f32[2,256,128]{2,1,0:T(8,128)S(1)} %collective-permute-done.15.near, ...), custom_call_target="tpu_custom_call" | custom-call | tf_op jit(solution)/shard_map/pallas_call | solution.py:65
  59.6 2.1 %collective-permute-start.18 = (f32[2,256,128]{2,1,0:T(8,128)S(1)}, f32[2,256,128]{2,1,0:T(8,128)S(1)}, u32[]{:S(2)}, u32[]{:S(2)}) collective-permute-start(f32[2,256,128]{2,1,0:T(8,128)S(1)} %get-tuple-element.87), channel_id=1, source_target_pairs={{0,4},{1,2},{2,1},{3,7},{4,0},{5,6},{6,5},{7,3},{8,12},{9,10},{10,... | collective-permute-start | bytes 786440 | tf_op jit(solution)/shard_map/ppermute | solution.py:51
  61.7 4.3 %collective-permute-done.18.far = f32[2,256,128]{2,1,0:T(8,128)S(1)} collective-permute-done((f32[2,256,128]{2,1,0:T(8,128)S(1)}, f32[2,256,128]{2,1,0:T(8,128)S(1)}, u32[]{:S(2)}, u32[]{:S(2)}) %collective-permute-start.18) | collective-permute-done | bytes 262176 | tf_op jit(solution)/shard_map/ppermute | solution.py:51
  66.3 2.1 %collective-permute-start.19 = (f32[2,128,128]{2,1,0:T(8,128)S(1)}, f32[2,128,128]{2,1,0:T(8,128)S(1)}, u32[]{:S(2)}, u32[]{:S(2)}) collective-permute-start(f32[2,128,128]{2,1,0:T(8,128)S(1)} %get-tuple-element.89), channel_id=1, source_target_pairs={{0,4},{1,5},{2,6},{3,7},{4,0},{5,1},{6,2},{7,3},{8,12},{9,13},{10,... | collective-permute-start | bytes 393224 | tf_op jit(solution)/shard_map/ppermute | solution.py:51
  68.4 5.8 %collective-permute-done.19.near = f32[2,128,128]{2,1,0:T(8,128)S(1)} collective-permute-done((f32[2,128,128]{2,1,0:T(8,128)S(1)}, f32[2,128,128]{2,1,0:T(8,128)S(1)}, u32[]{:S(2)}, u32[]{:S(2)}) %collective-permute-start.19) | collective-permute-done | bytes 131104 | tf_op jit(solution)/shard_map/ppermute | solution.py:51
  74.4 4.0 %collective-permute-start.21 = (f32[2,128,128]{2,1,0:T(8,128)S(1)}, f32[2,128,128]{2,1,0:T(8,128)S(1)}, u32[]{:S(2)}, u32[]{:S(2)}) collective-permute-start(f32[2,128,128]{2,1,0:T(8,128)S(1)} %shard_map.121.s), channel_id=1, source_target_pairs={{0,4},{1,5},{2,6},{3,7},{4,0},{5,1},{6,2},{7,3},{8,12},{9,13},{10,... | collective-permute-start | bytes 393224 | tf_op jit(solution)/shard_map/ppermute | solution.py:51
  78.4 4.4 %collective-permute-done.21.near = f32[2,128,128]{2,1,0:T(8,128)S(1)} collective-permute-done((f32[2,128,128]{2,1,0:T(8,128)S(1)}, f32[2,128,128]{2,1,0:T(8,128)S(1)}, u32[]{:S(2)}, u32[]{:S(2)}) %collective-permute-start.21) | collective-permute-done | bytes 131104 | tf_op jit(solution)/shard_map/ppermute | solution.py:51
  83.0 2.5 %collective-permute-start.24 = (f32[2,256,128]{2,1,0:T(8,128)S(1)}, f32[2,256,128]{2,1,0:T(8,128)S(1)}, u32[]{:S(2)}, u32[]{:S(2)}) collective-permute-start(f32[2,256,128]{2,1,0:T(8,128)S(1)} %get-tuple-element.93), channel_id=1, source_target_pairs={{0,4},{1,2},{2,1},{3,7},{4,0},{5,6},{6,5},{7,3},{8,12},{9,10},{10,... | collective-permute-start | bytes 786440 | tf_op jit(solution)/shard_map/ppermute | solution.py:51
  85.6 4.3 %collective-permute-done.24.far = f32[2,256,128]{2,1,0:T(8,128)S(1)} collective-permute-done((f32[2,256,128]{2,1,0:T(8,128)S(1)}, f32[2,256,128]{2,1,0:T(8,128)S(1)}, u32[]{:S(2)}, u32[]{:S(2)}) %collective-permute-start.24) | collective-permute-done | bytes 262176 | tf_op jit(solution)/shard_map/ppermute | solution.py:51
  89.9 4.0 %shard_map.123 = (f32[2,256,128]{2,1,0:T(8,128)S(1)}, f32[2,256,128]{2,1,0:T(8,128)S(1)}, f32[2,256,128]{2,1,0:T(8,128)S(1)}, f32[3,128,256]{2,1,0:T(8,128)S(1)}...) custom-call(f32[1,128]{1,0:T(1,128)S(1)} %add.16.sc, ...), custom_call_target="tpu_custom_call" | custom-call | tf_op jit(solution)/shard_map/pallas_call | solution.py:65
  95.0 2.0 %collective-permute-start.28 = (f32[2,256,128]{2,1,0:T(8,128)S(1)}, f32[2,256,128]{2,1,0:T(8,128)S(1)}, u32[]{:S(2)}, u32[]{:S(2)}) collective-permute-start(f32[2,256,128]{2,1,0:T(8,128)S(1)} %get-tuple-element.99), channel_id=1, source_target_pairs={{0,4},{1,2},{2,1},{3,7},{4,0},{5,6},{6,5},{7,3},{8,12},{9,10},{10,... | collective-permute-start | bytes 786440 | tf_op jit(solution)/shard_map/ppermute | solution.py:51
  100.3 3.2 %collective-permute-done.28.far = f32[2,256,128]{2,1,0:T(8,128)S(1)} collective-permute-done((f32[2,256,128]{2,1,0:T(8,128)S(1)}, f32[2,256,128]{2,1,0:T(8,128)S(1)}, u32[]{:S(2)}, u32[]{:S(2)}) %collective-permute-start.28) | collective-permute-done | bytes 262176 | tf_op jit(solution)/shard_map/ppermute | solution.py:51
  103.5 2.1 %collective-permute-done.26.got = f32[3,64,256]{2,1,0:T(8,128)S(1)} collective-permute-done((f32[3,64,256]{2,1,0:T(8,128)S(1)}, f32[3,64,256]{2,1,0:T(8,128)S(1)}, u32[]{:S(2)}, u32[]{:S(2)}) %collective-permute-start.26) | collective-permute-done | bytes 196640 | tf_op jit(solution)/shard_map/ppermute | solution.py:332
  105.8 2.1 %collective-permute-start.32 = (f32[2,128,128]{2,1,0:T(8,128)S(1)}, f32[2,128,128]{2,1,0:T(8,128)S(1)}, u32[]{:S(2)}, u32[]{:S(2)}) collective-permute-start(f32[2,128,128]{2,1,0:T(8,128)S(1)} %get-tuple-element.108), channel_id=1, source_target_pairs={{0,4},{1,5},{2,6},{3,7},{4,0},{5,1},{6,2},{7,3},{8,12},{9,13},{10,... | collective-permute-start | bytes 393224 | tf_op jit(solution)/shard_map/ppermute | solution.py:51
  110.9 2.3 %collective-permute-done.34.got = f32[3,32,256]{2,1,0:T(8,128)S(1)} collective-permute-done((f32[3,32,256]{2,1,0:T(8,128)S(1)}, f32[3,32,256]{2,1,0:T(8,128)S(1)}, u32[]{:S(2)}, u32[]{:S(2)}) %collective-permute-start.34) | collective-permute-done | bytes 98336 | tf_op jit(solution)/shard_map/ppermute | solution.py:332
  115.5 2.1 %collective-permute-start.48 = (f32[3,16,256]{2,1,0:T(8,128)S(1)}, f32[3,16,256]{2,1,0:T(8,128)S(1)}, u32[]{:S(2)}, u32[]{:S(2)}) collective-permute-start(f32[3,16,256]{2,1,0:T(8,128)S(1)} %get-tuple-element.129), channel_id=1, source_target_pairs={{0,2},{1,3},{2,0},{3,1},{4,6},{5,7},{6,4},{7,5},{8,10},{9,11},{10,... | collective-permute-start | bytes 147464 | tf_op jit(solution)/shard_map/ppermute | solution.py:332
  117.5 2.2 %collective-permute-start.36 = (f32[3,16,256]{2,1,0:T(8,128)S(1)}, f32[3,16,256]{2,1,0:T(8,128)S(1)}, u32[]{:S(2)}, u32[]{:S(2)}) collective-permute-start(f32[3,16,256]{2,1,0:T(8,128)S(1)} %shard_map.131.cur), channel_id=1, source_target_pairs={{0,16},{4,20},{8,24},{12,28},{16,0},{20,4},{24,8},{28,12},{1,17},{... | collective-permute-start | bytes 147464 | tf_op jit(solution)/shard_map/ppermute | solution.py:332
  121.0 1.9 %collective-permute-start.49 = (f32[3,16,256]{2,1,0:T(8,128)S(1)}, f32[3,16,256]{2,1,0:T(8,128)S(1)}, u32[]{:S(2)}, u32[]{:S(2)}) collective-permute-start(f32[3,16,256]{2,1,0:T(8,128)S(1)} %shard_map.145.cur), channel_id=1, source_target_pairs={{0,16},{4,20},{8,24},{12,28},{16,0},{20,4},{24,8},{28,12},{1,17},{... | collective-permute-start | bytes 147464 | tf_op jit(solution)/shard_map/ppermute | solution.py:332
  129.2 2.1 %collective-permute-start.46 = (f32[3,32,256]{2,1,0:T(8,128)S(1)}, f32[3,32,256]{2,1,0:T(8,128)S(1)}, u32[]{:S(2)}, u32[]{:S(2)}) collective-permute-start(f32[3,32,256]{2,1,0:T(8,128)S(1)} %shard_map.141.cur), channel_id=1, source_target_pairs={{0,8},{4,12},{8,0},{12,4},{16,24},{20,28},{24,16},{28,20},{1,9},{5... | collective-permute-start | bytes 294920 | tf_op jit(solution)/shard_map/ppermute | solution.py:332
  137.2 2.5 %collective-permute-done.39.got = f32[3,64,256]{2,1,0:T(8,128)S(1)} collective-permute-done((f32[3,64,256]{2,1,0:T(8,128)S(1)}, f32[3,64,256]{2,1,0:T(8,128)S(1)}, u32[]{:S(2)}, u32[]{:S(2)}) %collective-permute-start.39) | collective-permute-done | bytes 196640 | tf_op jit(solution)/shard_map/ppermute | solution.py:332
  143.6 1.9 %shard_map.150 = (f32[4,256,256]{2,1,0:T(8,128)}, f32[4,256,256]{2,1,0:T(8,128)}) custom-call(f32[3,128,256]{2,1,0:T(8,128)S(1)} %shard_map.135.refs_0_, f32[3,128,256]{2,1,0:T(8,128)S(1)} %shard_map.143.refs_1_, f32[3,128,256]{2,1,0:T(8,128)S(1)} %shard_map.149.refs_2_, f32[3,128,256]{2,1,0:T(8,128)S(1)} %collective-permute-done.53.refs_3_, ...), custom_call_target="tpu_custom_call" | custom-call | tf_op jit(solution)/shard_map/pallas_call | solution.py:65
  (139 shorter events, 46.2 us)
Async XLA Ops:
  1.6 10.6 %collective-permute-start.3 = (f32[2,128,128]{2,1,0:T(8,128)S(1)}, f32[2,128,128]{2,1,0:T(8,128)S(1)}, u32[]{:S(2)}, u32[]{:S(2)}) collective-permute-start(f32[2,128,128]{2,1,0:T(8,128)S(1)} %pad_maximum_fusion.s), channel_id=1, source_target_pairs={{0,1},{1,0},{2,3},{3,2},{4,8},{5,9},{6,10},{7,11},{8,4},{9,5},{10,... | collective-permute-start | bytes 393224 | tf_op jit(solution)/shard_map/ppermute | solution.py:51
  2.1 10.1 %collective-permute-start.2 = (f32[2,128,128]{2,1,0:T(8,128)S(1)}, f32[2,128,128]{2,1,0:T(8,128)S(1)}, u32[]{:S(2)}, u32[]{:S(2)}) collective-permute-start(f32[2,128,128]{2,1,0:T(8,128)S(1)} %pad_maximum_fusion.s), channel_id=1, source_target_pairs={{0,4},{1,5},{2,6},{3,7},{4,0},{5,1},{6,2},{7,3},{8,12},{9,13},{10,... | collective-permute-start | bytes 393224 | tf_op jit(solution)/shard_map/ppermute | solution.py:51
  12.4 6.2 %collective-permute-start.4 = (f32[2,256,128]{2,1,0:T(8,128)S(1)}, f32[2,256,128]{2,1,0:T(8,128)S(1)}, u32[]{:S(2)}, u32[]{:S(2)}) collective-permute-start(f32[2,256,128]{2,1,0:T(8,128)S(1)} %get-tuple-element.69), channel_id=1, source_target_pairs={{0,1},{1,0},{2,3},{3,2},{4,5},{5,4},{6,7},{7,6},{8,9},{9,8},{10,11... | collective-permute-start | bytes 786440 | tf_op jit(solution)/shard_map/ppermute | solution.py:51
  12.5 6.4 %collective-permute-start.5 = (f32[2,256,128]{2,1,0:T(8,128)S(1)}, f32[2,256,128]{2,1,0:T(8,128)S(1)}, u32[]{:S(2)}, u32[]{:S(2)}) collective-permute-start(f32[2,256,128]{2,1,0:T(8,128)S(1)} %get-tuple-element.70), channel_id=1, source_target_pairs={{0,4},{1,2},{2,1},{3,7},{4,0},{5,6},{6,5},{7,3},{8,12},{9,10},{10,... | collective-permute-start | bytes 786440 | tf_op jit(solution)/shard_map/ppermute | solution.py:51
  22.3 12.8 %collective-permute-start.6 = (f32[2,256,128]{2,1,0:T(8,128)S(1)}, f32[2,256,128]{2,1,0:T(8,128)S(1)}, u32[]{:S(2)}, u32[]{:S(2)}) collective-permute-start(f32[2,256,128]{2,1,0:T(8,128)S(1)} %get-tuple-element.77), channel_id=1, source_target_pairs={{0,1},{1,0},{2,3},{3,2},{4,5},{5,4},{6,7},{7,6},{8,9},{9,8},{10,11... | collective-permute-start | bytes 786440 | tf_op jit(solution)/shard_map/ppermute | solution.py:51
  22.5 12.6 %collective-permute-start.7 = (f32[2,256,128]{2,1,0:T(8,128)S(1)}, f32[2,256,128]{2,1,0:T(8,128)S(1)}, u32[]{:S(2)}, u32[]{:S(2)}) collective-permute-start(f32[2,256,128]{2,1,0:T(8,128)S(1)} %get-tuple-element.78), channel_id=1, source_target_pairs={{0,4},{1,2},{2,1},{3,7},{4,0},{5,6},{6,5},{7,3},{8,12},{9,10},{10,... | collective-permute-start | bytes 786440 | tf_op jit(solution)/shard_map/ppermute | solution.py:51
  35.4 5.9 %collective-permute-start.8 = (f32[2,128,128]{2,1,0:T(8,128)S(1)}, f32[2,128,128]{2,1,0:T(8,128)S(1)}, u32[]{:S(2)}, u32[]{:S(2)}) collective-permute-start(f32[2,128,128]{2,1,0:T(8,128)S(1)} %get-tuple-element.80), channel_id=1, source_target_pairs={{0,4},{1,5},{2,6},{3,7},{4,0},{5,1},{6,2},{7,3},{8,12},{9,13},{10,... | collective-permute-start | bytes 393224 | tf_op jit(solution)/shard_map/ppermute | solution.py:51
  41.7 7.3 %collective-permute-start.13 = (f32[2,128,128]{2,1,0:T(8,128)S(1)}, f32[2,128,128]{2,1,0:T(8,128)S(1)}, u32[]{:S(2)}, u32[]{:S(2)}) collective-permute-start(f32[2,128,128]{2,1,0:T(8,128)S(1)} %shard_map.117.s), channel_id=1, source_target_pairs={{0,4},{1,5},{2,6},{3,7},{4,0},{5,1},{6,2},{7,3},{8,12},{9,13},{10,... | collective-permute-start | bytes 393224 | tf_op jit(solution)/shard_map/ppermute | solution.py:51
  49.2 6.9 %collective-permute-start.16 = (f32[2,256,128]{2,1,0:T(8,128)S(1)}, f32[2,256,128]{2,1,0:T(8,128)S(1)}, u32[]{:S(2)}, u32[]{:S(2)}) collective-permute-start(f32[2,256,128]{2,1,0:T(8,128)S(1)} %get-tuple-element.84), channel_id=1, source_target_pairs={{0,4},{1,2},{2,1},{3,7},{4,0},{5,6},{6,5},{7,3},{8,12},{9,10},{10,... | collective-permute-start | bytes 786440 | tf_op jit(solution)/shard_map/ppermute | solution.py:51
  59.6 6.5 %collective-permute-start.18 = (f32[2,256,128]{2,1,0:T(8,128)S(1)}, f32[2,256,128]{2,1,0:T(8,128)S(1)}, u32[]{:S(2)}, u32[]{:S(2)}) collective-permute-start(f32[2,256,128]{2,1,0:T(8,128)S(1)} %get-tuple-element.87), channel_id=1, source_target_pairs={{0,4},{1,2},{2,1},{3,7},{4,0},{5,6},{6,5},{7,3},{8,12},{9,10},{10,... | collective-permute-start | bytes 786440 | tf_op jit(solution)/shard_map/ppermute | solution.py:51
  66.3 7.9 %collective-permute-start.19 = (f32[2,128,128]{2,1,0:T(8,128)S(1)}, f32[2,128,128]{2,1,0:T(8,128)S(1)}, u32[]{:S(2)}, u32[]{:S(2)}) collective-permute-start(f32[2,128,128]{2,1,0:T(8,128)S(1)} %get-tuple-element.89), channel_id=1, source_target_pairs={{0,4},{1,5},{2,6},{3,7},{4,0},{5,1},{6,2},{7,3},{8,12},{9,13},{10,... | collective-permute-start | bytes 393224 | tf_op jit(solution)/shard_map/ppermute | solution.py:51
  68.4 5.9 %collective-permute-start.20 = (f32[2,128,128]{2,1,0:T(8,128)S(1)}, f32[2,128,128]{2,1,0:T(8,128)S(1)}, u32[]{:S(2)}, u32[]{:S(2)}) collective-permute-start(f32[2,128,128]{2,1,0:T(8,128)S(1)} %get-tuple-element.90), channel_id=1, source_target_pairs={{0,1},{1,0},{2,3},{3,2},{4,8},{5,9},{6,10},{7,11},{8,4},{9,5},{10,... | collective-permute-start | bytes 393224 | tf_op jit(solution)/shard_map/ppermute | solution.py:51
  74.4 8.4 %collective-permute-start.21 = (f32[2,128,128]{2,1,0:T(8,128)S(1)}, f32[2,128,128]{2,1,0:T(8,128)S(1)}, u32[]{:S(2)}, u32[]{:S(2)}) collective-permute-start(f32[2,128,128]{2,1,0:T(8,128)S(1)} %shard_map.121.s), channel_id=1, source_target_pairs={{0,4},{1,5},{2,6},{3,7},{4,0},{5,1},{6,2},{7,3},{8,12},{9,13},{10,... | collective-permute-start | bytes 393224 | tf_op jit(solution)/shard_map/ppermute | solution.py:51
  83.0 6.9 %collective-permute-start.24 = (f32[2,256,128]{2,1,0:T(8,128)S(1)}, f32[2,256,128]{2,1,0:T(8,128)S(1)}, u32[]{:S(2)}, u32[]{:S(2)}) collective-permute-start(f32[2,256,128]{2,1,0:T(8,128)S(1)} %get-tuple-element.93), channel_id=1, source_target_pairs={{0,4},{1,2},{2,1},{3,7},{4,0},{5,6},{6,5},{7,3},{8,12},{9,10},{10,... | collective-permute-start | bytes 786440 | tf_op jit(solution)/shard_map/ppermute | solution.py:51
  94.6 5.7 %collective-permute-start.27 = (f32[2,256,128]{2,1,0:T(8,128)S(1)}, f32[2,256,128]{2,1,0:T(8,128)S(1)}, u32[]{:S(2)}, u32[]{:S(2)}) collective-permute-start(f32[2,256,128]{2,1,0:T(8,128)S(1)} %get-tuple-element.98), channel_id=1, source_target_pairs={{0,1},{1,0},{2,3},{3,2},{4,5},{5,4},{6,7},{7,6},{8,9},{9,8},{10,11... | collective-permute-start | bytes 786440 | tf_op jit(solution)/shard_map/ppermute | solution.py:51
  95.0 8.5 %collective-permute-start.28 = (f32[2,256,128]{2,1,0:T(8,128)S(1)}, f32[2,256,128]{2,1,0:T(8,128)S(1)}, u32[]{:S(2)}, u32[]{:S(2)}) collective-permute-start(f32[2,256,128]{2,1,0:T(8,128)S(1)} %get-tuple-element.99), channel_id=1, source_target_pairs={{0,4},{1,2},{2,1},{3,7},{4,0},{5,6},{6,5},{7,3},{8,12},{9,10},{10,... | collective-permute-start | bytes 786440 | tf_op jit(solution)/shard_map/ppermute | solution.py:51
  97.1 8.5 %collective-permute-start.26 = (f32[3,64,256]{2,1,0:T(8,128)S(1)}, f32[3,64,256]{2,1,0:T(8,128)S(1)}, u32[]{:S(2)}, u32[]{:S(2)}) collective-permute-start(f32[3,64,256]{2,1,0:T(8,128)S(1)} %get-tuple-element.97), channel_id=1, source_target_pairs={{0,4},{4,0},{8,12},{12,8},{16,20},{20,16},{24,28},{28,24},{1,5},{5... | collective-permute-start | bytes 589832 | tf_op jit(solution)/shard_map/ppermute | solution.py:332
  97.9 10.1 %collective-permute-start.41 = (f32[3,64,256]{2,1,0:T(8,128)S(1)}, f32[3,64,256]{2,1,0:T(8,128)S(1)}, u32[]{:S(2)}, u32[]{:S(2)}) collective-permute-start(f32[3,64,256]{2,1,0:T(8,128)S(1)} %get-tuple-element.121), channel_id=1, source_target_pairs={{0,2},{1,3},{2,0},{3,1},{4,6},{5,7},{6,4},{7,5},{8,10},{9,11},{10,... | collective-permute-start | bytes 589832 | tf_op jit(solution)/shard_map/ppermute | solution.py:332
  99.0 10.6 %collective-permute-start.30 = (f32[3,64,256]{2,1,0:T(8,128)S(1)}, f32[3,64,256]{2,1,0:T(8,128)S(1)}, u32[]{:S(2)}, u32[]{:S(2)}) collective-permute-start(f32[3,64,256]{2,1,0:T(8,128)S(1)} %get-tuple-element.106), channel_id=1, source_target_pairs={{0,8},{4,12},{8,0},{12,4},{16,24},{20,28},{24,16},{28,20},{1,9},{5... | collective-permute-start | bytes 589832 | tf_op jit(solution)/shard_map/ppermute | solution.py:332
  105.8 9.6 %collective-permute-start.32 = (f32[2,128,128]{2,1,0:T(8,128)S(1)}, f32[2,128,128]{2,1,0:T(8,128)S(1)}, u32[]{:S(2)}, u32[]{:S(2)}) collective-permute-start(f32[2,128,128]{2,1,0:T(8,128)S(1)} %get-tuple-element.108), channel_id=1, source_target_pairs={{0,4},{1,5},{2,6},{3,7},{4,0},{5,1},{6,2},{7,3},{8,12},{9,13},{10,... | collective-permute-start | bytes 393224 | tf_op jit(solution)/shard_map/ppermute | solution.py:51
  107.9 7.6 %collective-permute-start.33 = (f32[2,128,128]{2,1,0:T(8,128)S(1)}, f32[2,128,128]{2,1,0:T(8,128)S(1)}, u32[]{:S(2)}, u32[]{:S(2)}) collective-permute-start(f32[2,128,128]{2,1,0:T(8,128)S(1)} %get-tuple-element.109), channel_id=1, source_target_pairs={{0,1},{1,0},{2,3},{3,2},{4,8},{5,9},{6,10},{7,11},{8,4},{9,5},{10,... | collective-permute-start | bytes 393224 | tf_op jit(solution)/shard_map/ppermute | solution.py:51
  108.1 6.4 %collective-permute-start.42 = (f32[3,32,256]{2,1,0:T(8,128)S(1)}, f32[3,32,256]{2,1,0:T(8,128)S(1)}, u32[]{:S(2)}, u32[]{:S(2)}) collective-permute-start(f32[3,32,256]{2,1,0:T(8,128)S(1)} %get-tuple-element.123), channel_id=1, source_target_pairs={{0,8},{4,12},{8,0},{12,4},{16,24},{20,28},{24,16},{28,20},{1,9},{5... | collective-permute-start | bytes 294920 | tf_op jit(solution)/shard_map/ppermute | solution.py:332
  109.7 5.8 %collective-permute-start.31 = (f32[3,32,256]{2,1,0:T(8,128)S(1)}, f32[3,32,256]{2,1,0:T(8,128)S(1)}, u32[]{:S(2)}, u32[]{:S(2)}) collective-permute-start(f32[3,32,256]{2,1,0:T(8,128)S(1)} %get-tuple-element.107), channel_id=1, source_target_pairs={{0,4},{4,0},{8,12},{12,8},{16,20},{20,16},{24,28},{28,24},{1,5},{5... | collective-permute-start | bytes 294920 | tf_op jit(solution)/shard_map/ppermute | solution.py:332
  114.5 5.3 %collective-permute-start.43 = (f32[3,16,256]{2,1,0:T(8,128)S(1)}, f32[3,16,256]{2,1,0:T(8,128)S(1)}, u32[]{:S(2)}, u32[]{:S(2)}) collective-permute-start(f32[3,16,256]{2,1,0:T(8,128)S(1)} %get-tuple-element.125), channel_id=1, source_target_pairs={{0,4},{4,0},{8,12},{12,8},{16,20},{20,16},{24,28},{28,24},{1,5},{5... | collective-permute-start | bytes 147464 | tf_op jit(solution)/shard_map/ppermute | solution.py:332
  115.5 5.5 %collective-permute-start.48 = (f32[3,16,256]{2,1,0:T(8,128)S(1)}, f32[3,16,256]{2,1,0:T(8,128)S(1)}, u32[]{:S(2)}, u32[]{:S(2)}) collective-permute-start(f32[3,16,256]{2,1,0:T(8,128)S(1)} %get-tuple-element.129), channel_id=1, source_target_pairs={{0,2},{1,3},{2,0},{3,1},{4,6},{5,7},{6,4},{7,5},{8,10},{9,11},{10,... | collective-permute-start | bytes 147464 | tf_op jit(solution)/shard_map/ppermute | solution.py:332
  117.5 6.5 %collective-permute-start.36 = (f32[3,16,256]{2,1,0:T(8,128)S(1)}, f32[3,16,256]{2,1,0:T(8,128)S(1)}, u32[]{:S(2)}, u32[]{:S(2)}) collective-permute-start(f32[3,16,256]{2,1,0:T(8,128)S(1)} %shard_map.131.cur), channel_id=1, source_target_pairs={{0,16},{4,20},{8,24},{12,28},{16,0},{20,4},{24,8},{28,12},{1,17},{... | collective-permute-start | bytes 147464 | tf_op jit(solution)/shard_map/ppermute | solution.py:332
  121.0 6.0 %collective-permute-start.49 = (f32[3,16,256]{2,1,0:T(8,128)S(1)}, f32[3,16,256]{2,1,0:T(8,128)S(1)}, u32[]{:S(2)}, u32[]{:S(2)}) collective-permute-start(f32[3,16,256]{2,1,0:T(8,128)S(1)} %shard_map.145.cur), channel_id=1, source_target_pairs={{0,16},{4,20},{8,24},{12,28},{16,0},{20,4},{24,8},{28,12},{1,17},{... | collective-permute-start | bytes 147464 | tf_op jit(solution)/shard_map/ppermute | solution.py:332
  128.2 5.7 %collective-permute-start.38 = (f32[3,32,256]{2,1,0:T(8,128)S(1)}, f32[3,32,256]{2,1,0:T(8,128)S(1)}, u32[]{:S(2)}, u32[]{:S(2)}) collective-permute-start(f32[3,32,256]{2,1,0:T(8,128)S(1)} %shard_map.133.cur), channel_id=1, source_target_pairs={{0,2},{1,3},{2,0},{3,1},{4,6},{5,7},{6,4},{7,5},{8,10},{9,11},{10,... | collective-permute-start | bytes 294920 | tf_op jit(solution)/shard_map/ppermute | solution.py:332
  129.2 6.2 %collective-permute-start.46 = (f32[3,32,256]{2,1,0:T(8,128)S(1)}, f32[3,32,256]{2,1,0:T(8,128)S(1)}, u32[]{:S(2)}, u32[]{:S(2)}) collective-permute-start(f32[3,32,256]{2,1,0:T(8,128)S(1)} %shard_map.141.cur), channel_id=1, source_target_pairs={{0,8},{4,12},{8,0},{12,4},{16,24},{20,28},{24,16},{28,20},{1,9},{5... | collective-permute-start | bytes 294920 | tf_op jit(solution)/shard_map/ppermute | solution.py:332
  133.9 5.7 %collective-permute-start.39 = (f32[3,64,256]{2,1,0:T(8,128)S(1)}, f32[3,64,256]{2,1,0:T(8,128)S(1)}, u32[]{:S(2)}, u32[]{:S(2)}) collective-permute-start(f32[3,64,256]{2,1,0:T(8,128)S(1)} %shard_map.134.cur), channel_id=1, source_target_pairs={{0,4},{4,0},{8,12},{12,8},{16,20},{20,16},{24,28},{28,24},{1,5},{5... | collective-permute-start | bytes 589832 | tf_op jit(solution)/shard_map/ppermute | solution.py:332
  135.4 5.7 %collective-permute-start.47 = (f32[3,64,256]{2,1,0:T(8,128)S(1)}, f32[3,64,256]{2,1,0:T(8,128)S(1)}, u32[]{:S(2)}, u32[]{:S(2)}) collective-permute-start(f32[3,64,256]{2,1,0:T(8,128)S(1)} %shard_map.142.cur), channel_id=1, source_target_pairs={{0,2},{1,3},{2,0},{3,1},{4,6},{5,7},{6,4},{7,5},{8,10},{9,11},{10,... | collective-permute-start | bytes 589832 | tf_op jit(solution)/shard_map/ppermute | solution.py:332
  136.0 5.7 %collective-permute-start.52 = (f32[3,64,256]{2,1,0:T(8,128)S(1)}, f32[3,64,256]{2,1,0:T(8,128)S(1)}, u32[]{:S(2)}, u32[]{:S(2)}) collective-permute-start(f32[3,64,256]{2,1,0:T(8,128)S(1)} %shard_map.148.cur), channel_id=1, source_target_pairs={{0,8},{4,12},{8,0},{12,4},{16,24},{20,28},{24,16},{28,20},{1,9},{5... | collective-permute-start | bytes 589832 | tf_op jit(solution)/shard_map/ppermute | solution.py:332
  (30 other events, 106.7 us)

commit v5 on v4

--- a/solution.py
+++ b/solution.py
@@ -32,23 +32,68 @@
     return right, left
 
 
-def swap_pairs(n_row, n_col, axis, far):
+def snake(row):
+    return row ^ ((row >> 1) & 1)
+
+
+def work_row():
+    row = lax.axis_index("row")
+    return snake(row)
+
+
+def trades():
+    return (lax.axis_index("row") >> 1) % 2 == 1
+
+
+def across(k, far):
+    return (k + 1 if k % 2 else k - 1) if far else k ^ 1
+
+
+def row_pairs(n_row, n_col, far, stored):
+    pairs = []
+    for row in range(n_row):
+        for j in range(n_col):
+            other = across(row, far)
+            inside = 0 <= other < n_row
+            source = other if inside else row
+            source = source if stored else snake(source)
+            at = j if inside else j ^ 1
+            pairs.append((source * n_col + at, snake(row) * n_col + j))
+    return sorted(pairs)
+
+
+def col_pairs(n_row, n_col, far):
     pairs = []
     for i in range(n_row):
         for j in range(n_col):
-            k, count = (i, n_row) if axis == "row" else (j, n_col)
-            other = k ^ 1 if not far else (k + 1 if k % 2 else k - 1)
-            if axis == "row":
-                to = (other, j) if 0 <= other < count else (i, j ^ 1)
-            else:
-                to = (i, other) if 0 <= other < count else (i ^ 1, j)
+            other = across(j, far)
+            to = (i, other) if 0 <= other < n_col else (i ^ (2 if n_row % 4 == 0 else 1), j)
             pairs.append((i * n_col + j, to[0] * n_col + to[1]))
     return pairs
 
 
+def trade_pairs(n_row, n_col):
+    pairs = []
+    for i in range(n_row):
+        for j in range(n_col):
+            to = (snake(i), j) if snake(i) != i else (i, j ^ 1)
+            pairs.append((i * n_col + j, to[0] * n_col + to[1]))
+    return pairs
+
+
+def move(array, pairs):
+    return lax.ppermute(array, ("row", "col"), pairs)
+
+
 def swap(array, axis, far):
-    pairs = swap_pairs(lax.axis_size("row"), lax.axis_size("col"), axis, far)
-    return lax.ppermute(array, ("row", "col"), pairs)
+    n_row, n_col = lax.axis_size("row"), lax.axis_size("col")
+    if axis == "row":
+        return move(array, row_pairs(n_row, n_col, far, False))
+    return move(array, col_pairs(n_row, n_col, far))
+
+
+def trade(array):
+    return move(array, trade_pairs(lax.axis_size("row"), lax.axis_size("col")))
 
 
 def swap_both(to_near, to_far, axis):
@@ -78,7 +123,7 @@
 class Place:
     def __init__(self, sc, sizes):
         n_row, n_col, rows, cols, rim = sizes
-        self.i, self.j = lax.axis_index("row"), lax.axis_index("col")
+        self.i, self.j = work_row(), lax.axis_index("col")
         self.even_row = self.i % 2 == 0
         self.even_col = self.j % 2 == 0
         self.up = self.i > 0
@@ -142,7 +187,7 @@
 
     peak = lax.fori_loop(0, n_row, peak_of, jnp.float32(0.0))
     mine = buf[
-        pl.ds(pl.multiple_of(lax.axis_index("row") * rows + rim, rim), rows),
+        pl.ds(pl.multiple_of(work_row() * rows + rim, rim), rows),
         pl.ds(pl.multiple_of(lax.axis_index("col") * cols + rim, rim), cols),
     ]
     out[...] = mine + light_ratio * peak
@@ -159,6 +204,7 @@
 
 
 def stage(*arrays):
+    arrays = [pltpu.with_memory_space_constraint(a, pltpu.HBM) for a in arrays]
     size = sum(a.size * a.dtype.itemsize for a in arrays)
     return pl.pallas_call(
         stage_body,
@@ -169,6 +215,19 @@
         compiler_params=pltpu.CompilerParams(vmem_limit_bytes=size + (1 << 20)),
         cost_estimate=pl.CostEstimate(flops=0, bytes_accessed=2 * size, transcendentals=0),
     )(*arrays)
+
+
+def first_halo_body(sizes, s, near, far, out, own):
+    _, _, rows, _, rim = sizes
+    at = Place(None, sizes)
+    here = jnp.where(trades(), near[...], s[...])
+    beside = jnp.where(trades(), s[...], near[...])
+    above = jnp.where(at.even_row, far[...], beside)
+    below = jnp.where(at.even_row, beside, far[...])
+    own[...] = here
+    out[:, :rim] = jnp.where(at.up, above, 0.0)
+    out[:, rim : rim + rows] = here
+    out[:, rim + rows :] = jnp.where(at.down, below, 0.0)
 
 
 def halo_body(sizes, sc, s, near, far, mid, to_near, to_far, ext):
@@ -185,7 +244,7 @@
     to_far[...] = ext[:, pl.ds(at.far_row_at, width)]
 
 
-def view_body(sizes, last, sc, mid, near, far, pr, pi, view, right_t, left_t, *refs):
+def view_body(sizes, last, sc, mid, near, far, pr, pi, view, traded, right_t, left_t, *refs):
     if last:
         gm, to_near, to_far, *parts, spec_scr, win_scr, wave_scr, mix_scr, term_scr = refs
     else:
@@ -198,10 +257,11 @@
     first = at.col == 0
     middle = at.col == half
     for part in range(2):
-        a, b = near[part], far[part]
+        rows_of = pl.ds(at.row, width) if mid.shape[1] > width else slice(None)
+        a, b = near[part, rows_of], far[part, rows_of]
         lft = jnp.where(at.has_left, jnp.where(at.even_col, b, a), 0.0)
         rgt = jnp.where(at.has_right, jnp.where(at.even_col, a, b), 0.0)
-        own = mid[part]
+        own = mid[part, rows_of]
         rl, ro, rr = (pltpu.roll(t, half, 1) for t in (lft, own, rgt))
         win_scr[part, :, :rim] = jnp.where(
             first, lft, jnp.where(middle, jnp.where(lane < half, rl, ro), own)
@@ -222,7 +282,8 @@
         spec = jnp.dot(left_t[...], tall, preferred_element_type=F32)
         spec_scr[m] = spec
         total = total + (spec[:width] * spec[:width] + spec[width:] * spec[width:])
-    factor = view[...] / jnp.maximum(jnp.sqrt(total), amp_floor) - 1.0
+    amps = jnp.where(trades(), traded[...], view[...])
+    factor = amps / jnp.maximum(jnp.sqrt(total), amp_floor) - 1.0
     for m in range(modes):
         rows_of = slice(m * width, (m + 1) * width)
         wave_scr[rows_of, :width] = (spec_scr[m, :width] * factor).astype(BF16)
@@ -281,6 +342,11 @@
     out[...] = s[...] + grad / denom[...][None]
 
 
+def leave_body(state, traded, out_re, out_im):
+    for k, out in enumerate((out_re, out_im)):
+        out[...] = jnp.where(trades(), traded[k], state[k])
+
+
 def bit_of(axis, level):
     return lax.shift_right_logical(lax.axis_index(("row", "col")[axis]), level) % 2
 
@@ -332,7 +398,7 @@
     return lax.ppermute(array, name, [(i, i ^ (1 << level)) for i in range(count)])
 
 
-def sum_terms(keeps, sends, n_row, n_col, beside):
+def sum_terms(keeps, sends, n_row, n_col, beside, late):
     colors = len(keeps)
     each, height, width = keeps[0].shape
     row_bits = [(0, k) for k in range(n_row.bit_length() - 1)]
@@ -365,6 +431,8 @@
         for c in range(colors):
             where = orders[c][r]
             got = swap_bit(curs[c], where)
+            if c == 0 and r == len(turn) - 2:
+                got = late(got)
             outs = [(each, 2 * height, width)]
             (curs[c],) = call(functools.partial(join_body, where), outs)(curs[c], got)
         height *= 2
@@ -379,15 +447,17 @@
     spots[...] = mine.astype(F32)
 
 
-def all_spots(known, n_row, n_col):
-    bits = [(1, k) for k in range(n_col.bit_length() - 1)]
-    local_bits = len(bits)
-    bits += [(0, k) for k in range(n_row.bit_length() - 1)]
+def spot_bits(n_row, n_col):
+    bits = [(0, 0)] + [(1, k) for k in range(n_col.bit_length() - 1)]
+    return bits + [(0, k) for k in range(1, n_row.bit_length() - 1)]
+
+
+def gather_spots(known, bits):
     stops = []
     for where in bits:
         known = known + swap_bit(known, where)
         stops.append(known)
-    return stops[local_bits - 1], known
+    return stops
 
 
 def local(obj_re, obj_im, probe_re, probe_im, amps, positions):
@@ -402,24 +472,28 @@
     state = jnp.stack([obj_re, obj_im])
     shape = (-(-2 * n_row * n_col // 128), 128)
     (known,) = call(functools.partial(enter_body, n_col), [shape], smem=1)(positions.reshape(2))
-    sc, every = all_spots(known, n_row, n_col)
+    bits = spot_bits(n_row, n_col)
+    local_bits = n_col.bit_length()
+    stops = gather_spots(known, bits[:local_bits])
     view = amps.reshape(width, width)
+    traded = trade(view)
     staged = stage(probe_re, probe_im, view, right_t, left_t)
     probe_re, probe_im, view, right_t, left_t = staged
 
     grid = (n_row * rows + 2 * rim, n_col * cols + 3 * rim)
-    (denom,) = call(
+    light = call(
         functools.partial(light_body, sizes, n_dev),
         [(rows, cols)],
         [pltpu.VMEM(grid, F32), pltpu.VMEM((2, width, width + rim), F32)],
         1,
         extra=4 << 20,
         cost=pl.CostEstimate(flops=8 * n_dev * width * width, bytes_accessed=10**7, transcendentals=0),
-    )(every.reshape(-1).astype(jnp.int32), probe_re, probe_im)
+    )
 
     strip = (2, width, cols)
     tile = (2, rows, cols)
     tall = pltpu.VMEM((2, rows + 2 * rim, cols), F32)
+    first_halo = call(functools.partial(first_halo_body, sizes), [(2, rows + 2 * rim, cols), tile])
     halo = call(functools.partial(halo_body, sizes), [strip] * 3, [tall])
     fold = call(functools.partial(fold_body, sizes), [tile] * 3, [tall])
     step = call(functools.partial(step_body, sizes), [tile])
@@ -429,13 +503,25 @@
 
     for turn in range(ITERS):
         last = turn == ITERS - 1
-        near, far = swap_both(state, state, "row")
-        mid, to_near, to_far = halo(sc, state, near, far)
+        if turn == 0:
+            near = swap(state, "row", False)
+            far = move(state, row_pairs(n_row, n_col, True, True))
+            near, far, sc = lax.optimization_barrier((near, far, stops[-1]))
+            most = gather_spots(sc, bits[local_bits:-1])[-1]
+            mid, state = first_halo(state, near, far)
+            to_near = to_far = mid
+        else:
+            near, far = swap_both(state, state, "row")
+            mid, to_near, to_far = halo(sc, state, near, far)
         near, far = swap_both(to_near, to_far, "col")
+        if turn == 0:
+            near, far, most = lax.optimization_barrier((near, far, most))
+            every = gather_spots(most, bits[-1:])[-1]
+            (denom,) = light(every.reshape(-1).astype(jnp.int32), probe_re, probe_im)
         outs = [strip] * 3 + ([terms] * 2 * COLORS if last else [])
         scr = scratch + ([pltpu.VMEM((2 * modes + 1, width, width), F32)] if last else [])
         res = call(functools.partial(view_body, sizes, last), outs, scr, extra=8 << 20)(
-            sc, mid, near, far, probe_re, probe_im, view, right_t, left_t
+            sc, mid, near, far, probe_re, probe_im, view, traded, right_t, left_t
         )
         gm, to_near, to_far = res[:3]
         near, far = swap_both(to_near, to_far, "col")
@@ -455,14 +541,22 @@
         elif r == 1:
             gots[2], a, b = lax.optimization_barrier((gots[2], *held["both"]))
             (held["state"],) = step(state, held["own"], a, b, denom)
+            held["traded"] = trade(held["state"])
         return gots
 
-    mine, other = sum_terms(res[3::2], res[4::2], n_row, n_col, beside)
+    def late(got):
+        got, held["traded"], held["state"] = lax.optimization_barrier(
+            (got, held["traded"], held["state"])
+        )
+        return got
+
+    mine, other = sum_terms(res[3::2], res[4::2], n_row, n_col, beside, late)
     shape = (modes, width, width)
     new_re, new_im = call(functools.partial(probe_body, rim), [shape] * 2)(
         *mine, *other, probe_re, probe_im
     )
-    return (held["state"][0], held["state"][1], new_re, new_im)
+    done_re, done_im = call(leave_body, [(rows, cols)] * 2)(held["state"], held["traded"])
+    return (done_re, done_im, new_re, new_im)
 
 
 def solution(mesh):

time: 146 us -> 139 us (0.952)
  local copies, waits for them, and re-layouts: 5.76 us -> 0.01 us
  waiting for transfers between devices: 55.4 us -> 50.2 us
  Pallas kernels: 19.6 us -> 22.1 us
  starting transfers between devices: 62.7 us -> 64.8 us
    unnamed x12 -> x4, local copies, waits for them, and re-layouts: 5.1 us -> 0.01 us
    ppermute x32, waiting for transfers between devices: 25.4 us -> 22.3 us  [swap_bit(): lax.ppermute(array, name, [(i, i ^ 1 << level) for i in range(count)])]
    ppermute x24 -> x26, waiting for transfers between devices: 30.1 us -> 27.9 us  [move(): return lax.ppermute(array, ('row', 'col'), pairs)]
    pallas_call x1, Pallas kernels: 0.28 us -> 1.95 us  [stage(): pl.pallas_call(stage_body, out_shape=[jax.ShapeDtypeStruct(a.shape, a.dty...]
    ppermute x24 -> x26, starting transfers between devices: 31.5 us -> 32.4 us  [move(): return lax.ppermute(array, ('row', 'col'), pairs)]
    pallas_call x39 -> x40, Pallas kernels: 19.4 us -> 20.1 us  [run(): pl.pallas_call(body, out_shape=[jax.ShapeDtypeStruct(s, F32) for s in out...]
  transfers between devices with their start and end apart: 56 -> 58, of which waited for: 26 -> 25; matrix products, arithmetic and copies ran while one was open for 0% -> 0% of each run, Pallas kernels for 4% -> 6%
where the time goes in v5:
time: 139 us
  starting transfers between devices  64.8 us (47%)
  waiting for transfers between devices  50.2 us (36%)
  Pallas kernels  22.1 us (16%)
    ppermute x32, starting transfers between devices, swap_bit(): lax.ppermute(array, name, [(i, i ^ 1 << level) for i in range(count)])  32.4 us
    ppermute x26, starting transfers between devices, move(): return lax.ppermute(array, ('row', 'col'), pairs)  32.4 us
    ppermute x26, waiting for transfers between devices, move(): return lax.ppermute(array, ('row', 'col'), pairs)  27.9 us
    ppermute x32, waiting for transfers between devices, swap_bit(): lax.ppermute(array, name, [(i, i ^ 1 << level) for i in range(count)])  22.3 us
    pallas_call x40, Pallas kernels, run(): pl.pallas_call(body, out_shape=[jax.ShapeDtypeStruct(s, F32) for s in out...  20.1 us
  transfers between devices with their start and end apart: 58, of which 25 were waited for; matrix products, arithmetic and copies ran while one was open for 0% of the time, Pallas kernels for 6%

profile of v5, /device:TPU:0, one launch (start us, length us, event | category | flops | bytes accessed | tf_op | source)
XLA Modules:
  0.0 139.0 jit_solution(3549750722826343091)
XLA Ops:
  2.1 4.1 %collective-permute-start = (f32[2,128,128]{2,1,0:T(8,128)S(1)}, f32[2,128,128]{2,1,0:T(8,128)S(1)}, u32[]{:S(2)}, u32[]{:S(2)}) collective-permute-start(f32[2,128,128]{2,1,0:T(8,128)S(1)} %pad_maximum_fusion.s), channel_id=1, source_target_pairs={{0,4},{1,5},{2,6},{3,7},{4,0},{5,1},{6,2},{7,3},{8,12},{9,13},{10,... | collective-permute-start | bytes 393224 | tf_op jit(solution)/shard_map/ppermute | solution.py:85
  6.8 4.3 %collective-permute-done.2 = f32[1,128]{1,0:T(1,128)S(1)} collective-permute-done((f32[1,128]{1,0:T(1,128)S(1)}, f32[1,128]{1,0:T(1,128)S(1)}, u32[]{:S(2)}, u32[]{:S(2)}) %collective-permute-start.2) | collective-permute-done | bytes 544 | tf_op jit(solution)/shard_map/ppermute | solution.py:398
  13.8 2.0 %collective-permute-done.4 = f32[1,128]{1,0:T(1,128)S(1)} collective-permute-done((f32[1,128]{1,0:T(1,128)S(1)}, f32[1,128]{1,0:T(1,128)S(1)}, u32[]{:S(2)}, u32[]{:S(2)}) %collective-permute-start.4) | collective-permute-done | bytes 544 | tf_op jit(solution)/shard_map/ppermute | solution.py:398
  17.6 2.9 %collective-permute-start.7 = (f32[1,128]{1,0:T(1,128)S(1)}, f32[1,128]{1,0:T(1,128)S(1)}, u32[]{:S(2)}, u32[]{:S(2)}) collective-permute-start(f32[1,128]{1,0:T(1,128)S(1)} %add.17.sc), channel_id=1, source_target_pairs={{0,8},{4,12},{8,0},{12,4},{16,24},{20,28},{24,16},{28,20},{1,9},{5... | collective-permute-start | bytes 1544 | tf_op jit(solution)/shard_map/ppermute | solution.py:398
  20.5 2.0 %shard_map.113 = (f32[4,256,256]{2,1,0:T(8,128)S(1)}, f32[4,256,256]{2,1,0:T(8,128)S(1)}, f32[256,256]{1,0:T(8,128)S(1)}, bf16[512,512]{1,0:T(8,128)(2,1)S(1)}, bf16[512,512]{1,0:T(8,128)(2,1)S(1)}) custom-call(f32[4,256,256]{2,1,0:T(8,128)} %refs_0_.1, f32[4,256,256]{2,1,0:T(8,128)} %refs_1_.1, f32[256,256]{1,0:T(8,128)} %bitcast.7, ...), custom_call_target="tpu_custom_call" | custom-call | bytes 6815744 | tf_op jit(solution)/shard_map/pallas_call | solution.py:209
  23.8 3.5 %shard_map.114 = (f32[2,256,128]{2,1,0:T(8,128)S(1)}, f32[2,256,128]{2,1,0:T(8,128)S(1)}, f32[2,256,128]{2,1,0:T(8,128)S(1)}) custom-call(f32[1,128]{1,0:T(1,128)S(1)} %add.17.sc, f32[2,384,128]{2,1,0:T(8,128)S(1)} %get-tuple-element.82.mid, f32[2,384,128]{2,1,0:T(8,128)S(1)} %collective-permute-done.5.near, f32[2,384,128]{2,1,0:T(8,128)S(1)} %collective-permute-done.6.far, ...), custom_call_target="tpu_custom_call" | custom-call | tf_op jit(solution)/shard_map/pallas_call | solution.py:110
  27.5 3.7 %collective-permute-start.10 = (f32[2,256,128]{2,1,0:T(8,128)S(1)}, f32[2,256,128]{2,1,0:T(8,128)S(1)}, u32[]{:S(2)}, u32[]{:S(2)}) collective-permute-start(f32[2,256,128]{2,1,0:T(8,128)S(1)} %get-tuple-element.92), channel_id=1, source_target_pairs={{0,8},{1,2},{2,1},{3,11},{4,12},{5,6},{6,5},{7,15},{8,0},{9,10},{1... | collective-permute-start | bytes 786440 | tf_op jit(solution)/shard_map/ppermute | solution.py:85
  31.2 3.2 %collective-permute-start.13 = (f32[1,128]{1,0:T(1,128)S(1)}, f32[1,128]{1,0:T(1,128)S(1)}, u32[]{:S(2)}, u32[]{:S(2)}) collective-permute-start(f32[1,128]{1,0:T(1,128)S(1)} %add.18), channel_id=1, source_target_pairs={{0,16},{4,20},{8,24},{12,28},{16,0},{20,4},{24,8},{28,12},{1,17},{... | collective-permute-start | bytes 1544 | tf_op jit(solution)/shard_map/ppermute | solution.py:398
  37.6 4.2 %shard_map.116.denom = f32[128,128]{1,0:T(8,128)S(1)} custom-call(s32[128]{0:T(128)S(1)} %convert_bitcast_fusion.sc, f32[4,256,256]{2,1,0:T(8,128)S(1)} %get-tuple-element.85.pr.refs_6_, f32[4,256,256]{2,1,0:T(8,128)S(1)} %get-tuple-element.86.pi.refs_7_), custom_call_target="tpu_custom_call" | custom-call | flops 16777216 | bytes 10000000 | tf_op jit(solution)/shard_map/pallas_call | solution.py:110
  42.5 2.8 %collective-permute-start.14 = (f32[2,128,128]{2,1,0:T(8,128)S(1)}, f32[2,128,128]{2,1,0:T(8,128)S(1)}, u32[]{:S(2)}, u32[]{:S(2)}) collective-permute-start(f32[2,128,128]{2,1,0:T(8,128)S(1)} %shard_map.117.s), channel_id=1, source_target_pairs={{0,4},{1,5},{2,6},{3,7},{4,0},{5,1},{6,2},{7,3},{8,12},{9,13},{10,... | collective-permute-start | bytes 393224 | tf_op jit(solution)/shard_map/ppermute | solution.py:85
  45.3 2.9 %collective-permute-done.14.near = f32[2,128,128]{2,1,0:T(8,128)S(1)} collective-permute-done((f32[2,128,128]{2,1,0:T(8,128)S(1)}, f32[2,128,128]{2,1,0:T(8,128)S(1)}, u32[]{:S(2)}, u32[]{:S(2)}) %collective-permute-start.14) | collective-permute-done | bytes 131104 | tf_op jit(solution)/shard_map/ppermute | solution.py:85
  48.5 2.8 %collective-permute-start.17 = (f32[2,256,128]{2,1,0:T(8,128)S(1)}, f32[2,256,128]{2,1,0:T(8,128)S(1)}, u32[]{:S(2)}, u32[]{:S(2)}) collective-permute-start(f32[2,256,128]{2,1,0:T(8,128)S(1)} %get-tuple-element.99), channel_id=1, source_target_pairs={{0,8},{1,2},{2,1},{3,11},{4,12},{5,6},{6,5},{7,15},{8,0},{9,10},{1... | collective-permute-start | bytes 786440 | tf_op jit(solution)/shard_map/ppermute | solution.py:85
  51.3 4.3 %collective-permute-done.17.far = f32[2,256,128]{2,1,0:T(8,128)S(1)} collective-permute-done((f32[2,256,128]{2,1,0:T(8,128)S(1)}, f32[2,256,128]{2,1,0:T(8,128)S(1)}, u32[]{:S(2)}, u32[]{:S(2)}) %collective-permute-start.17) | collective-permute-done | bytes 262176 | tf_op jit(solution)/shard_map/ppermute | solution.py:85
  55.7 3.4 %shard_map.119 = (f32[2,256,128]{2,1,0:T(8,128)S(1)}, f32[2,256,128]{2,1,0:T(8,128)S(1)}, f32[2,256,128]{2,1,0:T(8,128)S(1)}) custom-call(f32[1,128]{1,0:T(1,128)S(1)} %add.17.sc, f32[2,256,128]{2,1,0:T(8,128)S(1)} %get-tuple-element.97.mid, f32[2,256,128]{2,1,0:T(8,128)S(1)} %collective-permute-done.16.near, ...), custom_call_target="tpu_custom_call" | custom-call | tf_op jit(solution)/shard_map/pallas_call | solution.py:110
  59.2 2.1 %collective-permute-start.19 = (f32[2,256,128]{2,1,0:T(8,128)S(1)}, f32[2,256,128]{2,1,0:T(8,128)S(1)}, u32[]{:S(2)}, u32[]{:S(2)}) collective-permute-start(f32[2,256,128]{2,1,0:T(8,128)S(1)} %get-tuple-element.102), channel_id=1, source_target_pairs={{0,8},{1,2},{2,1},{3,11},{4,12},{5,6},{6,5},{7,15},{8,0},{9,10},{1... | collective-permute-start | bytes 786440 | tf_op jit(solution)/shard_map/ppermute | solution.py:85
  61.3 4.3 %collective-permute-done.19.far = f32[2,256,128]{2,1,0:T(8,128)S(1)} collective-permute-done((f32[2,256,128]{2,1,0:T(8,128)S(1)}, f32[2,256,128]{2,1,0:T(8,128)S(1)}, u32[]{:S(2)}, u32[]{:S(2)}) %collective-permute-start.19) | collective-permute-done | bytes 262176 | tf_op jit(solution)/shard_map/ppermute | solution.py:85
  67.3 4.2 %collective-permute-done.20.near = f32[2,128,128]{2,1,0:T(8,128)S(1)} collective-permute-done((f32[2,128,128]{2,1,0:T(8,128)S(1)}, f32[2,128,128]{2,1,0:T(8,128)S(1)}, u32[]{:S(2)}, u32[]{:S(2)}) %collective-permute-start.20) | collective-permute-done | bytes 131104 | tf_op jit(solution)/shard_map/ppermute | solution.py:85
  71.6 3.8 %collective-permute-start.22 = (f32[2,128,128]{2,1,0:T(8,128)S(1)}, f32[2,128,128]{2,1,0:T(8,128)S(1)}, u32[]{:S(2)}, u32[]{:S(2)}) collective-permute-start(f32[2,128,128]{2,1,0:T(8,128)S(1)} %shard_map.121.s), channel_id=1, source_target_pairs={{0,4},{1,5},{2,6},{3,7},{4,0},{5,1},{6,2},{7,3},{8,12},{9,13},{10,... | collective-permute-start | bytes 393224 | tf_op jit(solution)/shard_map/ppermute | solution.py:85
  75.4 2.9 %collective-permute-done.22.near = f32[2,128,128]{2,1,0:T(8,128)S(1)} collective-permute-done((f32[2,128,128]{2,1,0:T(8,128)S(1)}, f32[2,128,128]{2,1,0:T(8,128)S(1)}, u32[]{:S(2)}, u32[]{:S(2)}) %collective-permute-start.22) | collective-permute-done | bytes 131104 | tf_op jit(solution)/shard_map/ppermute | solution.py:85
  78.6 3.1 %collective-permute-start.25 = (f32[2,256,128]{2,1,0:T(8,128)S(1)}, f32[2,256,128]{2,1,0:T(8,128)S(1)}, u32[]{:S(2)}, u32[]{:S(2)}) collective-permute-start(f32[2,256,128]{2,1,0:T(8,128)S(1)} %get-tuple-element.108), channel_id=1, source_target_pairs={{0,8},{1,2},{2,1},{3,11},{4,12},{5,6},{6,5},{7,15},{8,0},{9,10},{1... | collective-permute-start | bytes 786440 | tf_op jit(solution)/shard_map/ppermute | solution.py:85
  81.6 4.3 %collective-permute-done.25.far = f32[2,256,128]{2,1,0:T(8,128)S(1)} collective-permute-done((f32[2,256,128]{2,1,0:T(8,128)S(1)}, f32[2,256,128]{2,1,0:T(8,128)S(1)}, u32[]{:S(2)}, u32[]{:S(2)}) %collective-permute-start.25) | collective-permute-done | bytes 262176 | tf_op jit(solution)/shard_map/ppermute | solution.py:85
  86.0 4.0 %shard_map.123 = (f32[2,256,128]{2,1,0:T(8,128)S(1)}, f32[2,256,128]{2,1,0:T(8,128)S(1)}, f32[2,256,128]{2,1,0:T(8,128)S(1)}, f32[3,128,256]{2,1,0:T(8,128)S(1)}...) custom-call(f32[1,128]{1,0:T(1,128)S(1)} %add.17.sc, ...), custom_call_target="tpu_custom_call" | custom-call | tf_op jit(solution)/shard_map/pallas_call | solution.py:110
  91.1 2.0 %collective-permute-start.29 = (f32[2,256,128]{2,1,0:T(8,128)S(1)}, f32[2,256,128]{2,1,0:T(8,128)S(1)}, u32[]{:S(2)}, u32[]{:S(2)}) collective-permute-start(f32[2,256,128]{2,1,0:T(8,128)S(1)} %get-tuple-element.114), channel_id=1, source_target_pairs={{0,8},{1,2},{2,1},{3,11},{4,12},{5,6},{6,5},{7,15},{8,0},{9,10},{1... | collective-permute-start | bytes 786440 | tf_op jit(solution)/shard_map/ppermute | solution.py:85
  95.2 3.6 %collective-permute-done.29.far = f32[2,256,128]{2,1,0:T(8,128)S(1)} collective-permute-done((f32[2,256,128]{2,1,0:T(8,128)S(1)}, f32[2,256,128]{2,1,0:T(8,128)S(1)}, u32[]{:S(2)}, u32[]{:S(2)}) %collective-permute-start.29) | collective-permute-done | bytes 262176 | tf_op jit(solution)/shard_map/ppermute | solution.py:85
  101.3 2.1 %collective-permute-start.44 = (f32[3,32,256]{2,1,0:T(8,128)S(1)}, f32[3,32,256]{2,1,0:T(8,128)S(1)}, u32[]{:S(2)}, u32[]{:S(2)}) collective-permute-start(f32[3,32,256]{2,1,0:T(8,128)S(1)} %get-tuple-element.143), channel_id=1, source_target_pairs={{0,8},{4,12},{8,0},{12,4},{16,24},{20,28},{24,16},{28,20},{1,9},{5... | collective-permute-start | bytes 294920 | tf_op jit(solution)/shard_map/ppermute | solution.py:398
  105.6 2.1 %collective-permute-start.31 = (f32[3,16,256]{2,1,0:T(8,128)S(1)}, f32[3,16,256]{2,1,0:T(8,128)S(1)}, u32[]{:S(2)}, u32[]{:S(2)}) collective-permute-start(f32[3,16,256]{2,1,0:T(8,128)S(1)} %get-tuple-element.119), channel_id=1, source_target_pairs={{0,8},{4,12},{8,0},{12,4},{16,24},{20,28},{24,16},{28,20},{1,9},{5... | collective-permute-start | bytes 147464 | tf_op jit(solution)/shard_map/ppermute | solution.py:398
  112.0 2.2 %collective-permute-start.46 = (f32[3,16,256]{2,1,0:T(8,128)S(1)}, f32[3,16,256]{2,1,0:T(8,128)S(1)}, u32[]{:S(2)}, u32[]{:S(2)}) collective-permute-start(f32[3,16,256]{2,1,0:T(8,128)S(1)} %shard_map.140.cur), channel_id=1, source_target_pairs={{0,16},{4,20},{8,24},{12,28},{16,0},{20,4},{24,8},{28,12},{1,17},{... | collective-permute-start | bytes 147464 | tf_op jit(solution)/shard_map/ppermute | solution.py:398
  115.0 2.1 %collective-permute-done.32.got = f32[3,16,256]{2,1,0:T(8,128)S(1)} collective-permute-done((f32[3,16,256]{2,1,0:T(8,128)S(1)}, f32[3,16,256]{2,1,0:T(8,128)S(1)}, u32[]{:S(2)}, u32[]{:S(2)}) %collective-permute-start.32) | collective-permute-done | bytes 49184 | tf_op jit(solution)/shard_map/ppermute | solution.py:398
  123.8 2.0 %collective-permute-start.53 = (f32[3,32,256]{2,1,0:T(8,128)S(1)}, f32[3,32,256]{2,1,0:T(8,128)S(1)}, u32[]{:S(2)}, u32[]{:S(2)}) collective-permute-start(f32[3,32,256]{2,1,0:T(8,128)S(1)} %shard_map.148.cur), channel_id=1, source_target_pairs={{0,4},{4,0},{8,12},{12,8},{16,20},{20,16},{24,28},{28,24},{1,5},{5... | collective-permute-start | bytes 294920 | tf_op jit(solution)/shard_map/ppermute | solution.py:398
  130.7 2.0 %collective-permute-done.41.got = f32[3,64,256]{2,1,0:T(8,128)S(1)} collective-permute-done((f32[3,64,256]{2,1,0:T(8,128)S(1)}, f32[3,64,256]{2,1,0:T(8,128)S(1)}, u32[]{:S(2)}, u32[]{:S(2)}) %collective-permute-start.41) | collective-permute-done | bytes 196640 | tf_op jit(solution)/shard_map/ppermute | solution.py:398
  133.4 1.9 %collective-permute-done.54.got = f32[3,64,256]{2,1,0:T(8,128)S(1)} collective-permute-done((f32[3,64,256]{2,1,0:T(8,128)S(1)}, f32[3,64,256]{2,1,0:T(8,128)S(1)}, u32[]{:S(2)}, u32[]{:S(2)}) %collective-permute-start.54) | collective-permute-done | bytes 196640 | tf_op jit(solution)/shard_map/ppermute | solution.py:398
  137.1 1.9 %shard_map.151 = (f32[4,256,256]{2,1,0:T(8,128)}, f32[4,256,256]{2,1,0:T(8,128)}) custom-call(f32[3,128,256]{2,1,0:T(8,128)S(1)} %shard_map.136.refs_0_, f32[3,128,256]{2,1,0:T(8,128)S(1)} %shard_map.144.refs_1_, f32[3,128,256]{2,1,0:T(8,128)S(1)} %shard_map.150.refs_2_, f32[3,128,256]{2,1,0:T(8,128)S(1)} %collective-permute-done.55.refs_3_, ...), custom_call_target="tpu_custom_call" | custom-call | tf_op jit(solution)/shard_map/pallas_call | solution.py:110
  (135 shorter events, 41.1 us)
Async XLA Ops:
  1.5 14.3 %collective-permute-start.1 = (f32[2,128,128]{2,1,0:T(8,128)S(1)}, f32[2,128,128]{2,1,0:T(8,128)S(1)}, u32[]{:S(2)}, u32[]{:S(2)}) collective-permute-start(f32[2,128,128]{2,1,0:T(8,128)S(1)} %pad_maximum_fusion.s), channel_id=1, source_target_pairs={{0,1},{1,0},{2,3},{3,2},{4,12},{5,13},{6,14},{7,15},{8,4},{9,5},{1... | collective-permute-start | bytes 393224 | tf_op jit(solution)/shard_map/ppermute | solution.py:85
  2.1 13.7 %collective-permute-start = (f32[2,128,128]{2,1,0:T(8,128)S(1)}, f32[2,128,128]{2,1,0:T(8,128)S(1)}, u32[]{:S(2)}, u32[]{:S(2)}) collective-permute-start(f32[2,128,128]{2,1,0:T(8,128)S(1)} %pad_maximum_fusion.s), channel_id=1, source_target_pairs={{0,4},{1,5},{2,6},{3,7},{4,0},{5,1},{6,2},{7,3},{8,12},{9,13},{10,... | collective-permute-start | bytes 393224 | tf_op jit(solution)/shard_map/ppermute | solution.py:85
  15.9 7.9 %collective-permute-start.6 = (f32[2,384,128]{2,1,0:T(8,128)S(1)}, f32[2,384,128]{2,1,0:T(8,128)S(1)}, u32[]{:S(2)}, u32[]{:S(2)}) collective-permute-start(f32[2,384,128]{2,1,0:T(8,128)S(1)} %get-tuple-element.82.mid), channel_id=1, source_target_pairs={{0,8},{1,2},{2,1},{3,11},{4,12},{5,6},{6,5},{7,15},{8,0},{9,10},{1... | collective-permute-start | bytes 1179656 | tf_op jit(solution)/shard_map/ppermute | solution.py:85
  16.8 7.1 %collective-permute-start.5 = (f32[2,384,128]{2,1,0:T(8,128)S(1)}, f32[2,384,128]{2,1,0:T(8,128)S(1)}, u32[]{:S(2)}, u32[]{:S(2)}) collective-permute-start(f32[2,384,128]{2,1,0:T(8,128)S(1)} %get-tuple-element.82.mid), channel_id=1, source_target_pairs={{0,1},{1,0},{2,3},{3,2},{4,5},{5,4},{6,7},{7,6},{8,9},{9,8},{10,11... | collective-permute-start | bytes 1179656 | tf_op jit(solution)/shard_map/ppermute | solution.py:85
  17.6 6.2 %collective-permute-start.8 = (f32[256,256]{1,0:T(8,128)S(1)}, f32[256,256]{1,0:T(8,128)S(1)}, u32[]{:S(2)}, u32[]{:S(2)}) collective-permute-start(f32[256,256]{1,0:T(8,128)S(1)} %bitcast.8), channel_id=1, source_target_pairs={{0,1},{1,0},{2,3},{3,2},{4,5},{5,4},{6,7},{7,6},{8,12},{9,13},{10,... | collective-permute-start | bytes 786440 | tf_op jit(solution)/shard_map/ppermute | solution.py:85
  17.6 6.2 %collective-permute-start.7 = (f32[1,128]{1,0:T(1,128)S(1)}, f32[1,128]{1,0:T(1,128)S(1)}, u32[]{:S(2)}, u32[]{:S(2)}) collective-permute-start(f32[1,128]{1,0:T(1,128)S(1)} %add.17.sc), channel_id=1, source_target_pairs={{0,8},{4,12},{8,0},{12,4},{16,24},{20,28},{24,16},{28,20},{1,9},{5... | collective-permute-start | bytes 1544 | tf_op jit(solution)/shard_map/ppermute | solution.py:398
  27.4 7.0 %collective-permute-start.9 = (f32[2,256,128]{2,1,0:T(8,128)S(1)}, f32[2,256,128]{2,1,0:T(8,128)S(1)}, u32[]{:S(2)}, u32[]{:S(2)}) collective-permute-start(f32[2,256,128]{2,1,0:T(8,128)S(1)} %get-tuple-element.91), channel_id=1, source_target_pairs={{0,1},{1,0},{2,3},{3,2},{4,5},{5,4},{6,7},{7,6},{8,9},{9,8},{10,11... | collective-permute-start | bytes 786440 | tf_op jit(solution)/shard_map/ppermute | solution.py:85
  27.5 8.0 %collective-permute-start.10 = (f32[2,256,128]{2,1,0:T(8,128)S(1)}, f32[2,256,128]{2,1,0:T(8,128)S(1)}, u32[]{:S(2)}, u32[]{:S(2)}) collective-permute-start(f32[2,256,128]{2,1,0:T(8,128)S(1)} %get-tuple-element.92), channel_id=1, source_target_pairs={{0,8},{1,2},{2,1},{3,11},{4,12},{5,6},{6,5},{7,15},{8,0},{9,10},{1... | collective-permute-start | bytes 786440 | tf_op jit(solution)/shard_map/ppermute | solution.py:85
  31.2 6.4 %collective-permute-start.13 = (f32[1,128]{1,0:T(1,128)S(1)}, f32[1,128]{1,0:T(1,128)S(1)}, u32[]{:S(2)}, u32[]{:S(2)}) collective-permute-start(f32[1,128]{1,0:T(1,128)S(1)} %add.18), channel_id=1, source_target_pairs={{0,16},{4,20},{8,24},{12,28},{16,0},{20,4},{24,8},{28,12},{1,17},{... | collective-permute-start | bytes 1544 | tf_op jit(solution)/shard_map/ppermute | solution.py:398
  35.8 6.1 %collective-permute-start.11 = (f32[2,128,128]{2,1,0:T(8,128)S(1)}, f32[2,128,128]{2,1,0:T(8,128)S(1)}, u32[]{:S(2)}, u32[]{:S(2)}) collective-permute-start(f32[2,128,128]{2,1,0:T(8,128)S(1)} %get-tuple-element.94), channel_id=1, source_target_pairs={{0,4},{1,5},{2,6},{3,7},{4,0},{5,1},{6,2},{7,3},{8,12},{9,13},{10,... | collective-permute-start | bytes 393224 | tf_op jit(solution)/shard_map/ppermute | solution.py:85
  42.5 5.8 %collective-permute-start.14 = (f32[2,128,128]{2,1,0:T(8,128)S(1)}, f32[2,128,128]{2,1,0:T(8,128)S(1)}, u32[]{:S(2)}, u32[]{:S(2)}) collective-permute-start(f32[2,128,128]{2,1,0:T(8,128)S(1)} %shard_map.117.s), channel_id=1, source_target_pairs={{0,4},{1,5},{2,6},{3,7},{4,0},{5,1},{6,2},{7,3},{8,12},{9,13},{10,... | collective-permute-start | bytes 393224 | tf_op jit(solution)/shard_map/ppermute | solution.py:85
  48.5 7.1 %collective-permute-start.17 = (f32[2,256,128]{2,1,0:T(8,128)S(1)}, f32[2,256,128]{2,1,0:T(8,128)S(1)}, u32[]{:S(2)}, u32[]{:S(2)}) collective-permute-start(f32[2,256,128]{2,1,0:T(8,128)S(1)} %get-tuple-element.99), channel_id=1, source_target_pairs={{0,8},{1,2},{2,1},{3,11},{4,12},{5,6},{6,5},{7,15},{8,0},{9,10},{1... | collective-permute-start | bytes 786440 | tf_op jit(solution)/shard_map/ppermute | solution.py:85
  59.2 6.5 %collective-permute-start.19 = (f32[2,256,128]{2,1,0:T(8,128)S(1)}, f32[2,256,128]{2,1,0:T(8,128)S(1)}, u32[]{:S(2)}, u32[]{:S(2)}) collective-permute-start(f32[2,256,128]{2,1,0:T(8,128)S(1)} %get-tuple-element.102), channel_id=1, source_target_pairs={{0,8},{1,2},{2,1},{3,11},{4,12},{5,6},{6,5},{7,15},{8,0},{9,10},{1... | collective-permute-start | bytes 786440 | tf_op jit(solution)/shard_map/ppermute | solution.py:85
  65.9 5.6 %collective-permute-start.20 = (f32[2,128,128]{2,1,0:T(8,128)S(1)}, f32[2,128,128]{2,1,0:T(8,128)S(1)}, u32[]{:S(2)}, u32[]{:S(2)}) collective-permute-start(f32[2,128,128]{2,1,0:T(8,128)S(1)} %get-tuple-element.104), channel_id=1, source_target_pairs={{0,4},{1,5},{2,6},{3,7},{4,0},{5,1},{6,2},{7,3},{8,12},{9,13},{10,... | collective-permute-start | bytes 393224 | tf_op jit(solution)/shard_map/ppermute | solution.py:85
  71.6 6.7 %collective-permute-start.22 = (f32[2,128,128]{2,1,0:T(8,128)S(1)}, f32[2,128,128]{2,1,0:T(8,128)S(1)}, u32[]{:S(2)}, u32[]{:S(2)}) collective-permute-start(f32[2,128,128]{2,1,0:T(8,128)S(1)} %shard_map.121.s), channel_id=1, source_target_pairs={{0,4},{1,5},{2,6},{3,7},{4,0},{5,1},{6,2},{7,3},{8,12},{9,13},{10,... | collective-permute-start | bytes 393224 | tf_op jit(solution)/shard_map/ppermute | solution.py:85
  78.6 7.4 %collective-permute-start.25 = (f32[2,256,128]{2,1,0:T(8,128)S(1)}, f32[2,256,128]{2,1,0:T(8,128)S(1)}, u32[]{:S(2)}, u32[]{:S(2)}) collective-permute-start(f32[2,256,128]{2,1,0:T(8,128)S(1)} %get-tuple-element.108), channel_id=1, source_target_pairs={{0,8},{1,2},{2,1},{3,11},{4,12},{5,6},{6,5},{7,15},{8,0},{9,10},{1... | collective-permute-start | bytes 786440 | tf_op jit(solution)/shard_map/ppermute | solution.py:85
  91.1 7.8 %collective-permute-start.29 = (f32[2,256,128]{2,1,0:T(8,128)S(1)}, f32[2,256,128]{2,1,0:T(8,128)S(1)}, u32[]{:S(2)}, u32[]{:S(2)}) collective-permute-start(f32[2,256,128]{2,1,0:T(8,128)S(1)} %get-tuple-element.114), channel_id=1, source_target_pairs={{0,8},{1,2},{2,1},{3,11},{4,12},{5,6},{6,5},{7,15},{8,0},{9,10},{1... | collective-permute-start | bytes 786440 | tf_op jit(solution)/shard_map/ppermute | solution.py:85
  93.1 5.7 %collective-permute-start.27 = (f32[3,64,256]{2,1,0:T(8,128)S(1)}, f32[3,64,256]{2,1,0:T(8,128)S(1)}, u32[]{:S(2)}, u32[]{:S(2)}) collective-permute-start(f32[3,64,256]{2,1,0:T(8,128)S(1)} %get-tuple-element.112), channel_id=1, source_target_pairs={{0,4},{4,0},{8,12},{12,8},{16,20},{20,16},{24,28},{28,24},{1,5},{5... | collective-permute-start | bytes 589832 | tf_op jit(solution)/shard_map/ppermute | solution.py:398
  93.3 8.0 %collective-permute-start.43 = (f32[3,64,256]{2,1,0:T(8,128)S(1)}, f32[3,64,256]{2,1,0:T(8,128)S(1)}, u32[]{:S(2)}, u32[]{:S(2)}) collective-permute-start(f32[3,64,256]{2,1,0:T(8,128)S(1)} %get-tuple-element.141), channel_id=1, source_target_pairs={{0,2},{1,3},{2,0},{3,1},{4,6},{5,7},{6,4},{7,5},{8,10},{9,11},{10,... | collective-permute-start | bytes 589832 | tf_op jit(solution)/shard_map/ppermute | solution.py:398
  94.1 9.3 %collective-permute-start.36 = (f32[3,64,256]{2,1,0:T(8,128)S(1)}, f32[3,64,256]{2,1,0:T(8,128)S(1)}, u32[]{:S(2)}, u32[]{:S(2)}) collective-permute-start(f32[3,64,256]{2,1,0:T(8,128)S(1)} %get-tuple-element.127), channel_id=1, source_target_pairs={{0,8},{4,12},{8,0},{12,4},{16,24},{20,28},{24,16},{28,20},{1,9},{5... | collective-permute-start | bytes 589832 | tf_op jit(solution)/shard_map/ppermute | solution.py:398
  99.1 10.1 %collective-permute-start.38 = (f32[2,128,128]{2,1,0:T(8,128)S(1)}, f32[2,128,128]{2,1,0:T(8,128)S(1)}, u32[]{:S(2)}, u32[]{:S(2)}) collective-permute-start(f32[2,128,128]{2,1,0:T(8,128)S(1)} %get-tuple-element.129), channel_id=1, source_target_pairs={{0,4},{1,5},{2,6},{3,7},{4,0},{5,1},{6,2},{7,3},{8,12},{9,13},{10,... | collective-permute-start | bytes 393224 | tf_op jit(solution)/shard_map/ppermute | solution.py:85
  100.3 8.9 %collective-permute-start.39 = (f32[2,128,128]{2,1,0:T(8,128)S(1)}, f32[2,128,128]{2,1,0:T(8,128)S(1)}, u32[]{:S(2)}, u32[]{:S(2)}) collective-permute-start(f32[2,128,128]{2,1,0:T(8,128)S(1)} %get-tuple-element.130), channel_id=1, source_target_pairs={{0,1},{1,0},{2,3},{3,2},{4,12},{5,13},{6,14},{7,15},{8,16},{9,17},... | collective-permute-start | bytes 393224 | tf_op jit(solution)/shard_map/ppermute | solution.py:85
  101.3 6.3 %collective-permute-start.44 = (f32[3,32,256]{2,1,0:T(8,128)S(1)}, f32[3,32,256]{2,1,0:T(8,128)S(1)}, u32[]{:S(2)}, u32[]{:S(2)}) collective-permute-start(f32[3,32,256]{2,1,0:T(8,128)S(1)} %get-tuple-element.143), channel_id=1, source_target_pairs={{0,8},{4,12},{8,0},{12,4},{16,24},{20,28},{24,16},{28,20},{1,9},{5... | collective-permute-start | bytes 294920 | tf_op jit(solution)/shard_map/ppermute | solution.py:398
  103.5 5.7 %collective-permute-start.37 = (f32[3,32,256]{2,1,0:T(8,128)S(1)}, f32[3,32,256]{2,1,0:T(8,128)S(1)}, u32[]{:S(2)}, u32[]{:S(2)}) collective-permute-start(f32[3,32,256]{2,1,0:T(8,128)S(1)} %get-tuple-element.128), channel_id=1, source_target_pairs={{0,4},{4,0},{8,12},{12,8},{16,20},{20,16},{24,28},{28,24},{1,5},{5... | collective-permute-start | bytes 294920 | tf_op jit(solution)/shard_map/ppermute | solution.py:398
  105.6 5.4 %collective-permute-start.31 = (f32[3,16,256]{2,1,0:T(8,128)S(1)}, f32[3,16,256]{2,1,0:T(8,128)S(1)}, u32[]{:S(2)}, u32[]{:S(2)}) collective-permute-start(f32[3,16,256]{2,1,0:T(8,128)S(1)} %get-tuple-element.119), channel_id=1, source_target_pairs={{0,8},{4,12},{8,0},{12,4},{16,24},{20,28},{24,16},{28,20},{1,9},{5... | collective-permute-start | bytes 147464 | tf_op jit(solution)/shard_map/ppermute | solution.py:398
  111.1 6.1 %collective-permute-start.32 = (f32[3,16,256]{2,1,0:T(8,128)S(1)}, f32[3,16,256]{2,1,0:T(8,128)S(1)}, u32[]{:S(2)}, u32[]{:S(2)}) collective-permute-start(f32[3,16,256]{2,1,0:T(8,128)S(1)} %shard_map.127.cur), channel_id=1, source_target_pairs={{0,16},{4,20},{8,24},{12,28},{16,0},{20,4},{24,8},{28,12},{1,17},{... | collective-permute-start | bytes 147464 | tf_op jit(solution)/shard_map/ppermute | solution.py:398
  112.0 6.2 %collective-permute-start.46 = (f32[3,16,256]{2,1,0:T(8,128)S(1)}, f32[3,16,256]{2,1,0:T(8,128)S(1)}, u32[]{:S(2)}, u32[]{:S(2)}) collective-permute-start(f32[3,16,256]{2,1,0:T(8,128)S(1)} %shard_map.140.cur), channel_id=1, source_target_pairs={{0,16},{4,20},{8,24},{12,28},{16,0},{20,4},{24,8},{28,12},{1,17},{... | collective-permute-start | bytes 147464 | tf_op jit(solution)/shard_map/ppermute | solution.py:398
  120.3 5.5 %collective-permute-start.40 = (f32[2,128,128]{2,1,0:T(8,128)S(1)}, f32[2,128,128]{2,1,0:T(8,128)S(1)}, u32[]{:S(2)}, u32[]{:S(2)}) collective-permute-start(f32[2,128,128]{2,1,0:T(8,128)S(1)} %shard_map.133.state), channel_id=1, source_target_pairs={{0,1},{1,0},{2,3},{3,2},{4,5},{5,4},{6,7},{7,6},{8,12},{9,13},{10,... | collective-permute-start | bytes 393224 | tf_op jit(solution)/shard_map/ppermute | solution.py:85
  123.8 5.7 %collective-permute-start.53 = (f32[3,32,256]{2,1,0:T(8,128)S(1)}, f32[3,32,256]{2,1,0:T(8,128)S(1)}, u32[]{:S(2)}, u32[]{:S(2)}) collective-permute-start(f32[3,32,256]{2,1,0:T(8,128)S(1)} %shard_map.148.cur), channel_id=1, source_target_pairs={{0,4},{4,0},{8,12},{12,8},{16,20},{20,16},{24,28},{28,24},{1,5},{5... | collective-permute-start | bytes 294920 | tf_op jit(solution)/shard_map/ppermute | solution.py:398
  126.1 6.6 %collective-permute-start.41 = (f32[3,64,256]{2,1,0:T(8,128)S(1)}, f32[3,64,256]{2,1,0:T(8,128)S(1)}, u32[]{:S(2)}, u32[]{:S(2)}) collective-permute-start(f32[3,64,256]{2,1,0:T(8,128)S(1)} %shard_map.135.cur), channel_id=1, source_target_pairs={{0,4},{4,0},{8,12},{12,8},{16,20},{20,16},{24,28},{28,24},{1,5},{5... | collective-permute-start | bytes 589832 | tf_op jit(solution)/shard_map/ppermute | solution.py:398
  127.5 5.7 %collective-permute-start.49 = (f32[3,64,256]{2,1,0:T(8,128)S(1)}, f32[3,64,256]{2,1,0:T(8,128)S(1)}, u32[]{:S(2)}, u32[]{:S(2)}) collective-permute-start(f32[3,64,256]{2,1,0:T(8,128)S(1)} %shard_map.143.cur), channel_id=1, source_target_pairs={{0,2},{1,3},{2,0},{3,1},{4,6},{5,7},{6,4},{7,5},{8,10},{9,11},{10,... | collective-permute-start | bytes 589832 | tf_op jit(solution)/shard_map/ppermute | solution.py:398
  129.5 5.7 %collective-permute-start.54 = (f32[3,64,256]{2,1,0:T(8,128)S(1)}, f32[3,64,256]{2,1,0:T(8,128)S(1)}, u32[]{:S(2)}, u32[]{:S(2)}) collective-permute-start(f32[3,64,256]{2,1,0:T(8,128)S(1)} %shard_map.149.cur), channel_id=1, source_target_pairs={{0,8},{4,12},{8,0},{12,4},{16,24},{20,28},{24,16},{28,20},{1,9},{5... | collective-permute-start | bytes 589832 | tf_op jit(solution)/shard_map/ppermute | solution.py:398
  (28 other events, 118.2 us)

commit v6 on v5

--- a/solution.py
+++ b/solution.py
@@ -23,13 +23,37 @@
 
 
 def tables(width):
-    index = np.arange(width)
-    angle = (index[:, None] * index[None, :] % width) * (2.0 * math.pi / width)
-    real = (np.cos(angle) / math.sqrt(width)).astype(np.float32)
-    imag = (-np.sin(angle) / math.sqrt(width)).astype(np.float32)
-    right = np.block([[real, imag], [-imag, real]]).astype(BF16)
-    left = np.block([[real, -imag], [imag, real]]).astype(BF16)
-    return right, left
+    half = width // 2
+    angle = (np.arange(half)[:, None] * np.arange(width)[None, :] % width) * (2.0 * math.pi / width)
+    real = np.cos(angle) / math.sqrt(width)
+    imag = -np.sin(angle) / math.sqrt(width)
+    pairs = []
+    for k in range(2):
+        re, im = real[:, k::2], imag[:, k::2]
+        pairs.append(np.block([[re, im], [-im, re]]))
+    return np.stack(pairs + [p.T for p in pairs]).astype(np.float32).astype(BF16)
+
+
+def sort_body(view, out):
+    width = view.shape[0]
+    half = width // 2
+    row = lax.broadcasted_iota(jnp.int32, (width, width), 0)
+    col = lax.broadcasted_iota(jnp.int32, (width, width), 1)
+
+    def source(k):
+        return jnp.where(k < half, 2 * k, 2 * (k - half) + 1)
+
+    def picked(left, rows):
+        pick = jnp.where(col == source(row) if rows else row == source(col), 1.0, 0.0).astype(BF16)
+        total = jnp.zeros((width, width), F32)
+        for _ in range(3):
+            part = left.astype(BF16)
+            left = left - part.astype(F32)
+            pair = (pick, part) if rows else (part, pick)
+            total = total + jnp.dot(*pair, preferred_element_type=F32)
+        return total
+
+    out[...] = picked(picked(view[...], True), False)
 
 
 def snake(row):
@@ -244,11 +268,11 @@
     to_far[...] = ext[:, pl.ds(at.far_row_at, width)]
 
 
-def view_body(sizes, last, sc, mid, near, far, pr, pi, view, traded, right_t, left_t, *refs):
+def view_body(sizes, last, sc, mid, near, far, pr, pi, view, traded, tabs, *refs):
     if last:
-        gm, to_near, to_far, *parts, spec_scr, win_scr, wave_scr, mix_scr, term_scr = refs
+        gm, to_near, to_far, *parts, spec_scr, win_scr, wave_e, wave_o, mix_e, mix_o, term_scr = refs
     else:
-        gm, to_near, to_far, spec_scr, win_scr, wave_scr, mix_scr = refs
+        gm, to_near, to_far, spec_scr, win_scr, wave_e, wave_o, mix_e, mix_o = refs
     _, _, _, _, rim = sizes
     at = Place(sc, sizes)
     modes, width = pr.shape[0], pr.shape[1]
@@ -269,32 +293,62 @@
         win_scr[part, :, rim:] = jnp.where(
             first, own, jnp.where(middle, jnp.where(lane < half, ro, rr), rgt)
         )
+    even, odd, even_t, odd_t = range(4)
     for m in range(modes):
         wr, wi = win_scr[0], win_scr[1]
-        rows_of = slice(m * width, (m + 1) * width)
-        wave_scr[rows_of, :width] = (pr[m] * wr - pi[m] * wi).astype(BF16)
-        wave_scr[rows_of, width:] = (pr[m] * wi + pi[m] * wr).astype(BF16)
-    mix_scr[...] = jnp.dot(wave_scr[...], right_t[...], preferred_element_type=F32).astype(BF16)
-    total = jnp.zeros((width, width), F32)
+        here = slice(m * width, (m + 1) * width)
+        for k, psi in enumerate((pr[m] * wr - pi[m] * wi, pr[m] * wi + pi[m] * wr)):
+            lanes = slice(k * rim, (k + 1) * rim)
+            wave_e[here, lanes] = (psi[:, :rim] + psi[:, rim:]).astype(BF16)
+            wave_o[here, lanes] = (psi[:, :rim] - psi[:, rim:]).astype(BF16)
+    mix_e[...] = jnp.dot(wave_e[...], tabs[even], preferred_element_type=F32)
+    mix_o[...] = jnp.dot(wave_o[...], tabs[odd], preferred_element_type=F32)
+    total = [jnp.zeros((rim, width), F32), jnp.zeros((rim, width), F32)]
     for m in range(modes):
-        mixed = mix_scr[m * width : (m + 1) * width]
-        tall = jnp.concatenate([mixed[:, :width], mixed[:, width:]], axis=0)
-        spec = jnp.dot(left_t[...], tall, preferred_element_type=F32)
-        spec_scr[m] = spec
-        total = total + (spec[:width] * spec[:width] + spec[width:] * spec[width:])
-    amps = jnp.where(trades(), traded[...], view[...])
-    factor = amps / jnp.maximum(jnp.sqrt(total), amp_floor) - 1.0
-    for m in range(modes):
-        rows_of = slice(m * width, (m + 1) * width)
-        wave_scr[rows_of, :width] = (spec_scr[m, :width] * factor).astype(BF16)
-        wave_scr[rows_of, width:] = (spec_scr[m, width:] * factor).astype(BF16)
-    mix_scr[...] = jnp.dot(wave_scr[...], left_t[...], preferred_element_type=F32).astype(BF16)
+        top, low = slice(m * width, m * width + rim), slice(m * width + rim, (m + 1) * width)
+        for k, sign in ((0, 1.0), (1, -1.0)):
+            e = mix_e[top] + sign * mix_e[low]
+            o = mix_o[top] + sign * mix_o[low]
+            tall = jnp.concatenate(
+                [
+                    jnp.concatenate([e[:, :rim], o[:, :rim]], axis=1),
+                    jnp.concatenate([e[:, rim:], o[:, rim:]], axis=1),
+                ],
+                axis=0,
+            ).astype(BF16)
+            spec = jnp.dot(tabs[even_t + k], tall, preferred_element_type=F32)
+            spec_scr[m, k] = spec
+            total[k] = total[k] + (spec[:rim] * spec[:rim] + spec[rim:] * spec[rim:])
+    for k in range(2):
+        band = slice(k * rim, (k + 1) * rim)
+        amps = jnp.where(trades(), traded[band], view[band])
+        factor = amps / jnp.maximum(jnp.sqrt(total[k]), amp_floor) - 1.0
+        for m in range(modes):
+            here = slice((2 * m + k) * rim, (2 * m + k + 1) * rim)
+            for part in range(2):
+                lanes = slice(part * rim, (part + 1) * rim)
+                change = spec_scr[m, k, lanes] * factor
+                wave_e[here, lanes] = change[:, :rim].astype(BF16)
+                wave_o[here, lanes] = change[:, rim:].astype(BF16)
+    mix_e[...] = jnp.dot(wave_e[...], tabs[even_t], preferred_element_type=F32)
+    mix_o[...] = jnp.dot(wave_o[...], tabs[odd_t], preferred_element_type=F32)
     grad = [jnp.zeros((width, width), F32), jnp.zeros((width, width), F32)]
     for m in range(modes):
-        mixed = mix_scr[m * width : (m + 1) * width]
-        tall = jnp.concatenate([mixed[:, :width], mixed[:, width:]], axis=0)
-        back = jnp.dot(right_t[...], tall, preferred_element_type=F32)
-        er, ei = back[:width], back[width:]
+        ends = []
+        for k in range(2):
+            here = slice((2 * m + k) * rim, (2 * m + k + 1) * rim)
+            plus, minus = mix_e[here] + mix_o[here], mix_e[here] - mix_o[here]
+            tall = jnp.concatenate(
+                [
+                    jnp.concatenate([plus[:, :rim], minus[:, :rim]], axis=1),
+                    jnp.concatenate([plus[:, rim:], minus[:, rim:]], axis=1),
+                ],
+                axis=0,
+            ).astype(BF16)
+            ends.append(jnp.dot(tabs[even + k], tall, preferred_element_type=F32))
+        plus, minus = ends[0] + ends[1], ends[0] - ends[1]
+        er = jnp.concatenate([plus[:rim], minus[:rim]], axis=0)
+        ei = jnp.concatenate([plus[rim:], minus[rim:]], axis=0)
         grad[0] = grad[0] + (pr[m] * er + pi[m] * ei)
         grad[1] = grad[1] + (pr[m] * ei - pi[m] * er)
         if last:
@@ -467,18 +521,16 @@
     n_row, n_col = lax.axis_size("row"), lax.axis_size("col")
     n_dev = n_row * n_col
     sizes = (n_row, n_col, rows, cols, rim)
-    right_np, left_np = tables(width)
-    right_t, left_t = jnp.asarray(right_np), jnp.asarray(left_np)
+    tabs = jnp.asarray(tables(width))
     state = jnp.stack([obj_re, obj_im])
     shape = (-(-2 * n_row * n_col // 128), 128)
     (known,) = call(functools.partial(enter_body, n_col), [shape], smem=1)(positions.reshape(2))
     bits = spot_bits(n_row, n_col)
     local_bits = n_col.bit_length()
     stops = gather_spots(known, bits[:local_bits])
-    view = amps.reshape(width, width)
-    traded = trade(view)
-    staged = stage(probe_re, probe_im, view, right_t, left_t)
-    probe_re, probe_im, view, right_t, left_t = staged
+    (view,) = call(sort_body, [(width, width)])(amps.reshape(width, width))
+    view_raw = view
+    probe_re, probe_im, tabs = stage(probe_re, probe_im, tabs)
 
     grid = (n_row * rows + 2 * rim, n_col * cols + 3 * rim)
     light = call(
@@ -497,8 +549,9 @@
     halo = call(functools.partial(halo_body, sizes), [strip] * 3, [tall])
     fold = call(functools.partial(fold_body, sizes), [tile] * 3, [tall])
     step = call(functools.partial(step_body, sizes), [tile])
-    scratch = [pltpu.VMEM((modes, 2 * width, width), F32), pltpu.VMEM((2, width, width), F32)]
-    scratch += [pltpu.VMEM((modes * width, 2 * width), BF16)] * 2
+    scratch = [pltpu.VMEM((modes, 2, width, width), F32), pltpu.VMEM((2, width, width), F32)]
+    scratch += [pltpu.VMEM((modes * width, width), BF16)] * 2
+    scratch += [pltpu.VMEM((modes * width, width), F32)] * 2
     terms = ((2 * modes + 1) // COLORS, rim, width)
 
     for turn in range(ITERS):
@@ -506,7 +559,8 @@
         if turn == 0:
             near = swap(state, "row", False)
             far = move(state, row_pairs(n_row, n_col, True, True))
-            near, far, sc = lax.optimization_barrier((near, far, stops[-1]))
+            near, far, sc, view_late = lax.optimization_barrier((near, far, stops[-1], view_raw))
+            traded = trade(view_late)
             most = gather_spots(sc, bits[local_bits:-1])[-1]
             mid, state = first_halo(state, near, far)
             to_near = to_far = mid
@@ -521,7 +575,7 @@
         outs = [strip] * 3 + ([terms] * 2 * COLORS if last else [])
         scr = scratch + ([pltpu.VMEM((2 * modes + 1, width, width), F32)] if last else [])
         res = call(functools.partial(view_body, sizes, last), outs, scr, extra=8 << 20)(
-            sc, mid, near, far, probe_re, probe_im, view, traded, right_t, left_t
+            sc, mid, near, far, probe_re, probe_im, view, traded, tabs
         )
         gm, to_near, to_far = res[:3]
         near, far = swap_both(to_near, to_far, "col")

time: 139 us -> 137 us (0.986)
  Pallas kernels: 22.1 us -> 20.6 us
    pallas_call x40 -> x41, Pallas kernels: 20.1 us -> 18.9 us  [run(): pl.pallas_call(body, out_shape=[jax.ShapeDtypeStruct(s, F32) for s in out...]
where the time goes in v6:
time: 137 us
  starting transfers between devices  64.8 us (47%)
  waiting for transfers between devices  49.8 us (36%)
  Pallas kernels  20.6 us (15%)
    ppermute x32, starting transfers between devices, swap_bit(): lax.ppermute(array, name, [(i, i ^ 1 << level) for i in range(count)])  32.5 us
    ppermute x26, starting transfers between devices, move(): return lax.ppermute(array, ('row', 'col'), pairs)  32.4 us
    ppermute x26, waiting for transfers between devices, move(): return lax.ppermute(array, ('row', 'col'), pairs)  28 us
    ppermute x32, waiting for transfers between devices, swap_bit(): lax.ppermute(array, name, [(i, i ^ 1 << level) for i in range(count)])  21.8 us
    pallas_call x41, Pallas kernels, run(): pl.pallas_call(body, out_shape=[jax.ShapeDtypeStruct(s, F32) for s in out...  18.9 us
  transfers between devices with their start and end apart: 58, of which 25 were waited for; matrix products, arithmetic and copies ran while one was open for 0% of the time, Pallas kernels for 6%

profile of v6, /device:TPU:0, one launch (start us, length us, event | category | flops | bytes accessed | tf_op | source)
XLA Modules:
  0.0 137.2 jit_solution(16224028518187351087)
XLA Ops:
  2.1 4.1 %collective-permute-start = (f32[2,128,128]{2,1,0:T(8,128)S(1)}, f32[2,128,128]{2,1,0:T(8,128)S(1)}, u32[]{:S(2)}, u32[]{:S(2)}) collective-permute-start(f32[2,128,128]{2,1,0:T(8,128)S(1)} %pad_maximum_fusion.s), channel_id=1, source_target_pairs={{0,4},{1,5},{2,6},{3,7},{4,0},{5,1},{6,2},{7,3},{8,12},{9,13},{10,... | collective-permute-start | bytes 393224 | tf_op jit(solution)/shard_map/ppermute | solution.py:109
  6.8 4.3 %collective-permute-done.2 = f32[1,128]{1,0:T(1,128)S(1)} collective-permute-done((f32[1,128]{1,0:T(1,128)S(1)}, f32[1,128]{1,0:T(1,128)S(1)}, u32[]{:S(2)}, u32[]{:S(2)}) %collective-permute-start.2) | collective-permute-done | bytes 544 | tf_op jit(solution)/shard_map/ppermute | solution.py:452
  17.6 2.9 %collective-permute-start.7 = (f32[1,128]{1,0:T(1,128)S(1)}, f32[1,128]{1,0:T(1,128)S(1)}, u32[]{:S(2)}, u32[]{:S(2)}) collective-permute-start(f32[1,128]{1,0:T(1,128)S(1)} %add.17.sc), channel_id=1, source_target_pairs={{0,8},{4,12},{8,0},{12,4},{16,24},{20,28},{24,16},{28,20},{1,9},{5... | collective-permute-start | bytes 1544 | tf_op jit(solution)/shard_map/ppermute | solution.py:452
  23.9 2.9 %shard_map.106 = (f32[2,256,128]{2,1,0:T(8,128)S(1)}, f32[2,256,128]{2,1,0:T(8,128)S(1)}, f32[2,256,128]{2,1,0:T(8,128)S(1)}) custom-call(f32[1,128]{1,0:T(1,128)S(1)} %add.17.sc, f32[2,384,128]{2,1,0:T(8,128)S(1)} %get-tuple-element.81.mid, f32[2,384,128]{2,1,0:T(8,128)S(1)} %collective-permute-done.5.near, f32[2,384,128]{2,1,0:T(8,128)S(1)} %collective-permute-done.6.far, ...), custom_call_target="tpu_custom_call" | custom-call | tf_op jit(solution)/shard_map/pallas_call | solution.py:134
  26.9 3.7 %collective-permute-start.10 = (f32[2,256,128]{2,1,0:T(8,128)S(1)}, f32[2,256,128]{2,1,0:T(8,128)S(1)}, u32[]{:S(2)}, u32[]{:S(2)}) collective-permute-start(f32[2,256,128]{2,1,0:T(8,128)S(1)} %get-tuple-element.90), channel_id=1, source_target_pairs={{0,8},{1,2},{2,1},{3,11},{4,12},{5,6},{6,5},{7,15},{8,0},{9,10},{1... | collective-permute-start | bytes 786440 | tf_op jit(solution)/shard_map/ppermute | solution.py:109
  30.6 3.2 %collective-permute-start.13 = (f32[1,128]{1,0:T(1,128)S(1)}, f32[1,128]{1,0:T(1,128)S(1)}, u32[]{:S(2)}, u32[]{:S(2)}) collective-permute-start(f32[1,128]{1,0:T(1,128)S(1)} %add.18), channel_id=1, source_target_pairs={{0,16},{4,20},{8,24},{12,28},{16,0},{20,4},{24,8},{28,12},{1,17},{... | collective-permute-start | bytes 1544 | tf_op jit(solution)/shard_map/ppermute | solution.py:452
  35.2 1.8 %collective-permute-start.11 = (f32[2,128,128]{2,1,0:T(8,128)S(1)}, f32[2,128,128]{2,1,0:T(8,128)S(1)}, u32[]{:S(2)}, u32[]{:S(2)}) collective-permute-start(f32[2,128,128]{2,1,0:T(8,128)S(1)} %get-tuple-element.92), channel_id=1, source_target_pairs={{0,4},{1,5},{2,6},{3,7},{4,0},{5,1},{6,2},{7,3},{8,12},{9,13},{10,... | collective-permute-start | bytes 393224 | tf_op jit(solution)/shard_map/ppermute | solution.py:109
  37.0 4.2 %shard_map.108.denom = f32[128,128]{1,0:T(8,128)S(1)} custom-call(s32[128]{0:T(128)S(1)} %convert_bitcast_fusion.sc, f32[4,256,256]{2,1,0:T(8,128)S(1)} %get-tuple-element.84.pr.refs_6_, f32[4,256,256]{2,1,0:T(8,128)S(1)} %get-tuple-element.85.pi.refs_7_), custom_call_target="tpu_custom_call" | custom-call | flops 16777216 | bytes 10000000 | tf_op jit(solution)/shard_map/pallas_call | solution.py:134
  41.9 2.8 %collective-permute-start.14 = (f32[2,128,128]{2,1,0:T(8,128)S(1)}, f32[2,128,128]{2,1,0:T(8,128)S(1)}, u32[]{:S(2)}, u32[]{:S(2)}) collective-permute-start(f32[2,128,128]{2,1,0:T(8,128)S(1)} %shard_map.109.s), channel_id=1, source_target_pairs={{0,4},{1,5},{2,6},{3,7},{4,0},{5,1},{6,2},{7,3},{8,12},{9,13},{10,... | collective-permute-start | bytes 393224 | tf_op jit(solution)/shard_map/ppermute | solution.py:109
  44.7 2.9 %collective-permute-done.14.near = f32[2,128,128]{2,1,0:T(8,128)S(1)} collective-permute-done((f32[2,128,128]{2,1,0:T(8,128)S(1)}, f32[2,128,128]{2,1,0:T(8,128)S(1)}, u32[]{:S(2)}, u32[]{:S(2)}) %collective-permute-start.14) | collective-permute-done | bytes 131104 | tf_op jit(solution)/shard_map/ppermute | solution.py:109
  47.9 2.8 %collective-permute-start.17 = (f32[2,256,128]{2,1,0:T(8,128)S(1)}, f32[2,256,128]{2,1,0:T(8,128)S(1)}, u32[]{:S(2)}, u32[]{:S(2)}) collective-permute-start(f32[2,256,128]{2,1,0:T(8,128)S(1)} %get-tuple-element.97), channel_id=1, source_target_pairs={{0,8},{1,2},{2,1},{3,11},{4,12},{5,6},{6,5},{7,15},{8,0},{9,10},{1... | collective-permute-start | bytes 786440 | tf_op jit(solution)/shard_map/ppermute | solution.py:109
  50.7 4.3 %collective-permute-done.17.far = f32[2,256,128]{2,1,0:T(8,128)S(1)} collective-permute-done((f32[2,256,128]{2,1,0:T(8,128)S(1)}, f32[2,256,128]{2,1,0:T(8,128)S(1)}, u32[]{:S(2)}, u32[]{:S(2)}) %collective-permute-start.17) | collective-permute-done | bytes 262176 | tf_op jit(solution)/shard_map/ppermute | solution.py:109
  55.1 2.8 %shard_map.111 = (f32[2,256,128]{2,1,0:T(8,128)S(1)}, f32[2,256,128]{2,1,0:T(8,128)S(1)}, f32[2,256,128]{2,1,0:T(8,128)S(1)}) custom-call(f32[1,128]{1,0:T(1,128)S(1)} %add.17.sc, f32[2,256,128]{2,1,0:T(8,128)S(1)} %get-tuple-element.95.mid, f32[2,256,128]{2,1,0:T(8,128)S(1)} %collective-permute-done.16.near, ...), custom_call_target="tpu_custom_call" | custom-call | tf_op jit(solution)/shard_map/pallas_call | solution.py:134
  57.9 2.1 %collective-permute-start.19 = (f32[2,256,128]{2,1,0:T(8,128)S(1)}, f32[2,256,128]{2,1,0:T(8,128)S(1)}, u32[]{:S(2)}, u32[]{:S(2)}) collective-permute-start(f32[2,256,128]{2,1,0:T(8,128)S(1)} %get-tuple-element.100), channel_id=1, source_target_pairs={{0,8},{1,2},{2,1},{3,11},{4,12},{5,6},{6,5},{7,15},{8,0},{9,10},{1... | collective-permute-start | bytes 786440 | tf_op jit(solution)/shard_map/ppermute | solution.py:109
  60.1 4.3 %collective-permute-done.19.far = f32[2,256,128]{2,1,0:T(8,128)S(1)} collective-permute-done((f32[2,256,128]{2,1,0:T(8,128)S(1)}, f32[2,256,128]{2,1,0:T(8,128)S(1)}, u32[]{:S(2)}, u32[]{:S(2)}) %collective-permute-start.19) | collective-permute-done | bytes 262176 | tf_op jit(solution)/shard_map/ppermute | solution.py:109
  66.0 4.2 %collective-permute-done.20.near = f32[2,128,128]{2,1,0:T(8,128)S(1)} collective-permute-done((f32[2,128,128]{2,1,0:T(8,128)S(1)}, f32[2,128,128]{2,1,0:T(8,128)S(1)}, u32[]{:S(2)}, u32[]{:S(2)}) %collective-permute-start.20) | collective-permute-done | bytes 131104 | tf_op jit(solution)/shard_map/ppermute | solution.py:109
  70.4 3.8 %collective-permute-start.22 = (f32[2,128,128]{2,1,0:T(8,128)S(1)}, f32[2,128,128]{2,1,0:T(8,128)S(1)}, u32[]{:S(2)}, u32[]{:S(2)}) collective-permute-start(f32[2,128,128]{2,1,0:T(8,128)S(1)} %shard_map.113.s), channel_id=1, source_target_pairs={{0,4},{1,5},{2,6},{3,7},{4,0},{5,1},{6,2},{7,3},{8,12},{9,13},{10,... | collective-permute-start | bytes 393224 | tf_op jit(solution)/shard_map/ppermute | solution.py:109
  74.1 2.9 %collective-permute-done.22.near = f32[2,128,128]{2,1,0:T(8,128)S(1)} collective-permute-done((f32[2,128,128]{2,1,0:T(8,128)S(1)}, f32[2,128,128]{2,1,0:T(8,128)S(1)}, u32[]{:S(2)}, u32[]{:S(2)}) %collective-permute-start.22) | collective-permute-done | bytes 131104 | tf_op jit(solution)/shard_map/ppermute | solution.py:109
  77.3 3.0 %collective-permute-start.25 = (f32[2,256,128]{2,1,0:T(8,128)S(1)}, f32[2,256,128]{2,1,0:T(8,128)S(1)}, u32[]{:S(2)}, u32[]{:S(2)}) collective-permute-start(f32[2,256,128]{2,1,0:T(8,128)S(1)} %get-tuple-element.106), channel_id=1, source_target_pairs={{0,8},{1,2},{2,1},{3,11},{4,12},{5,6},{6,5},{7,15},{8,0},{9,10},{1... | collective-permute-start | bytes 786440 | tf_op jit(solution)/shard_map/ppermute | solution.py:109
  80.4 4.3 %collective-permute-done.25.far = f32[2,256,128]{2,1,0:T(8,128)S(1)} collective-permute-done((f32[2,256,128]{2,1,0:T(8,128)S(1)}, f32[2,256,128]{2,1,0:T(8,128)S(1)}, u32[]{:S(2)}, u32[]{:S(2)}) %collective-permute-start.25) | collective-permute-done | bytes 262176 | tf_op jit(solution)/shard_map/ppermute | solution.py:109
  84.7 3.5 %shard_map.115 = (f32[2,256,128]{2,1,0:T(8,128)S(1)}, f32[2,256,128]{2,1,0:T(8,128)S(1)}, f32[2,256,128]{2,1,0:T(8,128)S(1)}, f32[3,128,256]{2,1,0:T(8,128)S(1)}...) custom-call(f32[1,128]{1,0:T(1,128)S(1)} %add.17.sc, ...), custom_call_target="tpu_custom_call" | custom-call | tf_op jit(solution)/shard_map/pallas_call | solution.py:134
  89.3 2.0 %collective-permute-start.29 = (f32[2,256,128]{2,1,0:T(8,128)S(1)}, f32[2,256,128]{2,1,0:T(8,128)S(1)}, u32[]{:S(2)}, u32[]{:S(2)}) collective-permute-start(f32[2,256,128]{2,1,0:T(8,128)S(1)} %get-tuple-element.112), channel_id=1, source_target_pairs={{0,8},{1,2},{2,1},{3,11},{4,12},{5,6},{6,5},{7,15},{8,0},{9,10},{1... | collective-permute-start | bytes 786440 | tf_op jit(solution)/shard_map/ppermute | solution.py:109
  93.5 3.6 %collective-permute-done.29.far = f32[2,256,128]{2,1,0:T(8,128)S(1)} collective-permute-done((f32[2,256,128]{2,1,0:T(8,128)S(1)}, f32[2,256,128]{2,1,0:T(8,128)S(1)}, u32[]{:S(2)}, u32[]{:S(2)}) %collective-permute-start.29) | collective-permute-done | bytes 262176 | tf_op jit(solution)/shard_map/ppermute | solution.py:109
  99.6 2.1 %collective-permute-start.44 = (f32[3,32,256]{2,1,0:T(8,128)S(1)}, f32[3,32,256]{2,1,0:T(8,128)S(1)}, u32[]{:S(2)}, u32[]{:S(2)}) collective-permute-start(f32[3,32,256]{2,1,0:T(8,128)S(1)} %get-tuple-element.141), channel_id=1, source_target_pairs={{0,8},{4,12},{8,0},{12,4},{16,24},{20,28},{24,16},{28,20},{1,9},{5... | collective-permute-start | bytes 294920 | tf_op jit(solution)/shard_map/ppermute | solution.py:452
  103.9 2.1 %collective-permute-start.31 = (f32[3,16,256]{2,1,0:T(8,128)S(1)}, f32[3,16,256]{2,1,0:T(8,128)S(1)}, u32[]{:S(2)}, u32[]{:S(2)}) collective-permute-start(f32[3,16,256]{2,1,0:T(8,128)S(1)} %get-tuple-element.117), channel_id=1, source_target_pairs={{0,8},{4,12},{8,0},{12,4},{16,24},{20,28},{24,16},{28,20},{1,9},{5... | collective-permute-start | bytes 147464 | tf_op jit(solution)/shard_map/ppermute | solution.py:452
  107.5 1.8 %collective-permute-start.50 = (f32[3,16,256]{2,1,0:T(8,128)S(1)}, f32[3,16,256]{2,1,0:T(8,128)S(1)}, u32[]{:S(2)}, u32[]{:S(2)}) collective-permute-start(f32[3,16,256]{2,1,0:T(8,128)S(1)} %get-tuple-element.147), channel_id=1, source_target_pairs={{0,2},{1,3},{2,0},{3,1},{4,6},{5,7},{6,4},{7,5},{8,10},{9,11},{10,... | collective-permute-start | bytes 147464 | tf_op jit(solution)/shard_map/ppermute | solution.py:452
  110.3 2.2 %collective-permute-start.46 = (f32[3,16,256]{2,1,0:T(8,128)S(1)}, f32[3,16,256]{2,1,0:T(8,128)S(1)}, u32[]{:S(2)}, u32[]{:S(2)}) collective-permute-start(f32[3,16,256]{2,1,0:T(8,128)S(1)} %shard_map.132.cur), channel_id=1, source_target_pairs={{0,16},{4,20},{8,24},{12,28},{16,0},{20,4},{24,8},{28,12},{1,17},{... | collective-permute-start | bytes 147464 | tf_op jit(solution)/shard_map/ppermute | solution.py:452
  113.3 2.1 %collective-permute-done.32.got = f32[3,16,256]{2,1,0:T(8,128)S(1)} collective-permute-done((f32[3,16,256]{2,1,0:T(8,128)S(1)}, f32[3,16,256]{2,1,0:T(8,128)S(1)}, u32[]{:S(2)}, u32[]{:S(2)}) %collective-permute-start.32) | collective-permute-done | bytes 49184 | tf_op jit(solution)/shard_map/ppermute | solution.py:452
  122.1 2.1 %collective-permute-start.53 = (f32[3,32,256]{2,1,0:T(8,128)S(1)}, f32[3,32,256]{2,1,0:T(8,128)S(1)}, u32[]{:S(2)}, u32[]{:S(2)}) collective-permute-start(f32[3,32,256]{2,1,0:T(8,128)S(1)} %shard_map.140.cur), channel_id=1, source_target_pairs={{0,4},{4,0},{8,12},{12,8},{16,20},{20,16},{24,28},{28,24},{1,5},{5... | collective-permute-start | bytes 294920 | tf_op jit(solution)/shard_map/ppermute | solution.py:452
  129.0 1.9 %collective-permute-done.41.got = f32[3,64,256]{2,1,0:T(8,128)S(1)} collective-permute-done((f32[3,64,256]{2,1,0:T(8,128)S(1)}, f32[3,64,256]{2,1,0:T(8,128)S(1)}, u32[]{:S(2)}, u32[]{:S(2)}) %collective-permute-start.41) | collective-permute-done | bytes 196640 | tf_op jit(solution)/shard_map/ppermute | solution.py:452
  131.7 1.9 %collective-permute-done.54.got = f32[3,64,256]{2,1,0:T(8,128)S(1)} collective-permute-done((f32[3,64,256]{2,1,0:T(8,128)S(1)}, f32[3,64,256]{2,1,0:T(8,128)S(1)}, u32[]{:S(2)}, u32[]{:S(2)}) %collective-permute-start.54) | collective-permute-done | bytes 196640 | tf_op jit(solution)/shard_map/ppermute | solution.py:452
  135.4 1.9 %shard_map.143 = (f32[4,256,256]{2,1,0:T(8,128)}, f32[4,256,256]{2,1,0:T(8,128)}) custom-call(f32[3,128,256]{2,1,0:T(8,128)S(1)} %shard_map.128.refs_0_, f32[3,128,256]{2,1,0:T(8,128)S(1)} %shard_map.136.refs_1_, f32[3,128,256]{2,1,0:T(8,128)S(1)} %shard_map.142.refs_2_, f32[3,128,256]{2,1,0:T(8,128)S(1)} %collective-permute-done.55.refs_3_, ...), custom_call_target="tpu_custom_call" | custom-call | tf_op jit(solution)/shard_map/pallas_call | solution.py:134
  (136 shorter events, 41.5 us)
Async XLA Ops:
  1.6 14.3 %collective-permute-start.1 = (f32[2,128,128]{2,1,0:T(8,128)S(1)}, f32[2,128,128]{2,1,0:T(8,128)S(1)}, u32[]{:S(2)}, u32[]{:S(2)}) collective-permute-start(f32[2,128,128]{2,1,0:T(8,128)S(1)} %pad_maximum_fusion.s), channel_id=1, source_target_pairs={{0,1},{1,0},{2,3},{3,2},{4,12},{5,13},{6,14},{7,15},{8,4},{9,5},{1... | collective-permute-start | bytes 393224 | tf_op jit(solution)/shard_map/ppermute | solution.py:109
  2.1 13.7 %collective-permute-start = (f32[2,128,128]{2,1,0:T(8,128)S(1)}, f32[2,128,128]{2,1,0:T(8,128)S(1)}, u32[]{:S(2)}, u32[]{:S(2)}) collective-permute-start(f32[2,128,128]{2,1,0:T(8,128)S(1)} %pad_maximum_fusion.s), channel_id=1, source_target_pairs={{0,4},{1,5},{2,6},{3,7},{4,0},{5,1},{6,2},{7,3},{8,12},{9,13},{10,... | collective-permute-start | bytes 393224 | tf_op jit(solution)/shard_map/ppermute | solution.py:109
  15.9 7.9 %collective-permute-start.6 = (f32[2,384,128]{2,1,0:T(8,128)S(1)}, f32[2,384,128]{2,1,0:T(8,128)S(1)}, u32[]{:S(2)}, u32[]{:S(2)}) collective-permute-start(f32[2,384,128]{2,1,0:T(8,128)S(1)} %get-tuple-element.81.mid), channel_id=1, source_target_pairs={{0,8},{1,2},{2,1},{3,11},{4,12},{5,6},{6,5},{7,15},{8,0},{9,10},{1... | collective-permute-start | bytes 1179656 | tf_op jit(solution)/shard_map/ppermute | solution.py:109
  16.8 7.1 %collective-permute-start.5 = (f32[2,384,128]{2,1,0:T(8,128)S(1)}, f32[2,384,128]{2,1,0:T(8,128)S(1)}, u32[]{:S(2)}, u32[]{:S(2)}) collective-permute-start(f32[2,384,128]{2,1,0:T(8,128)S(1)} %get-tuple-element.81.mid), channel_id=1, source_target_pairs={{0,1},{1,0},{2,3},{3,2},{4,5},{5,4},{6,7},{7,6},{8,9},{9,8},{10,11... | collective-permute-start | bytes 1179656 | tf_op jit(solution)/shard_map/ppermute | solution.py:109
  17.6 6.3 %collective-permute-start.8 = (f32[256,256]{1,0:T(8,128)S(1)}, f32[256,256]{1,0:T(8,128)S(1)}, u32[]{:S(2)}, u32[]{:S(2)}) collective-permute-start(f32[256,256]{1,0:T(8,128)S(1)} %shard_map.103.view), channel_id=1, source_target_pairs={{0,1},{1,0},{2,3},{3,2},{4,5},{5,4},{6,7},{7,6},{8,12},{9,13},{10,... | collective-permute-start | bytes 786440 | tf_op jit(solution)/shard_map/ppermute | solution.py:109
  17.6 6.2 %collective-permute-start.7 = (f32[1,128]{1,0:T(1,128)S(1)}, f32[1,128]{1,0:T(1,128)S(1)}, u32[]{:S(2)}, u32[]{:S(2)}) collective-permute-start(f32[1,128]{1,0:T(1,128)S(1)} %add.17.sc), channel_id=1, source_target_pairs={{0,8},{4,12},{8,0},{12,4},{16,24},{20,28},{24,16},{28,20},{1,9},{5... | collective-permute-start | bytes 1544 | tf_op jit(solution)/shard_map/ppermute | solution.py:452
  26.8 7.0 %collective-permute-start.9 = (f32[2,256,128]{2,1,0:T(8,128)S(1)}, f32[2,256,128]{2,1,0:T(8,128)S(1)}, u32[]{:S(2)}, u32[]{:S(2)}) collective-permute-start(f32[2,256,128]{2,1,0:T(8,128)S(1)} %get-tuple-element.89), channel_id=1, source_target_pairs={{0,1},{1,0},{2,3},{3,2},{4,5},{5,4},{6,7},{7,6},{8,9},{9,8},{10,11... | collective-permute-start | bytes 786440 | tf_op jit(solution)/shard_map/ppermute | solution.py:109
  26.9 8.1 %collective-permute-start.10 = (f32[2,256,128]{2,1,0:T(8,128)S(1)}, f32[2,256,128]{2,1,0:T(8,128)S(1)}, u32[]{:S(2)}, u32[]{:S(2)}) collective-permute-start(f32[2,256,128]{2,1,0:T(8,128)S(1)} %get-tuple-element.90), channel_id=1, source_target_pairs={{0,8},{1,2},{2,1},{3,11},{4,12},{5,6},{6,5},{7,15},{8,0},{9,10},{1... | collective-permute-start | bytes 786440 | tf_op jit(solution)/shard_map/ppermute | solution.py:109
  30.6 6.4 %collective-permute-start.13 = (f32[1,128]{1,0:T(1,128)S(1)}, f32[1,128]{1,0:T(1,128)S(1)}, u32[]{:S(2)}, u32[]{:S(2)}) collective-permute-start(f32[1,128]{1,0:T(1,128)S(1)} %add.18), channel_id=1, source_target_pairs={{0,16},{4,20},{8,24},{12,28},{16,0},{20,4},{24,8},{28,12},{1,17},{... | collective-permute-start | bytes 1544 | tf_op jit(solution)/shard_map/ppermute | solution.py:452
  35.2 6.1 %collective-permute-start.11 = (f32[2,128,128]{2,1,0:T(8,128)S(1)}, f32[2,128,128]{2,1,0:T(8,128)S(1)}, u32[]{:S(2)}, u32[]{:S(2)}) collective-permute-start(f32[2,128,128]{2,1,0:T(8,128)S(1)} %get-tuple-element.92), channel_id=1, source_target_pairs={{0,4},{1,5},{2,6},{3,7},{4,0},{5,1},{6,2},{7,3},{8,12},{9,13},{10,... | collective-permute-start | bytes 393224 | tf_op jit(solution)/shard_map/ppermute | solution.py:109
  41.9 5.8 %collective-permute-start.14 = (f32[2,128,128]{2,1,0:T(8,128)S(1)}, f32[2,128,128]{2,1,0:T(8,128)S(1)}, u32[]{:S(2)}, u32[]{:S(2)}) collective-permute-start(f32[2,128,128]{2,1,0:T(8,128)S(1)} %shard_map.109.s), channel_id=1, source_target_pairs={{0,4},{1,5},{2,6},{3,7},{4,0},{5,1},{6,2},{7,3},{8,12},{9,13},{10,... | collective-permute-start | bytes 393224 | tf_op jit(solution)/shard_map/ppermute | solution.py:109
  47.9 7.1 %collective-permute-start.17 = (f32[2,256,128]{2,1,0:T(8,128)S(1)}, f32[2,256,128]{2,1,0:T(8,128)S(1)}, u32[]{:S(2)}, u32[]{:S(2)}) collective-permute-start(f32[2,256,128]{2,1,0:T(8,128)S(1)} %get-tuple-element.97), channel_id=1, source_target_pairs={{0,8},{1,2},{2,1},{3,11},{4,12},{5,6},{6,5},{7,15},{8,0},{9,10},{1... | collective-permute-start | bytes 786440 | tf_op jit(solution)/shard_map/ppermute | solution.py:109
  57.9 6.5 %collective-permute-start.19 = (f32[2,256,128]{2,1,0:T(8,128)S(1)}, f32[2,256,128]{2,1,0:T(8,128)S(1)}, u32[]{:S(2)}, u32[]{:S(2)}) collective-permute-start(f32[2,256,128]{2,1,0:T(8,128)S(1)} %get-tuple-element.100), channel_id=1, source_target_pairs={{0,8},{1,2},{2,1},{3,11},{4,12},{5,6},{6,5},{7,15},{8,0},{9,10},{1... | collective-permute-start | bytes 786440 | tf_op jit(solution)/shard_map/ppermute | solution.py:109
  64.6 5.6 %collective-permute-start.20 = (f32[2,128,128]{2,1,0:T(8,128)S(1)}, f32[2,128,128]{2,1,0:T(8,128)S(1)}, u32[]{:S(2)}, u32[]{:S(2)}) collective-permute-start(f32[2,128,128]{2,1,0:T(8,128)S(1)} %get-tuple-element.102), channel_id=1, source_target_pairs={{0,4},{1,5},{2,6},{3,7},{4,0},{5,1},{6,2},{7,3},{8,12},{9,13},{10,... | collective-permute-start | bytes 393224 | tf_op jit(solution)/shard_map/ppermute | solution.py:109
  70.4 6.7 %collective-permute-start.22 = (f32[2,128,128]{2,1,0:T(8,128)S(1)}, f32[2,128,128]{2,1,0:T(8,128)S(1)}, u32[]{:S(2)}, u32[]{:S(2)}) collective-permute-start(f32[2,128,128]{2,1,0:T(8,128)S(1)} %shard_map.113.s), channel_id=1, source_target_pairs={{0,4},{1,5},{2,6},{3,7},{4,0},{5,1},{6,2},{7,3},{8,12},{9,13},{10,... | collective-permute-start | bytes 393224 | tf_op jit(solution)/shard_map/ppermute | solution.py:109
  77.3 7.4 %collective-permute-start.25 = (f32[2,256,128]{2,1,0:T(8,128)S(1)}, f32[2,256,128]{2,1,0:T(8,128)S(1)}, u32[]{:S(2)}, u32[]{:S(2)}) collective-permute-start(f32[2,256,128]{2,1,0:T(8,128)S(1)} %get-tuple-element.106), channel_id=1, source_target_pairs={{0,8},{1,2},{2,1},{3,11},{4,12},{5,6},{6,5},{7,15},{8,0},{9,10},{1... | collective-permute-start | bytes 786440 | tf_op jit(solution)/shard_map/ppermute | solution.py:109
  89.3 7.8 %collective-permute-start.29 = (f32[2,256,128]{2,1,0:T(8,128)S(1)}, f32[2,256,128]{2,1,0:T(8,128)S(1)}, u32[]{:S(2)}, u32[]{:S(2)}) collective-permute-start(f32[2,256,128]{2,1,0:T(8,128)S(1)} %get-tuple-element.112), channel_id=1, source_target_pairs={{0,8},{1,2},{2,1},{3,11},{4,12},{5,6},{6,5},{7,15},{8,0},{9,10},{1... | collective-permute-start | bytes 786440 | tf_op jit(solution)/shard_map/ppermute | solution.py:109
  91.4 5.7 %collective-permute-start.27 = (f32[3,64,256]{2,1,0:T(8,128)S(1)}, f32[3,64,256]{2,1,0:T(8,128)S(1)}, u32[]{:S(2)}, u32[]{:S(2)}) collective-permute-start(f32[3,64,256]{2,1,0:T(8,128)S(1)} %get-tuple-element.110), channel_id=1, source_target_pairs={{0,4},{4,0},{8,12},{12,8},{16,20},{20,16},{24,28},{28,24},{1,5},{5... | collective-permute-start | bytes 589832 | tf_op jit(solution)/shard_map/ppermute | solution.py:452
  91.6 8.0 %collective-permute-start.43 = (f32[3,64,256]{2,1,0:T(8,128)S(1)}, f32[3,64,256]{2,1,0:T(8,128)S(1)}, u32[]{:S(2)}, u32[]{:S(2)}) collective-permute-start(f32[3,64,256]{2,1,0:T(8,128)S(1)} %get-tuple-element.139), channel_id=1, source_target_pairs={{0,2},{1,3},{2,0},{3,1},{4,6},{5,7},{6,4},{7,5},{8,10},{9,11},{10,... | collective-permute-start | bytes 589832 | tf_op jit(solution)/shard_map/ppermute | solution.py:452
  92.4 9.3 %collective-permute-start.36 = (f32[3,64,256]{2,1,0:T(8,128)S(1)}, f32[3,64,256]{2,1,0:T(8,128)S(1)}, u32[]{:S(2)}, u32[]{:S(2)}) collective-permute-start(f32[3,64,256]{2,1,0:T(8,128)S(1)} %get-tuple-element.125), channel_id=1, source_target_pairs={{0,8},{4,12},{8,0},{12,4},{16,24},{20,28},{24,16},{28,20},{1,9},{5... | collective-permute-start | bytes 589832 | tf_op jit(solution)/shard_map/ppermute | solution.py:452
  97.4 10.1 %collective-permute-start.38 = (f32[2,128,128]{2,1,0:T(8,128)S(1)}, f32[2,128,128]{2,1,0:T(8,128)S(1)}, u32[]{:S(2)}, u32[]{:S(2)}) collective-permute-start(f32[2,128,128]{2,1,0:T(8,128)S(1)} %get-tuple-element.127), channel_id=1, source_target_pairs={{0,4},{1,5},{2,6},{3,7},{4,0},{5,1},{6,2},{7,3},{8,12},{9,13},{10,... | collective-permute-start | bytes 393224 | tf_op jit(solution)/shard_map/ppermute | solution.py:109
  98.6 8.9 %collective-permute-start.39 = (f32[2,128,128]{2,1,0:T(8,128)S(1)}, f32[2,128,128]{2,1,0:T(8,128)S(1)}, u32[]{:S(2)}, u32[]{:S(2)}) collective-permute-start(f32[2,128,128]{2,1,0:T(8,128)S(1)} %get-tuple-element.128), channel_id=1, source_target_pairs={{0,1},{1,0},{2,3},{3,2},{4,12},{5,13},{6,14},{7,15},{8,16},{9,17},... | collective-permute-start | bytes 393224 | tf_op jit(solution)/shard_map/ppermute | solution.py:109
  99.6 6.3 %collective-permute-start.44 = (f32[3,32,256]{2,1,0:T(8,128)S(1)}, f32[3,32,256]{2,1,0:T(8,128)S(1)}, u32[]{:S(2)}, u32[]{:S(2)}) collective-permute-start(f32[3,32,256]{2,1,0:T(8,128)S(1)} %get-tuple-element.141), channel_id=1, source_target_pairs={{0,8},{4,12},{8,0},{12,4},{16,24},{20,28},{24,16},{28,20},{1,9},{5... | collective-permute-start | bytes 294920 | tf_op jit(solution)/shard_map/ppermute | solution.py:452
  101.8 5.7 %collective-permute-start.37 = (f32[3,32,256]{2,1,0:T(8,128)S(1)}, f32[3,32,256]{2,1,0:T(8,128)S(1)}, u32[]{:S(2)}, u32[]{:S(2)}) collective-permute-start(f32[3,32,256]{2,1,0:T(8,128)S(1)} %get-tuple-element.126), channel_id=1, source_target_pairs={{0,4},{4,0},{8,12},{12,8},{16,20},{20,16},{24,28},{28,24},{1,5},{5... | collective-permute-start | bytes 294920 | tf_op jit(solution)/shard_map/ppermute | solution.py:452
  103.9 5.5 %collective-permute-start.31 = (f32[3,16,256]{2,1,0:T(8,128)S(1)}, f32[3,16,256]{2,1,0:T(8,128)S(1)}, u32[]{:S(2)}, u32[]{:S(2)}) collective-permute-start(f32[3,16,256]{2,1,0:T(8,128)S(1)} %get-tuple-element.117), channel_id=1, source_target_pairs={{0,8},{4,12},{8,0},{12,4},{16,24},{20,28},{24,16},{28,20},{1,9},{5... | collective-permute-start | bytes 147464 | tf_op jit(solution)/shard_map/ppermute | solution.py:452
  109.3 6.1 %collective-permute-start.32 = (f32[3,16,256]{2,1,0:T(8,128)S(1)}, f32[3,16,256]{2,1,0:T(8,128)S(1)}, u32[]{:S(2)}, u32[]{:S(2)}) collective-permute-start(f32[3,16,256]{2,1,0:T(8,128)S(1)} %shard_map.119.cur), channel_id=1, source_target_pairs={{0,16},{4,20},{8,24},{12,28},{16,0},{20,4},{24,8},{28,12},{1,17},{... | collective-permute-start | bytes 147464 | tf_op jit(solution)/shard_map/ppermute | solution.py:452
  110.3 6.2 %collective-permute-start.46 = (f32[3,16,256]{2,1,0:T(8,128)S(1)}, f32[3,16,256]{2,1,0:T(8,128)S(1)}, u32[]{:S(2)}, u32[]{:S(2)}) collective-permute-start(f32[3,16,256]{2,1,0:T(8,128)S(1)} %shard_map.132.cur), channel_id=1, source_target_pairs={{0,16},{4,20},{8,24},{12,28},{16,0},{20,4},{24,8},{28,12},{1,17},{... | collective-permute-start | bytes 147464 | tf_op jit(solution)/shard_map/ppermute | solution.py:452
  118.6 5.5 %collective-permute-start.40 = (f32[2,128,128]{2,1,0:T(8,128)S(1)}, f32[2,128,128]{2,1,0:T(8,128)S(1)}, u32[]{:S(2)}, u32[]{:S(2)}) collective-permute-start(f32[2,128,128]{2,1,0:T(8,128)S(1)} %shard_map.125.state), channel_id=1, source_target_pairs={{0,1},{1,0},{2,3},{3,2},{4,5},{5,4},{6,7},{7,6},{8,12},{9,13},{10,... | collective-permute-start | bytes 393224 | tf_op jit(solution)/shard_map/ppermute | solution.py:109
  122.1 5.7 %collective-permute-start.53 = (f32[3,32,256]{2,1,0:T(8,128)S(1)}, f32[3,32,256]{2,1,0:T(8,128)S(1)}, u32[]{:S(2)}, u32[]{:S(2)}) collective-permute-start(f32[3,32,256]{2,1,0:T(8,128)S(1)} %shard_map.140.cur), channel_id=1, source_target_pairs={{0,4},{4,0},{8,12},{12,8},{16,20},{20,16},{24,28},{28,24},{1,5},{5... | collective-permute-start | bytes 294920 | tf_op jit(solution)/shard_map/ppermute | solution.py:452
  124.3 6.6 %collective-permute-start.41 = (f32[3,64,256]{2,1,0:T(8,128)S(1)}, f32[3,64,256]{2,1,0:T(8,128)S(1)}, u32[]{:S(2)}, u32[]{:S(2)}) collective-permute-start(f32[3,64,256]{2,1,0:T(8,128)S(1)} %shard_map.127.cur), channel_id=1, source_target_pairs={{0,4},{4,0},{8,12},{12,8},{16,20},{20,16},{24,28},{28,24},{1,5},{5... | collective-permute-start | bytes 589832 | tf_op jit(solution)/shard_map/ppermute | solution.py:452
  125.8 5.7 %collective-permute-start.49 = (f32[3,64,256]{2,1,0:T(8,128)S(1)}, f32[3,64,256]{2,1,0:T(8,128)S(1)}, u32[]{:S(2)}, u32[]{:S(2)}) collective-permute-start(f32[3,64,256]{2,1,0:T(8,128)S(1)} %shard_map.135.cur), channel_id=1, source_target_pairs={{0,2},{1,3},{2,0},{3,1},{4,6},{5,7},{6,4},{7,5},{8,10},{9,11},{10,... | collective-permute-start | bytes 589832 | tf_op jit(solution)/shard_map/ppermute | solution.py:452
  127.8 5.7 %collective-permute-start.54 = (f32[3,64,256]{2,1,0:T(8,128)S(1)}, f32[3,64,256]{2,1,0:T(8,128)S(1)}, u32[]{:S(2)}, u32[]{:S(2)}) collective-permute-start(f32[3,64,256]{2,1,0:T(8,128)S(1)} %shard_map.141.cur), channel_id=1, source_target_pairs={{0,8},{4,12},{8,0},{12,4},{16,24},{20,28},{24,16},{28,20},{1,9},{5... | collective-permute-start | bytes 589832 | tf_op jit(solution)/shard_map/ppermute | solution.py:452
  (28 other events, 115.3 us)

commit v7 on v6

--- a/solution.py
+++ b/solution.py
@@ -270,13 +270,21 @@
 
 def view_body(sizes, last, sc, mid, near, far, pr, pi, view, traded, tabs, *refs):
     if last:
-        gm, to_near, to_far, *parts, spec_scr, win_scr, wave_e, wave_o, mix_e, mix_o, term_scr = refs
+        gm, to_near, to_far, *parts, spec_scr, win_scr, wave_e, wave_o, mix_e, mix_o = refs
     else:
         gm, to_near, to_far, spec_scr, win_scr, wave_e, wave_o, mix_e, mix_o = refs
     _, _, _, _, rim = sizes
     at = Place(sc, sizes)
     modes, width = pr.shape[0], pr.shape[1]
     half = rim // 2
+    upper = at.j % 2 == 1
+
+    def put(k, term):
+        each = parts[0].shape[0]
+        top, low = term[:rim], term[rim:]
+        parts[2 * (k // each)][k % each] = jnp.where(upper, low, top)
+        parts[2 * (k // each) + 1][k % each] = jnp.where(upper, top, low)
+
     lane = lax.broadcasted_iota(jnp.int32, (width, rim), 1)
     first = at.col == 0
     middle = at.col == half
@@ -353,8 +361,8 @@
         grad[1] = grad[1] + (pr[m] * ei - pi[m] * er)
         if last:
             wr, wi = win_scr[0], win_scr[1]
-            term_scr[m] = wr * er + wi * ei
-            term_scr[modes + m] = wr * ei - wi * er
+            put(m, wr * er + wi * ei)
+            put(modes + m, wr * ei - wi * er)
     for part in range(2):
         a, b = grad[part][:, :rim], grad[part][:, rim:]
         ra, rb = pltpu.roll(a, half, 1), pltpu.roll(b, half, 1)
@@ -367,13 +375,7 @@
         to_far[part] = jnp.where(at.even_col, lft, rgt)
     if last:
         wr, wi = win_scr[0], win_scr[1]
-        term_scr[2 * modes] = wr * wr + wi * wi
-        bit = at.j % 2
-        each = parts[0].shape[0]
-        for k, part in enumerate(parts):
-            at = slice((k // 2) * each, (k // 2 + 1) * each)
-            offset = (1 - bit if k % 2 else bit) * rim
-            part[...] = term_scr[at, pl.ds(pl.multiple_of(offset, rim), rim)]
+        put(2 * modes, wr * wr + wi * wi)
 
 
 def fold_body(sizes, sc, gm, near, far, own, to_near, to_far, buf):
@@ -425,9 +427,9 @@
 
 
 def probe_body(rim, *refs):
-    colors = (len(refs) - 4) // 2
-    mine, got = refs[:colors], refs[colors : 2 * colors]
-    pr, pi, new_re, new_im = refs[2 * colors :]
+    *parts, pr, pi, new_re, new_im, held, sem = refs
+    colors = len(parts) // 2
+    mine, got = parts[:colors], parts[colors:]
     modes = pr.shape[0]
     each = mine[0].shape[0]
     pixels = 4 * rim * rim
@@ -437,12 +439,34 @@
         return src[k // each][k % each]
 
     mean = (jnp.sum(term(mine, 2 * modes)) + jnp.sum(term(got, 2 * modes))) / pixels
+    places = []
     for src, offset in ((mine, bit * rim), (got, (1 - bit) * rim)):
-        rows = pl.ds(pl.multiple_of(offset, rim), rim)
         scale = probe_step / (term(src, 2 * modes) + mass_ratio * mean)
+        places.append((src, pl.ds(pl.multiple_of(offset, rim), rim), scale))
+    copies = []
+    for k, (old, out) in enumerate(((pr, new_re), (pi, new_im))):
         for m in range(modes):
-            new_re[m, rows] = pr[m, rows] + term(src, m) * scale
-            new_im[m, rows] = pi[m, rows] + term(src, modes + m) * scale
+            at = k * modes + m
+            for src, rows, scale in places:
+                held[at, rows] = old[m, rows] + term(src, at) * scale
+            copies.append(pltpu.make_async_copy(held.at[at], out.at[m], sem.at[at]))
+            copies[-1].start()
+    for copy in copies:
+        copy.wait()
+
+
+def update_probe(rim, parts, pr, pi):
+    shape = pr.shape
+    both = (2 * shape[0],) + shape[1:]
+    size = 4 * (2 * math.prod(both) + sum(p.size for p in parts))
+    return pl.pallas_call(
+        functools.partial(probe_body, rim),
+        out_shape=[jax.ShapeDtypeStruct(shape, F32)] * 2,
+        in_specs=[pl.BlockSpec(memory_space=pltpu.VMEM)] * (len(parts) + 2),
+        out_specs=[pl.BlockSpec(memory_space=pltpu.HBM)] * 2,
+        scratch_shapes=[pltpu.VMEM(both, F32), pltpu.SemaphoreType.DMA((both[0],))],
+        compiler_params=pltpu.CompilerParams(vmem_limit_bytes=size + (2 << 20)),
+    )(*parts, pr, pi)
 
 
 def swap_bit(array, where):
@@ -573,7 +597,7 @@
             every = gather_spots(most, bits[-1:])[-1]
             (denom,) = light(every.reshape(-1).astype(jnp.int32), probe_re, probe_im)
         outs = [strip] * 3 + ([terms] * 2 * COLORS if last else [])
-        scr = scratch + ([pltpu.VMEM((2 * modes + 1, width, width), F32)] if last else [])
+        scr = scratch
         res = call(functools.partial(view_body, sizes, last), outs, scr, extra=8 << 20)(
             sc, mid, near, far, probe_re, probe_im, view, traded, tabs
         )
@@ -589,7 +613,7 @@
 
     def beside(r, gots):
         if r == 0:
-            gots[0], a, b = lax.optimization_barrier((gots[0], near, far))
+            gots[1], a, b = lax.optimization_barrier((gots[1], near, far))
             held["own"], to_near, to_far = fold(sc, gm, a, b)
             held["both"] = swap_both(to_near, to_far, "row")
         elif r == 1:
@@ -605,10 +629,7 @@
         return got
 
     mine, other = sum_terms(res[3::2], res[4::2], n_row, n_col, beside, late)
-    shape = (modes, width, width)
-    new_re, new_im = call(functools.partial(probe_body, rim), [shape] * 2)(
-        *mine, *other, probe_re, probe_im
-    )
+    new_re, new_im = update_probe(rim, [*mine, *other], probe_re, probe_im)
     done_re, done_im = call(leave_body, [(rows, cols)] * 2)(held["state"], held["traded"])
     return (done_re, done_im, new_re, new_im)
 

time: 137 us -> 139 us (1.015)
    pallas_call x41 -> x40, Pallas kernels: 18.9 us -> 16.8 us  [run(): pl.pallas_call(body, out_shape=[jax.ShapeDtypeStruct(s, F32) for s in out...]
    pallas_call x0 -> x1, Pallas kernels: none -> 1.6 us  [update_probe(): pl.pallas_call(functools.partial(probe_body, rim), out_shape=[jax.ShapeDt...]
  transfers between devices with their start and end apart: 58 -> 58, of which waited for: 25 -> 24; matrix products, arithmetic and copies ran while one was open for 0% -> 0% of each run, Pallas kernels for 6% -> 6%
where the time goes in v7:
time: 139 us
  starting transfers between devices  65.9 us (47%)
  waiting for transfers between devices  51.1 us (37%)
  Pallas kernels  20.1 us (14%)
    ppermute x32, starting transfers between devices, swap_bit(): lax.ppermute(array, name, [(i, i ^ 1 << level) for i in range(count)])  33.5 us
    ppermute x26, starting transfers between devices, move(): return lax.ppermute(array, ('row', 'col'), pairs)  32.3 us
    ppermute x26, waiting for transfers between devices, move(): return lax.ppermute(array, ('row', 'col'), pairs)  27.9 us
    ppermute x32, waiting for transfers between devices, swap_bit(): lax.ppermute(array, name, [(i, i ^ 1 << level) for i in range(count)])  23.2 us
    pallas_call x40, Pallas kernels, run(): pl.pallas_call(body, out_shape=[jax.ShapeDtypeStruct(s, F32) for s in out...  16.8 us
  transfers between devices with their start and end apart: 58, of which 24 were waited for; matrix products, arithmetic and copies ran while one was open for 0% of the time, Pallas kernels for 6%

profile of v7, /device:TPU:0, one launch (start us, length us, event | category | flops | bytes accessed | tf_op | source)
XLA Modules:
  0.0 139.3 jit_solution(1632183902102426967)
XLA Ops:
  2.1 4.1 %collective-permute-start = (f32[2,128,128]{2,1,0:T(8,128)S(1)}, f32[2,128,128]{2,1,0:T(8,128)S(1)}, u32[]{:S(2)}, u32[]{:S(2)}) collective-permute-start(f32[2,128,128]{2,1,0:T(8,128)S(1)} %pad_maximum_fusion.s), channel_id=1, source_target_pairs={{0,4},{1,5},{2,6},{3,7},{4,0},{5,1},{6,2},{7,3},{8,12},{9,13},{10,... | collective-permute-start | bytes 393224 | tf_op jit(solution)/shard_map/ppermute | solution.py:109
  6.8 4.3 %collective-permute-done.2 = f32[1,128]{1,0:T(1,128)S(1)} collective-permute-done((f32[1,128]{1,0:T(1,128)S(1)}, f32[1,128]{1,0:T(1,128)S(1)}, u32[]{:S(2)}, u32[]{:S(2)}) %collective-permute-start.2) | collective-permute-done | bytes 544 | tf_op jit(solution)/shard_map/ppermute | solution.py:476
  17.6 2.9 %collective-permute-start.7 = (f32[1,128]{1,0:T(1,128)S(1)}, f32[1,128]{1,0:T(1,128)S(1)}, u32[]{:S(2)}, u32[]{:S(2)}) collective-permute-start(f32[1,128]{1,0:T(1,128)S(1)} %add.17.sc), channel_id=1, source_target_pairs={{0,8},{4,12},{8,0},{12,4},{16,24},{20,28},{24,16},{28,20},{1,9},{5... | collective-permute-start | bytes 1544 | tf_op jit(solution)/shard_map/ppermute | solution.py:476
  20.6 1.7 %shard_map.105 = (f32[4,256,256]{2,1,0:T(8,128)S(1)}, f32[4,256,256]{2,1,0:T(8,128)S(1)}, bf16[4,256,256]{2,1,0:T(8,128)(2,1)S(1)}) custom-call(f32[4,256,256]{2,1,0:T(8,128)} %refs_0_.1, f32[4,256,256]{2,1,0:T(8,128)} %refs_1_.1, bf16[4,256,256]{2,1,0:T(8,128)(2,1)} %constant.2.clone.refs_2_), custom_call_target="tpu_custom_call" | custom-call | bytes 5242880 | tf_op jit(solution)/shard_map/pallas_call | solution.py:233
  23.9 2.9 %shard_map.106 = (f32[2,256,128]{2,1,0:T(8,128)S(1)}, f32[2,256,128]{2,1,0:T(8,128)S(1)}, f32[2,256,128]{2,1,0:T(8,128)S(1)}) custom-call(f32[1,128]{1,0:T(1,128)S(1)} %add.17.sc, f32[2,384,128]{2,1,0:T(8,128)S(1)} %get-tuple-element.81.mid, f32[2,384,128]{2,1,0:T(8,128)S(1)} %collective-permute-done.5.near, f32[2,384,128]{2,1,0:T(8,128)S(1)} %collective-permute-done.6.far, ...), custom_call_target="tpu_custom_call" | custom-call | tf_op jit(solution)/shard_map/pallas_call | solution.py:134
  26.9 3.7 %collective-permute-start.10 = (f32[2,256,128]{2,1,0:T(8,128)S(1)}, f32[2,256,128]{2,1,0:T(8,128)S(1)}, u32[]{:S(2)}, u32[]{:S(2)}) collective-permute-start(f32[2,256,128]{2,1,0:T(8,128)S(1)} %get-tuple-element.90), channel_id=1, source_target_pairs={{0,8},{1,2},{2,1},{3,11},{4,12},{5,6},{6,5},{7,15},{8,0},{9,10},{1... | collective-permute-start | bytes 786440 | tf_op jit(solution)/shard_map/ppermute | solution.py:109
  30.6 3.2 %collective-permute-start.13 = (f32[1,128]{1,0:T(1,128)S(1)}, f32[1,128]{1,0:T(1,128)S(1)}, u32[]{:S(2)}, u32[]{:S(2)}) collective-permute-start(f32[1,128]{1,0:T(1,128)S(1)} %add.18), channel_id=1, source_target_pairs={{0,16},{4,20},{8,24},{12,28},{16,0},{20,4},{24,8},{28,12},{1,17},{... | collective-permute-start | bytes 1544 | tf_op jit(solution)/shard_map/ppermute | solution.py:476
  35.2 1.8 %collective-permute-start.11 = (f32[2,128,128]{2,1,0:T(8,128)S(1)}, f32[2,128,128]{2,1,0:T(8,128)S(1)}, u32[]{:S(2)}, u32[]{:S(2)}) collective-permute-start(f32[2,128,128]{2,1,0:T(8,128)S(1)} %get-tuple-element.92), channel_id=1, source_target_pairs={{0,4},{1,5},{2,6},{3,7},{4,0},{5,1},{6,2},{7,3},{8,12},{9,13},{10,... | collective-permute-start | bytes 393224 | tf_op jit(solution)/shard_map/ppermute | solution.py:109
  37.0 4.2 %shard_map.108.denom = f32[128,128]{1,0:T(8,128)S(1)} custom-call(s32[128]{0:T(128)S(1)} %convert_bitcast_fusion.sc, f32[4,256,256]{2,1,0:T(8,128)S(1)} %get-tuple-element.84.pr.refs_6_, f32[4,256,256]{2,1,0:T(8,128)S(1)} %get-tuple-element.85.pi.refs_7_), custom_call_target="tpu_custom_call" | custom-call | flops 16777216 | bytes 10000000 | tf_op jit(solution)/shard_map/pallas_call | solution.py:134
  41.9 2.8 %collective-permute-start.14 = (f32[2,128,128]{2,1,0:T(8,128)S(1)}, f32[2,128,128]{2,1,0:T(8,128)S(1)}, u32[]{:S(2)}, u32[]{:S(2)}) collective-permute-start(f32[2,128,128]{2,1,0:T(8,128)S(1)} %shard_map.109.s), channel_id=1, source_target_pairs={{0,4},{1,5},{2,6},{3,7},{4,0},{5,1},{6,2},{7,3},{8,12},{9,13},{10,... | collective-permute-start | bytes 393224 | tf_op jit(solution)/shard_map/ppermute | solution.py:109
  44.7 2.9 %collective-permute-done.14.near = f32[2,128,128]{2,1,0:T(8,128)S(1)} collective-permute-done((f32[2,128,128]{2,1,0:T(8,128)S(1)}, f32[2,128,128]{2,1,0:T(8,128)S(1)}, u32[]{:S(2)}, u32[]{:S(2)}) %collective-permute-start.14) | collective-permute-done | bytes 131104 | tf_op jit(solution)/shard_map/ppermute | solution.py:109
  47.9 2.8 %collective-permute-start.17 = (f32[2,256,128]{2,1,0:T(8,128)S(1)}, f32[2,256,128]{2,1,0:T(8,128)S(1)}, u32[]{:S(2)}, u32[]{:S(2)}) collective-permute-start(f32[2,256,128]{2,1,0:T(8,128)S(1)} %get-tuple-element.97), channel_id=1, source_target_pairs={{0,8},{1,2},{2,1},{3,11},{4,12},{5,6},{6,5},{7,15},{8,0},{9,10},{1... | collective-permute-start | bytes 786440 | tf_op jit(solution)/shard_map/ppermute | solution.py:109
  50.7 4.3 %collective-permute-done.17.far = f32[2,256,128]{2,1,0:T(8,128)S(1)} collective-permute-done((f32[2,256,128]{2,1,0:T(8,128)S(1)}, f32[2,256,128]{2,1,0:T(8,128)S(1)}, u32[]{:S(2)}, u32[]{:S(2)}) %collective-permute-start.17) | collective-permute-done | bytes 262176 | tf_op jit(solution)/shard_map/ppermute | solution.py:109
  55.1 2.8 %shard_map.111 = (f32[2,256,128]{2,1,0:T(8,128)S(1)}, f32[2,256,128]{2,1,0:T(8,128)S(1)}, f32[2,256,128]{2,1,0:T(8,128)S(1)}) custom-call(f32[1,128]{1,0:T(1,128)S(1)} %add.17.sc, f32[2,256,128]{2,1,0:T(8,128)S(1)} %get-tuple-element.95.mid, f32[2,256,128]{2,1,0:T(8,128)S(1)} %collective-permute-done.16.near, ...), custom_call_target="tpu_custom_call" | custom-call | tf_op jit(solution)/shard_map/pallas_call | solution.py:134
  57.9 2.1 %collective-permute-start.19 = (f32[2,256,128]{2,1,0:T(8,128)S(1)}, f32[2,256,128]{2,1,0:T(8,128)S(1)}, u32[]{:S(2)}, u32[]{:S(2)}) collective-permute-start(f32[2,256,128]{2,1,0:T(8,128)S(1)} %get-tuple-element.100), channel_id=1, source_target_pairs={{0,8},{1,2},{2,1},{3,11},{4,12},{5,6},{6,5},{7,15},{8,0},{9,10},{1... | collective-permute-start | bytes 786440 | tf_op jit(solution)/shard_map/ppermute | solution.py:109
  60.1 4.3 %collective-permute-done.19.far = f32[2,256,128]{2,1,0:T(8,128)S(1)} collective-permute-done((f32[2,256,128]{2,1,0:T(8,128)S(1)}, f32[2,256,128]{2,1,0:T(8,128)S(1)}, u32[]{:S(2)}, u32[]{:S(2)}) %collective-permute-start.19) | collective-permute-done | bytes 262176 | tf_op jit(solution)/shard_map/ppermute | solution.py:109
  66.0 4.2 %collective-permute-done.20.near = f32[2,128,128]{2,1,0:T(8,128)S(1)} collective-permute-done((f32[2,128,128]{2,1,0:T(8,128)S(1)}, f32[2,128,128]{2,1,0:T(8,128)S(1)}, u32[]{:S(2)}, u32[]{:S(2)}) %collective-permute-start.20) | collective-permute-done | bytes 131104 | tf_op jit(solution)/shard_map/ppermute | solution.py:109
  70.4 3.7 %collective-permute-start.22 = (f32[2,128,128]{2,1,0:T(8,128)S(1)}, f32[2,128,128]{2,1,0:T(8,128)S(1)}, u32[]{:S(2)}, u32[]{:S(2)}) collective-permute-start(f32[2,128,128]{2,1,0:T(8,128)S(1)} %shard_map.113.s), channel_id=1, source_target_pairs={{0,4},{1,5},{2,6},{3,7},{4,0},{5,1},{6,2},{7,3},{8,12},{9,13},{10,... | collective-permute-start | bytes 393224 | tf_op jit(solution)/shard_map/ppermute | solution.py:109
  74.1 2.9 %collective-permute-done.22.near = f32[2,128,128]{2,1,0:T(8,128)S(1)} collective-permute-done((f32[2,128,128]{2,1,0:T(8,128)S(1)}, f32[2,128,128]{2,1,0:T(8,128)S(1)}, u32[]{:S(2)}, u32[]{:S(2)}) %collective-permute-start.22) | collective-permute-done | bytes 131104 | tf_op jit(solution)/shard_map/ppermute | solution.py:109
  77.3 3.1 %collective-permute-start.25 = (f32[2,256,128]{2,1,0:T(8,128)S(1)}, f32[2,256,128]{2,1,0:T(8,128)S(1)}, u32[]{:S(2)}, u32[]{:S(2)}) collective-permute-start(f32[2,256,128]{2,1,0:T(8,128)S(1)} %get-tuple-element.106), channel_id=1, source_target_pairs={{0,8},{1,2},{2,1},{3,11},{4,12},{5,6},{6,5},{7,15},{8,0},{9,10},{1... | collective-permute-start | bytes 786440 | tf_op jit(solution)/shard_map/ppermute | solution.py:109
  80.4 4.3 %collective-permute-done.25.far = f32[2,256,128]{2,1,0:T(8,128)S(1)} collective-permute-done((f32[2,256,128]{2,1,0:T(8,128)S(1)}, f32[2,256,128]{2,1,0:T(8,128)S(1)}, u32[]{:S(2)}, u32[]{:S(2)}) %collective-permute-start.25) | collective-permute-done | bytes 262176 | tf_op jit(solution)/shard_map/ppermute | solution.py:109
  84.7 3.2 %shard_map.115 = (f32[2,256,128]{2,1,0:T(8,128)S(1)}, f32[2,256,128]{2,1,0:T(8,128)S(1)}, f32[2,256,128]{2,1,0:T(8,128)S(1)}, f32[3,128,256]{2,1,0:T(8,128)S(1)}...) custom-call(f32[1,128]{1,0:T(1,128)S(1)} %add.17.sc, ...), custom_call_target="tpu_custom_call" | custom-call | tf_op jit(solution)/shard_map/pallas_call | solution.py:134
  89.0 2.0 %collective-permute-start.36 = (f32[2,256,128]{2,1,0:T(8,128)S(1)}, f32[2,256,128]{2,1,0:T(8,128)S(1)}, u32[]{:S(2)}, u32[]{:S(2)}) collective-permute-start(f32[2,256,128]{2,1,0:T(8,128)S(1)} %get-tuple-element.120), channel_id=1, source_target_pairs={{0,8},{1,2},{2,1},{3,11},{4,12},{5,6},{6,5},{7,15},{8,0},{9,10},{1... | collective-permute-start | bytes 786440 | tf_op jit(solution)/shard_map/ppermute | solution.py:109
  93.2 3.6 %collective-permute-done.36.far = f32[2,256,128]{2,1,0:T(8,128)S(1)} collective-permute-done((f32[2,256,128]{2,1,0:T(8,128)S(1)}, f32[2,256,128]{2,1,0:T(8,128)S(1)}, u32[]{:S(2)}, u32[]{:S(2)}) %collective-permute-start.36) | collective-permute-done | bytes 262176 | tf_op jit(solution)/shard_map/ppermute | solution.py:109
  96.8 2.5 %collective-permute-done.34.got = f32[3,64,256]{2,1,0:T(8,128)S(1)} collective-permute-done((f32[3,64,256]{2,1,0:T(8,128)S(1)}, f32[3,64,256]{2,1,0:T(8,128)S(1)}, u32[]{:S(2)}, u32[]{:S(2)}) %collective-permute-start.34) | collective-permute-done | bytes 196640 | tf_op jit(solution)/shard_map/ppermute | solution.py:476
  100.8 2.4 %collective-permute-start.44 = (f32[3,32,256]{2,1,0:T(8,128)S(1)}, f32[3,32,256]{2,1,0:T(8,128)S(1)}, u32[]{:S(2)}, u32[]{:S(2)}) collective-permute-start(f32[3,32,256]{2,1,0:T(8,128)S(1)} %get-tuple-element.141), channel_id=1, source_target_pairs={{0,8},{4,12},{8,0},{12,4},{16,24},{20,28},{24,16},{28,20},{1,9},{5... | collective-permute-start | bytes 294920 | tf_op jit(solution)/shard_map/ppermute | solution.py:476
  104.0 2.0 %collective-permute-done.28.got = f32[3,32,256]{2,1,0:T(8,128)S(1)} collective-permute-done((f32[3,32,256]{2,1,0:T(8,128)S(1)}, f32[3,32,256]{2,1,0:T(8,128)S(1)}, u32[]{:S(2)}, u32[]{:S(2)}) %collective-permute-start.28) | collective-permute-done | bytes 98336 | tf_op jit(solution)/shard_map/ppermute | solution.py:476
  106.0 1.9 %collective-permute-start.29 = (f32[3,16,256]{2,1,0:T(8,128)S(1)}, f32[3,16,256]{2,1,0:T(8,128)S(1)}, u32[]{:S(2)}, u32[]{:S(2)}) collective-permute-start(f32[3,16,256]{2,1,0:T(8,128)S(1)} %get-tuple-element.114), channel_id=1, source_target_pairs={{0,8},{4,12},{8,0},{12,4},{16,24},{20,28},{24,16},{28,20},{1,9},{5... | collective-permute-start | bytes 147464 | tf_op jit(solution)/shard_map/ppermute | solution.py:476
  113.1 2.0 %collective-permute-start.30 = (f32[3,16,256]{2,1,0:T(8,128)S(1)}, f32[3,16,256]{2,1,0:T(8,128)S(1)}, u32[]{:S(2)}, u32[]{:S(2)}) collective-permute-start(f32[3,16,256]{2,1,0:T(8,128)S(1)} %shard_map.119.cur), channel_id=1, source_target_pairs={{0,16},{4,20},{8,24},{12,28},{16,0},{20,4},{24,8},{28,12},{1,17},{... | collective-permute-start | bytes 147464 | tf_op jit(solution)/shard_map/ppermute | solution.py:476
  121.8 1.8 %collective-permute-start.48 = (f32[3,32,256]{2,1,0:T(8,128)S(1)}, f32[3,32,256]{2,1,0:T(8,128)S(1)}, u32[]{:S(2)}, u32[]{:S(2)}) collective-permute-start(f32[3,32,256]{2,1,0:T(8,128)S(1)} %shard_map.134.cur), channel_id=1, source_target_pairs={{0,8},{4,12},{8,0},{12,4},{16,24},{20,28},{24,16},{28,20},{1,9},{5... | collective-permute-start | bytes 294920 | tf_op jit(solution)/shard_map/ppermute | solution.py:476
  126.6 1.7 %collective-permute-start.49 = (f32[3,64,256]{2,1,0:T(8,128)S(1)}, f32[3,64,256]{2,1,0:T(8,128)S(1)}, u32[]{:S(2)}, u32[]{:S(2)}) collective-permute-start(f32[3,64,256]{2,1,0:T(8,128)S(1)} %shard_map.135.cur), channel_id=1, source_target_pairs={{0,2},{1,3},{2,0},{3,1},{4,6},{5,7},{6,4},{7,5},{8,10},{9,11},{10,... | collective-permute-start | bytes 589832 | tf_op jit(solution)/shard_map/ppermute | solution.py:476
  130.8 2.1 %collective-permute-done.49.got = f32[3,64,256]{2,1,0:T(8,128)S(1)} collective-permute-done((f32[3,64,256]{2,1,0:T(8,128)S(1)}, f32[3,64,256]{2,1,0:T(8,128)S(1)}, u32[]{:S(2)}, u32[]{:S(2)}) %collective-permute-start.49) | collective-permute-done | bytes 196640 | tf_op jit(solution)/shard_map/ppermute | solution.py:476
  (136 shorter events, 43.7 us)
Async XLA Ops:
  1.6 14.3 %collective-permute-start.1 = (f32[2,128,128]{2,1,0:T(8,128)S(1)}, f32[2,128,128]{2,1,0:T(8,128)S(1)}, u32[]{:S(2)}, u32[]{:S(2)}) collective-permute-start(f32[2,128,128]{2,1,0:T(8,128)S(1)} %pad_maximum_fusion.s), channel_id=1, source_target_pairs={{0,1},{1,0},{2,3},{3,2},{4,12},{5,13},{6,14},{7,15},{8,4},{9,5},{1... | collective-permute-start | bytes 393224 | tf_op jit(solution)/shard_map/ppermute | solution.py:109
  2.1 13.7 %collective-permute-start = (f32[2,128,128]{2,1,0:T(8,128)S(1)}, f32[2,128,128]{2,1,0:T(8,128)S(1)}, u32[]{:S(2)}, u32[]{:S(2)}) collective-permute-start(f32[2,128,128]{2,1,0:T(8,128)S(1)} %pad_maximum_fusion.s), channel_id=1, source_target_pairs={{0,4},{1,5},{2,6},{3,7},{4,0},{5,1},{6,2},{7,3},{8,12},{9,13},{10,... | collective-permute-start | bytes 393224 | tf_op jit(solution)/shard_map/ppermute | solution.py:109
  15.9 7.9 %collective-permute-start.6 = (f32[2,384,128]{2,1,0:T(8,128)S(1)}, f32[2,384,128]{2,1,0:T(8,128)S(1)}, u32[]{:S(2)}, u32[]{:S(2)}) collective-permute-start(f32[2,384,128]{2,1,0:T(8,128)S(1)} %get-tuple-element.81.mid), channel_id=1, source_target_pairs={{0,8},{1,2},{2,1},{3,11},{4,12},{5,6},{6,5},{7,15},{8,0},{9,10},{1... | collective-permute-start | bytes 1179656 | tf_op jit(solution)/shard_map/ppermute | solution.py:109
  16.8 7.1 %collective-permute-start.5 = (f32[2,384,128]{2,1,0:T(8,128)S(1)}, f32[2,384,128]{2,1,0:T(8,128)S(1)}, u32[]{:S(2)}, u32[]{:S(2)}) collective-permute-start(f32[2,384,128]{2,1,0:T(8,128)S(1)} %get-tuple-element.81.mid), channel_id=1, source_target_pairs={{0,1},{1,0},{2,3},{3,2},{4,5},{5,4},{6,7},{7,6},{8,9},{9,8},{10,11... | collective-permute-start | bytes 1179656 | tf_op jit(solution)/shard_map/ppermute | solution.py:109
  17.6 6.3 %collective-permute-start.8 = (f32[256,256]{1,0:T(8,128)S(1)}, f32[256,256]{1,0:T(8,128)S(1)}, u32[]{:S(2)}, u32[]{:S(2)}) collective-permute-start(f32[256,256]{1,0:T(8,128)S(1)} %shard_map.103.view), channel_id=1, source_target_pairs={{0,1},{1,0},{2,3},{3,2},{4,5},{5,4},{6,7},{7,6},{8,12},{9,13},{10,... | collective-permute-start | bytes 786440 | tf_op jit(solution)/shard_map/ppermute | solution.py:109
  17.6 6.2 %collective-permute-start.7 = (f32[1,128]{1,0:T(1,128)S(1)}, f32[1,128]{1,0:T(1,128)S(1)}, u32[]{:S(2)}, u32[]{:S(2)}) collective-permute-start(f32[1,128]{1,0:T(1,128)S(1)} %add.17.sc), channel_id=1, source_target_pairs={{0,8},{4,12},{8,0},{12,4},{16,24},{20,28},{24,16},{28,20},{1,9},{5... | collective-permute-start | bytes 1544 | tf_op jit(solution)/shard_map/ppermute | solution.py:476
  26.8 7.0 %collective-permute-start.9 = (f32[2,256,128]{2,1,0:T(8,128)S(1)}, f32[2,256,128]{2,1,0:T(8,128)S(1)}, u32[]{:S(2)}, u32[]{:S(2)}) collective-permute-start(f32[2,256,128]{2,1,0:T(8,128)S(1)} %get-tuple-element.89), channel_id=1, source_target_pairs={{0,1},{1,0},{2,3},{3,2},{4,5},{5,4},{6,7},{7,6},{8,9},{9,8},{10,11... | collective-permute-start | bytes 786440 | tf_op jit(solution)/shard_map/ppermute | solution.py:109
  26.9 8.1 %collective-permute-start.10 = (f32[2,256,128]{2,1,0:T(8,128)S(1)}, f32[2,256,128]{2,1,0:T(8,128)S(1)}, u32[]{:S(2)}, u32[]{:S(2)}) collective-permute-start(f32[2,256,128]{2,1,0:T(8,128)S(1)} %get-tuple-element.90), channel_id=1, source_target_pairs={{0,8},{1,2},{2,1},{3,11},{4,12},{5,6},{6,5},{7,15},{8,0},{9,10},{1... | collective-permute-start | bytes 786440 | tf_op jit(solution)/shard_map/ppermute | solution.py:109
  30.6 6.4 %collective-permute-start.13 = (f32[1,128]{1,0:T(1,128)S(1)}, f32[1,128]{1,0:T(1,128)S(1)}, u32[]{:S(2)}, u32[]{:S(2)}) collective-permute-start(f32[1,128]{1,0:T(1,128)S(1)} %add.18), channel_id=1, source_target_pairs={{0,16},{4,20},{8,24},{12,28},{16,0},{20,4},{24,8},{28,12},{1,17},{... | collective-permute-start | bytes 1544 | tf_op jit(solution)/shard_map/ppermute | solution.py:476
  35.2 6.1 %collective-permute-start.11 = (f32[2,128,128]{2,1,0:T(8,128)S(1)}, f32[2,128,128]{2,1,0:T(8,128)S(1)}, u32[]{:S(2)}, u32[]{:S(2)}) collective-permute-start(f32[2,128,128]{2,1,0:T(8,128)S(1)} %get-tuple-element.92), channel_id=1, source_target_pairs={{0,4},{1,5},{2,6},{3,7},{4,0},{5,1},{6,2},{7,3},{8,12},{9,13},{10,... | collective-permute-start | bytes 393224 | tf_op jit(solution)/shard_map/ppermute | solution.py:109
  41.9 5.8 %collective-permute-start.14 = (f32[2,128,128]{2,1,0:T(8,128)S(1)}, f32[2,128,128]{2,1,0:T(8,128)S(1)}, u32[]{:S(2)}, u32[]{:S(2)}) collective-permute-start(f32[2,128,128]{2,1,0:T(8,128)S(1)} %shard_map.109.s), channel_id=1, source_target_pairs={{0,4},{1,5},{2,6},{3,7},{4,0},{5,1},{6,2},{7,3},{8,12},{9,13},{10,... | collective-permute-start | bytes 393224 | tf_op jit(solution)/shard_map/ppermute | solution.py:109
  47.9 7.1 %collective-permute-start.17 = (f32[2,256,128]{2,1,0:T(8,128)S(1)}, f32[2,256,128]{2,1,0:T(8,128)S(1)}, u32[]{:S(2)}, u32[]{:S(2)}) collective-permute-start(f32[2,256,128]{2,1,0:T(8,128)S(1)} %get-tuple-element.97), channel_id=1, source_target_pairs={{0,8},{1,2},{2,1},{3,11},{4,12},{5,6},{6,5},{7,15},{8,0},{9,10},{1... | collective-permute-start | bytes 786440 | tf_op jit(solution)/shard_map/ppermute | solution.py:109
  57.9 6.5 %collective-permute-start.19 = (f32[2,256,128]{2,1,0:T(8,128)S(1)}, f32[2,256,128]{2,1,0:T(8,128)S(1)}, u32[]{:S(2)}, u32[]{:S(2)}) collective-permute-start(f32[2,256,128]{2,1,0:T(8,128)S(1)} %get-tuple-element.100), channel_id=1, source_target_pairs={{0,8},{1,2},{2,1},{3,11},{4,12},{5,6},{6,5},{7,15},{8,0},{9,10},{1... | collective-permute-start | bytes 786440 | tf_op jit(solution)/shard_map/ppermute | solution.py:109
  64.7 5.6 %collective-permute-start.20 = (f32[2,128,128]{2,1,0:T(8,128)S(1)}, f32[2,128,128]{2,1,0:T(8,128)S(1)}, u32[]{:S(2)}, u32[]{:S(2)}) collective-permute-start(f32[2,128,128]{2,1,0:T(8,128)S(1)} %get-tuple-element.102), channel_id=1, source_target_pairs={{0,4},{1,5},{2,6},{3,7},{4,0},{5,1},{6,2},{7,3},{8,12},{9,13},{10,... | collective-permute-start | bytes 393224 | tf_op jit(solution)/shard_map/ppermute | solution.py:109
  70.4 6.7 %collective-permute-start.22 = (f32[2,128,128]{2,1,0:T(8,128)S(1)}, f32[2,128,128]{2,1,0:T(8,128)S(1)}, u32[]{:S(2)}, u32[]{:S(2)}) collective-permute-start(f32[2,128,128]{2,1,0:T(8,128)S(1)} %shard_map.113.s), channel_id=1, source_target_pairs={{0,4},{1,5},{2,6},{3,7},{4,0},{5,1},{6,2},{7,3},{8,12},{9,13},{10,... | collective-permute-start | bytes 393224 | tf_op jit(solution)/shard_map/ppermute | solution.py:109
  77.3 7.4 %collective-permute-start.25 = (f32[2,256,128]{2,1,0:T(8,128)S(1)}, f32[2,256,128]{2,1,0:T(8,128)S(1)}, u32[]{:S(2)}, u32[]{:S(2)}) collective-permute-start(f32[2,256,128]{2,1,0:T(8,128)S(1)} %get-tuple-element.106), channel_id=1, source_target_pairs={{0,8},{1,2},{2,1},{3,11},{4,12},{5,6},{6,5},{7,15},{8,0},{9,10},{1... | collective-permute-start | bytes 786440 | tf_op jit(solution)/shard_map/ppermute | solution.py:109
  89.0 7.7 %collective-permute-start.36 = (f32[2,256,128]{2,1,0:T(8,128)S(1)}, f32[2,256,128]{2,1,0:T(8,128)S(1)}, u32[]{:S(2)}, u32[]{:S(2)}) collective-permute-start(f32[2,256,128]{2,1,0:T(8,128)S(1)} %get-tuple-element.120), channel_id=1, source_target_pairs={{0,8},{1,2},{2,1},{3,11},{4,12},{5,6},{6,5},{7,15},{8,0},{9,10},{1... | collective-permute-start | bytes 786440 | tf_op jit(solution)/shard_map/ppermute | solution.py:109
  91.1 8.2 %collective-permute-start.34 = (f32[3,64,256]{2,1,0:T(8,128)S(1)}, f32[3,64,256]{2,1,0:T(8,128)S(1)}, u32[]{:S(2)}, u32[]{:S(2)}) collective-permute-start(f32[3,64,256]{2,1,0:T(8,128)S(1)} %get-tuple-element.118), channel_id=1, source_target_pairs={{0,2},{1,3},{2,0},{3,1},{4,6},{5,7},{6,4},{7,5},{8,10},{9,11},{10,... | collective-permute-start | bytes 589832 | tf_op jit(solution)/shard_map/ppermute | solution.py:476
  91.2 9.4 %collective-permute-start.27 = (f32[3,64,256]{2,1,0:T(8,128)S(1)}, f32[3,64,256]{2,1,0:T(8,128)S(1)}, u32[]{:S(2)}, u32[]{:S(2)}) collective-permute-start(f32[3,64,256]{2,1,0:T(8,128)S(1)} %get-tuple-element.110), channel_id=1, source_target_pairs={{0,4},{4,0},{8,12},{12,8},{16,20},{20,16},{24,28},{28,24},{1,5},{5... | collective-permute-start | bytes 589832 | tf_op jit(solution)/shard_map/ppermute | solution.py:476
  92.1 11.2 %collective-permute-start.38 = (f32[3,64,256]{2,1,0:T(8,128)S(1)}, f32[3,64,256]{2,1,0:T(8,128)S(1)}, u32[]{:S(2)}, u32[]{:S(2)}) collective-permute-start(f32[3,64,256]{2,1,0:T(8,128)S(1)} %get-tuple-element.127), channel_id=1, source_target_pairs={{0,8},{4,12},{8,0},{12,4},{16,24},{20,28},{24,16},{28,20},{1,9},{5... | collective-permute-start | bytes 589832 | tf_op jit(solution)/shard_map/ppermute | solution.py:476
  99.5 9.8 %collective-permute-start.40 = (f32[2,128,128]{2,1,0:T(8,128)S(1)}, f32[2,128,128]{2,1,0:T(8,128)S(1)}, u32[]{:S(2)}, u32[]{:S(2)}) collective-permute-start(f32[2,128,128]{2,1,0:T(8,128)S(1)} %get-tuple-element.129), channel_id=1, source_target_pairs={{0,4},{1,5},{2,6},{3,7},{4,0},{5,1},{6,2},{7,3},{8,12},{9,13},{10,... | collective-permute-start | bytes 393224 | tf_op jit(solution)/shard_map/ppermute | solution.py:109
  100.7 8.6 %collective-permute-start.41 = (f32[2,128,128]{2,1,0:T(8,128)S(1)}, f32[2,128,128]{2,1,0:T(8,128)S(1)}, u32[]{:S(2)}, u32[]{:S(2)}) collective-permute-start(f32[2,128,128]{2,1,0:T(8,128)S(1)} %get-tuple-element.130), channel_id=1, source_target_pairs={{0,1},{1,0},{2,3},{3,2},{4,12},{5,13},{6,14},{7,15},{8,16},{9,17},... | collective-permute-start | bytes 393224 | tf_op jit(solution)/shard_map/ppermute | solution.py:109
  100.8 7.0 %collective-permute-start.44 = (f32[3,32,256]{2,1,0:T(8,128)S(1)}, f32[3,32,256]{2,1,0:T(8,128)S(1)}, u32[]{:S(2)}, u32[]{:S(2)}) collective-permute-start(f32[3,32,256]{2,1,0:T(8,128)S(1)} %get-tuple-element.141), channel_id=1, source_target_pairs={{0,8},{4,12},{8,0},{12,4},{16,24},{20,28},{24,16},{28,20},{1,9},{5... | collective-permute-start | bytes 294920 | tf_op jit(solution)/shard_map/ppermute | solution.py:476
  103.3 6.0 %collective-permute-start.39 = (f32[3,32,256]{2,1,0:T(8,128)S(1)}, f32[3,32,256]{2,1,0:T(8,128)S(1)}, u32[]{:S(2)}, u32[]{:S(2)}) collective-permute-start(f32[3,32,256]{2,1,0:T(8,128)S(1)} %get-tuple-element.128), channel_id=1, source_target_pairs={{0,4},{4,0},{8,12},{12,8},{16,20},{20,16},{24,28},{28,24},{1,5},{5... | collective-permute-start | bytes 294920 | tf_op jit(solution)/shard_map/ppermute | solution.py:476
  106.0 7.1 %collective-permute-start.29 = (f32[3,16,256]{2,1,0:T(8,128)S(1)}, f32[3,16,256]{2,1,0:T(8,128)S(1)}, u32[]{:S(2)}, u32[]{:S(2)}) collective-permute-start(f32[3,16,256]{2,1,0:T(8,128)S(1)} %get-tuple-element.114), channel_id=1, source_target_pairs={{0,8},{4,12},{8,0},{12,4},{16,24},{20,28},{24,16},{28,20},{1,9},{5... | collective-permute-start | bytes 147464 | tf_op jit(solution)/shard_map/ppermute | solution.py:476
  109.4 5.7 %collective-permute-start.50 = (f32[3,16,256]{2,1,0:T(8,128)S(1)}, f32[3,16,256]{2,1,0:T(8,128)S(1)}, u32[]{:S(2)}, u32[]{:S(2)}) collective-permute-start(f32[3,16,256]{2,1,0:T(8,128)S(1)} %get-tuple-element.147), channel_id=1, source_target_pairs={{0,2},{1,3},{2,0},{3,1},{4,6},{5,7},{6,4},{7,5},{8,10},{9,11},{10,... | collective-permute-start | bytes 147464 | tf_op jit(solution)/shard_map/ppermute | solution.py:476
  112.0 5.6 %collective-permute-start.46 = (f32[3,16,256]{2,1,0:T(8,128)S(1)}, f32[3,16,256]{2,1,0:T(8,128)S(1)}, u32[]{:S(2)}, u32[]{:S(2)}) collective-permute-start(f32[3,16,256]{2,1,0:T(8,128)S(1)} %shard_map.132.cur), channel_id=1, source_target_pairs={{0,16},{4,20},{8,24},{12,28},{16,0},{20,4},{24,8},{28,12},{1,17},{... | collective-permute-start | bytes 147464 | tf_op jit(solution)/shard_map/ppermute | solution.py:476
  115.1 5.6 %collective-permute-start.51 = (f32[3,16,256]{2,1,0:T(8,128)S(1)}, f32[3,16,256]{2,1,0:T(8,128)S(1)}, u32[]{:S(2)}, u32[]{:S(2)}) collective-permute-start(f32[3,16,256]{2,1,0:T(8,128)S(1)} %shard_map.138.cur), channel_id=1, source_target_pairs={{0,16},{4,20},{8,24},{12,28},{16,0},{20,4},{24,8},{28,12},{1,17},{... | collective-permute-start | bytes 147464 | tf_op jit(solution)/shard_map/ppermute | solution.py:476
  121.2 7.1 %collective-permute-start.42 = (f32[2,128,128]{2,1,0:T(8,128)S(1)}, f32[2,128,128]{2,1,0:T(8,128)S(1)}, u32[]{:S(2)}, u32[]{:S(2)}) collective-permute-start(f32[2,128,128]{2,1,0:T(8,128)S(1)} %shard_map.126.state), channel_id=1, source_target_pairs={{0,1},{1,0},{2,3},{3,2},{4,5},{5,4},{6,7},{7,6},{8,12},{9,13},{10,... | collective-permute-start | bytes 393224 | tf_op jit(solution)/shard_map/ppermute | solution.py:109
  126.6 6.3 %collective-permute-start.49 = (f32[3,64,256]{2,1,0:T(8,128)S(1)}, f32[3,64,256]{2,1,0:T(8,128)S(1)}, u32[]{:S(2)}, u32[]{:S(2)}) collective-permute-start(f32[3,64,256]{2,1,0:T(8,128)S(1)} %shard_map.135.cur), channel_id=1, source_target_pairs={{0,2},{1,3},{2,0},{3,1},{4,6},{5,7},{6,4},{7,5},{8,10},{9,11},{10,... | collective-permute-start | bytes 589832 | tf_op jit(solution)/shard_map/ppermute | solution.py:476
  128.4 6.1 %collective-permute-start.43 = (f32[3,64,256]{2,1,0:T(8,128)S(1)}, f32[3,64,256]{2,1,0:T(8,128)S(1)}, u32[]{:S(2)}, u32[]{:S(2)}) collective-permute-start(f32[3,64,256]{2,1,0:T(8,128)S(1)} %shard_map.128.cur), channel_id=1, source_target_pairs={{0,4},{4,0},{8,12},{12,8},{16,20},{20,16},{24,28},{28,24},{1,5},{5... | collective-permute-start | bytes 589832 | tf_op jit(solution)/shard_map/ppermute | solution.py:476
  129.9 5.7 %collective-permute-start.54 = (f32[3,64,256]{2,1,0:T(8,128)S(1)}, f32[3,64,256]{2,1,0:T(8,128)S(1)}, u32[]{:S(2)}, u32[]{:S(2)}) collective-permute-start(f32[3,64,256]{2,1,0:T(8,128)S(1)} %shard_map.141.cur), channel_id=1, source_target_pairs={{0,8},{4,12},{8,0},{12,4},{16,24},{20,28},{24,16},{28,20},{1,9},{5... | collective-permute-start | bytes 589832 | tf_op jit(solution)/shard_map/ppermute | solution.py:476
  (28 other events, 115.1 us)
